TPU v7x, 512 devices: a whole 4x8x8 slice. The times are simulated.
512 devices in a mesh: ctx: 32 (over y, x), mp: 16 (over z, core).
Axes of the slice: x: 4, y: 8, z: 8, core: 2. Of those that a mesh axis runs over, the one named last changes fastest.
Arguments:
- source_rows: bfloat16 [16384, 3, 8192], P('ctx', None, 'mp'), may hold values from -6 to 6
- short_filters: bfloat16 [3, 7, 8192], P(None, None, 'mp'), may hold values from -2 to 2
- medium_filters: bfloat16 [128, 512], P(None, 'mp'), may hold values from -0.5 to 0.5
- skip_gain: float32 [8192], P('mp'), may hold values from 0.1 to 1.9
- out_weight: bfloat16 [8192, 8192], P('mp', 'ctx'), may hold values from -0.0625 to 0.0625
- doc_lengths: int32 [8], replicated, may hold values from 1 to 2048, 8192 in all
- block_packing_device: int32 [32, 16], replicated, may hold values from 0 to 31, as said below
Outputs:
- mixed: bfloat16 [8192, 8192], P('ctx', 'mp')
Inputs may be any that keep to these rules, and one draw needn't show every extreme that they name: `block_packing_device`: row c names, for the 16 blocks of stretch c in order, the packing device that holds each; the entries of one row differ, and some packing device is named in every row. A packing device keeps the blocks it holds in increasing order of their stretch, in its first slots.
All inputs are finite; a program needn't handle non-finite values.
Results may differ from a plain program's by a relative error of at most 0.02.
Values may be sent and summed in bfloat16 or wider, within the bound.
No kernel may reach another device: no remote copies, remote signals or barrier semaphores. Data moves between devices by JAX's collectives and lax.ppermute only.
A program may use at most 128 MiB of HBM per device.

v0:
```python
import jax
import jax.numpy as jnp
from jax import lax
from jax.sharding import PartitionSpec as P


def passed_along(block, axis, distance):
    devices = range(lax.axis_size(axis))
    route = [(i - distance, i) for i in devices if i - distance in devices]
    return lax.ppermute(block, axis, route)


def reach_back(positions, starts):
    begin = jnp.max(jnp.where(starts[None, :] <= positions[:, None], starts[None, :], 0), axis=1)
    return positions - begin


def short_conv(extended, filt, back, count):
    span = filt.shape[0]
    taps = filt.astype(jnp.float32)
    total = jnp.zeros((count, extended.shape[1]), jnp.float32)
    for step in range(span):
        keep = (back >= step).astype(jnp.float32)[:, None]
        piece = extended[span - 1 - step : span - 1 - step + count].astype(jnp.float32)
        total = total + taps[step][None, :] * piece * keep
    return total


def on_device(
    source_rows,
    short_filters,
    medium_filters,
    skip_gain,
    out_weight,
    doc_lengths,
    block_packing_device,
):
    stretches = lax.axis_size("ctx")
    rank_me = lax.axis_index("ctx")
    nb_own = block_packing_device.shape[1]
    blk = source_rows.shape[0] // stretches
    rows = nb_own * blk
    width = source_rows.shape[2]
    se_len = short_filters.shape[1]
    mr_len = medium_filters.shape[0]
    member = jnp.any(block_packing_device == rank_me, axis=1)
    flags = member.astype(jnp.int32)
    slots = jnp.cumsum(flags) - flags
    blocks = source_rows.reshape(stretches, blk, 3, width)
    outgoing = jnp.where(
        member[:, None, None, None], jnp.take(blocks, slots, axis=0), jnp.zeros((), jnp.bfloat16)
    )
    incoming = lax.all_to_all(outgoing, "ctx", split_axis=0, concat_axis=0, tiled=True)
    wanted = lax.dynamic_index_in_dim(block_packing_device, rank_me, 0, keepdims=False)
    stretch = jnp.take(incoming, wanted, axis=0).reshape(rows, 3, width)
    ends = jnp.cumsum(doc_lengths)
    starts = ends - doc_lengths
    base = rank_me * rows
    positions = base + jnp.arange(rows, dtype=jnp.int32)
    back = reach_back(positions, starts)
    span_cols = rows + mr_len - 1
    edge = stretch[rows - (se_len - 1) :]
    earlier = passed_along(edge, "ctx", 1)
    extended = jnp.concatenate([earlier, stretch], axis=0)
    query = short_conv(extended[:, 0], short_filters[0], back, rows)
    keyed = short_conv(extended[:, 1], short_filters[1], back, rows)
    valued = short_conv(extended[:, 2], short_filters[2], back, rows)
    z_vals = (keyed * valued).astype(jnp.bfloat16)
    z_prev = passed_along(z_vals[rows - (mr_len - 1) :], "ctx", 1)
    z_ext = jnp.concatenate([z_prev, z_vals], axis=0)
    groups_dev = medium_filters.shape[1]
    per_group = width // groups_dev
    reversed_taps = jnp.transpose(medium_filters[::-1])
    line = jnp.concatenate([reversed_taps, jnp.zeros((groups_dev, rows), jnp.bfloat16)], axis=1)
    band = jnp.tile(line, (1, rows + 1))[:, : rows * span_cols].reshape(groups_dev, rows, span_cols)
    ext_pos = base - (mr_len - 1) + jnp.arange(span_cols, dtype=jnp.int32)
    begin_rows = positions - back
    keep = ext_pos[None, :] >= begin_rows[:, None]
    band = jnp.where(keep[None, :, :], band, jnp.zeros((), jnp.bfloat16))
    medium = jnp.einsum(
        "gip,pgc->igc",
        band,
        z_ext.reshape(span_cols, groups_dev, per_group),
        preferred_element_type=jnp.float32,
    ).reshape(rows, width)
    hidden = (query * (medium + skip_gain[None, :] * z_vals.astype(jnp.float32))).astype(
        jnp.bfloat16
    )
    partial_value = jnp.dot(
        hidden,
        lax.all_gather(out_weight, "ctx", axis=1, tiled=True),
        preferred_element_type=jnp.float32,
    )
    return lax.psum_scatter(
        partial_value.astype(jnp.bfloat16), "mp", scatter_dimension=1, tiled=True
    )


def solution(mesh):
    return jax.shard_map(
        on_device,
        mesh=mesh,
        in_specs=(
            P("ctx", None, "mp"),
            P(None, None, "mp"),
            P(None, "mp"),
            P("mp"),
            P("mp", "ctx"),
            P(),
            P(),
        ),
        out_specs=P("ctx", "mp"),
        check_vma=False,
    )
```

profile of v0, /device:TPU:4, one launch (start us, length us, event | category | flops | bytes accessed | tf_op | source)
XLA Modules:
  0.0 223.7 jit_solution(3496047976561221424)
XLA Ops:
  6.5 0.0 copy-start
  6.5 0.0 all-gather.2.cloned.1.call-start
  6.5 0.7 all-gather.2.cloned.1.call-update
  7.3 0.7 compare_reduce_fusion
  8.0 0.1 copy.20
  8.1 0.1 reduce-window.14
  8.1 0.1 fusion.109
  8.3 0.0 copy-done
  8.3 0.6 gather_fusion
  8.9 0.0 copy-start.1
  8.9 0.0 copy-start.5
  9.0 0.0 copy-start.2
  9.0 1.5 select_select_fusion
  10.5 10.4 %all-to-all-start = ((bf16[32,16,3,512]{3,1,2,0:T(8,128)(2,1)}), bf16[32,16,3,512]{3,1,2,0:T(8,128)(2,1)S(1)}, u32[]{:S(2)}, u32[]{:S(2)}) async-start(bf16[32,16,3,512]{3,1,2,0:T(8,128)(2,1)} %select_select_fusion), calls=%async_computation | async-start | bytes 3145728 | tf_op jit(solution)/shard_map/all_to_all | solution.py:53
  20.9 0.0 reduce-scatter.2.cloned.1.call-start
  20.9 0.0 copy-done.1
  20.9 0.2 dynamic-slice_reduce_fusion
  21.1 0.1 broadcast_in_dim.54
  21.2 0.1 broadcast_in_dim.55
  21.3 0.0 copy-done.5
  21.3 0.2 reduce-window.15
  21.5 0.1 select_reduce_fusion
  21.6 0.0 copy-done.2
  21.6 0.0 copy-start.4
  21.7 0.6 fusion.111
  22.3 44.0 %all-to-all-done = bf16[32,16,3,512]{3,1,2,0:T(8,128)(2,1)S(1)} async-done(((bf16[32,16,3,512]{3,1,2,0:T(8,128)(2,1)}), bf16[32,16,3,512]{3,1,2,0:T(8,128)(2,1)S(1)}, u32[]{:S(2)}, u32[]{:S(2)}) %all-to-all-start) | async-done | bytes 1572896 | tf_op jit(solution)/shard_map/all_to_all | solution.py:53
  66.3 1.5 gather_fusion.1
  67.9 1.2 copy.22
  69.1 0.2 bitcast_select_fusion
  69.3 2.5 %collective-permute-start = (bf16[6,3,512]{2,0,1:T(8,128)(2,1)S(1)}, bf16[6,3,512]{2,0,1:T(8,128)(2,1)S(1)}, u32[]{:S(2)}, u32[]{:S(2)}) collective-permute-start(bf16[6,3,512]{2,0,1:T(8,128)(2,1)S(1)} %slice.268), channel_id=1, source_target_pairs={{0,16},{16,32},{32,48},{48,64},{64,80},{80,96},{96,112},{112,128},... | collective-permute-start | bytes 55304 | tf_op jit(solution)/shard_map/ppermute | solution.py:10
  71.7 0.1 rev.3
  71.8 0.6 tile.4
  72.4 0.8 copy.25
  73.2 3.0 %slice.325 = bf16[32,98048]{1,0:T(8,128)(2,1)} slice(bf16[32,98688]{1,0:T(8,128)(2,1)S(1)} %bitcast.156), slice={[0:32], [0:98048]} | slice | bytes 12550144 | tf_op jit(solution)/shard_map/slice | solution.py:75
  76.2 18.4 %reshape.310 = bf16[32,256,383]{2,1,0:T(8,128)(2,1)} reshape(bf16[32,98048]{1,0:T(8,128)(2,1)} %slice.325) | data formatting | bytes 12550144 | tf_op jit(solution)/shard_map/reshape | solution.py:75
  94.6 0.0 collective-permute-done
  94.6 1.6 fusion.7
  96.2 2.5 %collective-permute-start.1 = (bf16[127,512]{1,0:T(8,128)(2,1)S(1)}, bf16[127,512]{1,0:T(8,128)(2,1)S(1)}, u32[]{:S(2)}, u32[]{:S(2)}) collective-permute-start(bf16[127,512]{1,0:T(8,128)(2,1)S(1)} %slice.324), channel_id=1, source_target_pairs={{0,16},{16,32},{32,48},{48,64},{64,80},{80,96},{96,112},{112,128},... | collective-permute-start | bytes 390152 | tf_op jit(solution)/shard_map/ppermute | solution.py:10
  98.8 0.1 broadcast_compare_fusion
  98.9 7.1 %collective-permute-done.1 = bf16[127,512]{1,0:T(8,128)(2,1)S(1)} collective-permute-done((bf16[127,512]{1,0:T(8,128)(2,1)S(1)}, bf16[127,512]{1,0:T(8,128)(2,1)S(1)}, u32[]{:S(2)}, u32[]{:S(2)}) %collective-permute-start.1) | collective-permute-done | bytes 130080 | tf_op jit(solution)/shard_map/ppermute | solution.py:10
  106.0 0.1 pad_maximum_fusion
  106.0 0.2 copy.23
  106.3 5.6 %fusion = f32[32,16,256]{2,1,0:T(8,128)} fusion(bf16[383,32,16]{0,2,1:T(8,128)(2,1)S(1)} %bitcast.158, bf16[32,256,383]{2,1,0:T(8,128)(2,1)} %reshape.310, pred[256,383]{1,0:T(8,128)(4,1)S(1)} %broadcast_compare_fusion), kind=kOutput, calls=%fused_computation.3 | convolution fusion | flops 103538688 | bytes 7289600 | tf_op jit(solution)/shard_map/gip,pgc->igc/dot_general | solution.py:80
  111.8 1.2 copy.24
  113.1 26.6 %all-gather.2.cloned.1.call-done = bf16[512,8192]{1,0:T(8,128)(2,1)} async-done(((bf16[512,256]{1,0:T(8,128)(2,1)}), bf16[512,8192]{1,0:T(8,128)(2,1)}) %all-gather.2.cloned.1.call-update) | async-done | bytes 8388624 | tf_op jit(solution)/shard_map/all_gather | solution.py:91
  139.7 8.1 %convolution_convert_fusion = bf16[256,8192]{1,0:T(8,128)(2,1)} fusion(bf16[512,8192]{1,0:T(8,128)(2,1)} %all-gather.2.cloned.1.call-done, f32[256,512]{1,0:T(8,128)S(1)} %copy.24, bf16[256,512]{1,0:T(8,128)(2,1)S(1)} %fusion.7, bf16[6,3,512]{2,0,1:T(8,128)(2,1)S(1)} %collective-permute-done, bf16[256,3,512]{2,0,1:T(8,128)(2,1)S(1)} %bitcast_select_fusion, ...), kind=kOutput, calls=%fused_computation.2 | convolution fusion | flops 2156920832 | bytes 14466048 | tf_op jit(solution)/shard_map/dot_general | solution.py:89
  147.8 0.0 reduce-scatter.2.cloned.1.call-update
  147.8 69.1 %reduce-scatter.2.cloned.1.call-done = bf16[256,512]{1,0:T(8,128)(2,1)} async-done(((bf16[256,8192]{1,0:T(8,128)(2,1)}), bf16[256,512]{1,0:T(8,128)(2,1)}) %reduce-scatter.2.cloned.1.call-update) | async-done | bytes 262160 | tf_op jit(solution)/shard_map/reduce_scatter | solution.py:94
  (19 shorter events, 0.2 us)
Async XLA Ops:
  6.5 1.7 copy-start
  6.5 133.2 %all-gather.2.cloned.1.call-start = ((), (), s32[]{:S(2)}) async-start(), calls=%async_computation.2 | async-start | bytes 8650752 | tf_op jit(solution)/shard_map/all_gather | solution.py:91
  8.9 12.0 %copy-start.1 = (s32[32,16]{0,1:T(8,128)S(1)}, s32[32,16]{0,1:T(8,128)}, u32[]{:S(2)}) copy-start(s32[32,16]{0,1:T(8,128)} %param.13) | copy-start | bytes 6148
  8.9 12.3 %copy-start.5 = (s32[8]{0:T(128)S(1)}, s32[8]{0:T(128)}, u32[]{:S(2)}) copy-start(s32[8]{0:T(128)} %param.12) | copy-start | bytes 100
  9.0 12.7 %copy-start.2 = (bf16[3,7,512]{2,1,0:T(8,128)(2,1)S(1)}, bf16[3,7,512]{2,1,0:T(8,128)(2,1)}, u32[]{:S(2)}) copy-start(bf16[3,7,512]{2,1,0:T(8,128)(2,1)} %param.8) | copy-start | bytes 64516
  10.5 61.2 %copy-start.3 = (bf16[128,32]{0,1:T(8,128)(2,1)S(1)}, bf16[128,32]{0,1:T(8,128)(2,1)}, u32[]{:S(2)}) copy-start(bf16[128,32]{0,1:T(8,128)(2,1)} %param.9) | copy-start | bytes 24580
  10.5 55.8 %all-to-all-start = ((bf16[32,16,3,512]{3,1,2,0:T(8,128)(2,1)}), bf16[32,16,3,512]{3,1,2,0:T(8,128)(2,1)S(1)}, u32[]{:S(2)}, u32[]{:S(2)}) async-start(bf16[32,16,3,512]{3,1,2,0:T(8,128)(2,1)} %select_select_fusion), calls=%async_computation | async-start | bytes 3145728 | tf_op jit(solution)/shard_map/all_to_all | solution.py:53
  20.9 196.0 %reduce-scatter.2.cloned.1.call-start = ((), (), s32[]{:S(2)}) async-start(), calls=%async_computation.3 | async-start | bytes 4456448 | tf_op jit(solution)/shard_map/reduce_scatter | solution.py:94
  21.6 73.0 %copy-start.4 = (f32[256]{0:T(256)}, f32[256]{0:T(256)S(1)}, u32[]{:S(2)}) copy-start(f32[256]{0:T(256)S(1)} %get-tuple-element.38) | copy-start | bytes 3076
  69.3 25.3 %collective-permute-start = (bf16[6,3,512]{2,0,1:T(8,128)(2,1)S(1)}, bf16[6,3,512]{2,0,1:T(8,128)(2,1)S(1)}, u32[]{:S(2)}, u32[]{:S(2)}) collective-permute-start(bf16[6,3,512]{2,0,1:T(8,128)(2,1)S(1)} %slice.268), channel_id=1, source_target_pairs={{0,16},{16,32},{32,48},{48,64},{64,80},{80,96},{96,112},{112,128},... | collective-permute-start | bytes 55304 | tf_op jit(solution)/shard_map/ppermute | solution.py:10
  96.2 9.8 %collective-permute-start.1 = (bf16[127,512]{1,0:T(8,128)(2,1)S(1)}, bf16[127,512]{1,0:T(8,128)(2,1)S(1)}, u32[]{:S(2)}, u32[]{:S(2)}) collective-permute-start(bf16[127,512]{1,0:T(8,128)(2,1)S(1)} %slice.324), channel_id=1, source_target_pairs={{0,16},{16,32},{32,48},{48,64},{64,80},{80,96},{96,112},{112,128},... | collective-permute-start | bytes 390152 | tf_op jit(solution)/shard_map/ppermute | solution.py:10
Sparse Core Ops, SparseCore 0:
  10.4 129.2 all-gather.1
  148.0 68.8 reduce-scatter.1
where the time goes:
time: 224 us
  waiting for transfers between devices  148 us (66%)
  local copies, waits for them, and re-layouts  28.8 us (13%)
  starting transfers between devices  15.4 us (7%)
  matrix products  13.7 us (6%)
  between operations  13.6 us (6%)
  other arithmetic  4.66 us (2%)
    reduce_scatter x1, waiting for transfers between devices, on_device(): lax.psum_scatter(partial_value.astype(jnp.bfloat16), 'mp', scatter_dimens...  69.1 us
    all_to_all x1, waiting for transfers between devices, on_device(): lax.all_to_all(outgoing, 'ctx', split_axis=0, concat_axis=0, tiled=True)  44 us
    all_gather x1, waiting for transfers between devices, on_device(): lax.all_gather(out_weight, 'ctx', axis=1, tiled=True)  26.6 us
    reshape x1, local copies, waits for them, and re-layouts, on_device(): jnp.tile(line, (1, rows + 1))[:, :rows * span_cols]  18.4 us
    all_to_all x1, starting transfers between devices, on_device(): lax.all_to_all(outgoing, 'ctx', split_axis=0, concat_axis=0, tiled=True)  10.4 us
    dot_general x1, matrix products, on_device(): jnp.dot(hidden, lax.all_gather(out_weight, 'ctx', axis=1, tiled=True), pr...  8.1 us
    ppermute x2, waiting for transfers between devices, passed_along(): return lax.ppermute(block, axis, route)  7.09 us
    dot_general x1, matrix products, on_device(): jnp.einsum('gip,pgc->igc', band, z_ext.reshape(span_cols, groups_dev, per...  5.56 us
  transfers between devices with their start and end apart: 5, of which 4 were waited for; matrix products, arithmetic and copies ran while one was open for 17% of the time, Pallas kernels for 0%

commit v1 on v0

v1 whole, which is shorter than its diff:
```python
import functools

import jax
import jax.numpy as jnp
from jax import lax
from jax.experimental import pallas as pl
from jax.experimental.pallas import tpu as pltpu
from jax.sharding import Mesh, PartitionSpec as P

CTX = ("y", "x")
SHAPE4 = (8, 4, 8, 2)
BLK = 16
TAIL = 8
HALF = 128
F32, BF16 = jnp.float32, jnp.bfloat16


def smem():
    return pl.BlockSpec(memory_space=pltpu.SMEM)


def vmem():
    return pl.BlockSpec(memory_space=pltpu.VMEM)


def stretch_id():
    return lax.axis_index("y") * lax.axis_size("x") + lax.axis_index("x")


def call(body, outs, ins, args, flops, scratch=(), name=None):
    moved = sum(a.size * a.dtype.itemsize for a in args)
    moved += sum(o.size * o.dtype.itemsize for o in outs)
    return pl.pallas_call(
        body,
        out_shape=outs,
        in_specs=ins,
        out_specs=[vmem()] * len(outs),
        scratch_shapes=list(scratch),
        cost_estimate=pl.CostEstimate(flops=flops, bytes_accessed=moved, transcendentals=0),
        name=name,
    )(*args)


def reach_back(lengths, first, shape):
    at = first + lax.broadcasted_iota(jnp.int32, shape, 0)
    begin = jnp.zeros(shape, jnp.int32)
    start = jnp.int32(0)
    for doc in range(lengths.shape[0]):
        begin = jnp.where(at >= start, start, begin)
        start = start + lengths[doc]
    return at - begin


def short_rows(window, taps_ref, which, back):
    count = back.shape[0]
    total = jnp.zeros(back.shape, F32)
    for step in range(taps_ref.shape[1]):
        tap = taps_ref[which, step : step + 1, :].astype(F32)
        piece = window[TAIL - step : TAIL - step + count]
        total = total + jnp.where(back >= step, tap * piece, 0.0)
    return total


def pack_kernel(bpd, src, kv, q):
    me = stretch_id()

    def one(c, slot):
        mine = jnp.int32(0)
        for k in range(bpd.shape[1]):
            mine = mine | (bpd[c, k] == me).astype(jnp.int32)
        rows = pl.ds(pl.multiple_of(slot * BLK, BLK), BLK)
        kv[c, 0] = src[1, rows, :]
        kv[c, 1] = src[2, rows, :]
        q[c] = src[0, rows, :]
        return slot + mine

    lax.fori_loop(0, bpd.shape[0], one, jnp.int32(0))


def toeplitz_kernel(line, out):
    def one(g, carry):
        row = jnp.broadcast_to(line[pl.ds(g, 1), :], out.shape[1:])
        out[g] = pltpu.roll(row, 0, 1, stride=1, stride_axis=0).astype(BF16)
        return carry

    lax.fori_loop(0, out.shape[0], one, 0)


def z_kernel(bpd, lengths, kv, taps, z, send, head, buf):
    me = stretch_id()
    rows, width = z.shape
    for i in range(2):
        buf[i, 0:TAIL, :] = jnp.zeros((TAIL, width), F32)
    for k in range(rows // BLK):
        s = bpd[me, k]
        for i in range(2):
            buf[i, TAIL + k * BLK : TAIL + (k + 1) * BLK, :] = kv[s, i].astype(F32)

    step = 32

    def chunk(r, carry):
        at = pl.multiple_of(r * step, step)
        back = reach_back(lengths, me * rows + at, (step, width))
        wide = pl.ds(at, step + TAIL)
        keyed = short_rows(buf[0, wide, :], taps, 1, back)
        valued = short_rows(buf[1, wide, :], taps, 2, back)
        z[pl.ds(at, step), :] = (keyed * valued).astype(BF16)
        return carry

    lax.fori_loop(0, rows // step, chunk, 0)
    send[0:HALF, :] = z[rows - HALF :, :]
    for i in range(2):
        send[HALF + i * TAIL : HALF + (i + 1) * TAIL, :] = buf[i, rows : rows + TAIL, :].astype(BF16)
        head[i * TAIL : (i + 1) * TAIL, :] = buf[i, TAIL : 2 * TAIL, :].astype(BF16)


def medium_kernel(lengths, z, recv, head, taps, bands, gain, out, ext):
    me = stretch_id()
    rows, width = z.shape
    back = reach_back(lengths, me * rows, (TAIL, width))
    fixed = []
    for i in range(2):
        tail = recv[HALF + i * TAIL : HALF + (i + 1) * TAIL, :].astype(F32)
        mine = head[i * TAIL : (i + 1) * TAIL, :].astype(F32)
        fixed.append(short_rows(jnp.concatenate([tail, mine], axis=0), taps, 1 + i, back))
    first = (fixed[0] * fixed[1]).astype(BF16).astype(F32)
    ext[0:HALF, :] = recv[0:HALF, :]
    ext[HALF:, :] = z[...]
    later = z[TAIL : 2 * TAIL, :].astype(F32)
    ext[HALF : HALF + 2 * TAIL, :] = jnp.concatenate([first, later], axis=0).astype(BF16)
    lane = 128
    per = lane // (width // bands.shape[0])
    group = lax.broadcasted_iota(jnp.int32, (HALF, lane), 1) // (lane // per)
    for b in range(rows // HALF):
        back = reach_back(lengths, me * rows + b * HALF, (HALF, 2 * HALF))
        i = lax.broadcasted_iota(jnp.int32, (HALF, 2 * HALF), 0)
        p = lax.broadcasted_iota(jnp.int32, (HALF, 2 * HALF), 1)
        keep = jnp.where(i + HALF - p <= back, 1.0, 0.0).astype(BF16)
        for t in range(width // lane):
            cols = slice(t * lane, (t + 1) * lane)
            right = ext[b * HALF : (b + 2) * HALF, cols]
            total = jnp.zeros((HALF, lane), F32)
            for g in range(per):
                got = jnp.dot(bands[t * per + g] * keep, right, preferred_element_type=F32)
                total = jnp.where(group == g, got, total)
            zs = ext[(b + 1) * HALF : (b + 2) * HALF, cols].astype(F32)
            out[b * HALF : (b + 1) * HALF, cols] = total + gain[:, cols] * zs


def hidden_kernel(half, bpd, lengths, q, halo, taps, medium, out, buf):
    me = stretch_id()
    width = medium.shape[1]
    rows = medium.shape[0]
    if half == 0:
        buf[0:TAIL, :] = halo[...].astype(F32)
    else:
        s = bpd[me, half * HALF // BLK - 1]
        buf[0:TAIL, :] = q[s].astype(F32)[BLK - TAIL :]
    for k in range(HALF // BLK):
        s = bpd[me, half * HALF // BLK + k]
        buf[TAIL + k * BLK : TAIL + (k + 1) * BLK, :] = q[s].astype(F32)
    step = 32

    def chunk(r, carry):
        at = pl.multiple_of(r * step, step)
        first = half * HALF + at
        back = reach_back(lengths, me * rows + first, (step, width))
        query = short_rows(buf[pl.ds(at, step + TAIL), :], taps, 0, back)
        value = (query * medium[pl.ds(pl.multiple_of(first, step), step), :]).astype(BF16)
        for copy in range(out.shape[0]):
            out[copy, pl.ds(at, step), :] = value
        return carry

    lax.fori_loop(0, HALF // step, chunk, 0)


def project_kernel(own, other, weight, out):
    k = own.shape[1]
    lane = out.shape[2]
    step = 256

    def rows(r, carry):
        at = pl.ds(pl.multiple_of(r * step, step), step)
        for pair in range(out.shape[0] // 2):
            cols = slice(pair * 2 * lane, (pair + 1) * 2 * lane)
            got = jnp.dot(own[at, :], weight[0:k, cols], preferred_element_type=F32)
            got = got + jnp.dot(other[at, :], weight[k:, cols], preferred_element_type=F32)
            got = got.astype(BF16)
            out[2 * pair, at, :] = got[:, :lane]
            out[2 * pair + 1, at, :] = got[:, lane:]
        return carry

    lax.fori_loop(0, own.shape[0] // step, rows, 0)


def shape(dims, dtype=BF16):
    return jax.ShapeDtypeStruct(dims, dtype)


def passed_along(block):
    n = lax.axis_size(CTX)
    return lax.ppermute(block, CTX, [(i, i + 1) for i in range(n - 1)])


def weight_columns(out_weight):
    nx = lax.axis_size("x")
    core = lax.axis_index("core")
    width = out_weight.shape[1] // 2
    halves = (out_weight[:, :width], out_weight[:, width:])
    same = jnp.where(core == 0, halves[0], halves[1])
    flip = jnp.where(core == 0, halves[1], halves[0])
    route = lambda f: [
        (x * 2 + i, (2 * (x % 2) + f(i)) * 2 + x // 2) for x in range(nx) for i in range(2)
    ]
    a = lax.ppermute(same, ("x", "core"), route(lambda i: i))
    b = lax.ppermute(flip, ("x", "core"), route(lambda i: 1 - i))
    straight = lax.axis_index("x") % 2 == core
    own = jnp.where(straight, a, b)
    other = jnp.where(straight, b, a)
    both = jnp.concatenate([own, other], axis=0)
    return lax.all_gather(both, "y", axis=1, tiled=True)


def on_device(
    source_rows,
    short_filters,
    medium_filters,
    skip_gain,
    out_weight,
    doc_lengths,
    block_packing_device,
):
    ny, nx, nz = lax.axis_size("y"), lax.axis_size("x"), lax.axis_size("z")
    stretches = ny * nx
    width = source_rows.shape[2]
    rows = block_packing_device.shape[1] * BLK
    bpd = block_packing_device
    swap = [(0, 1), (1, 0)]

    kv_out, q_out = call(
        pack_kernel,
        [shape((stretches, 2, BLK, width)), shape((stretches, BLK, width))],
        [smem(), vmem()],
        (bpd, source_rows.transpose(1, 0, 2)),
        10**6,
        name="pack",
    )
    kv_in = lax.all_to_all(kv_out, CTX, split_axis=0, concat_axis=0, tiled=True)
    q_in = lax.all_to_all(q_out, CTX, split_axis=0, concat_axis=0, tiled=True)

    weight = weight_columns(out_weight)

    groups = medium_filters.shape[1]
    line = jnp.pad(medium_filters[::-1].T.astype(F32), ((0, 0), (1, HALF - 1)))
    (bands,) = call(
        toeplitz_kernel,
        [shape((groups, HALF, 2 * HALF))],
        [vmem()],
        (line,),
        10**8,
        name="bands",
    )
    bands, kv_in = lax.optimization_barrier((bands, kv_in))

    z, send, head = call(
        z_kernel,
        [shape((rows, width)), shape((HALF + 2 * TAIL, width)), shape((2 * TAIL, width))],
        [smem(), smem(), vmem(), vmem()],
        (bpd, doc_lengths, kv_in, short_filters),
        10**7,
        scratch=[pltpu.VMEM((2, rows + TAIL, width), F32)],
        name="gated",
    )
    recv = passed_along(send)
    (medium,) = call(
        medium_kernel,
        [shape((rows, width), F32)],
        [smem()] + [vmem()] * 6,
        (doc_lengths, z, recv, head, short_filters, bands, skip_gain.reshape(1, width)),
        10**9,
        scratch=[pltpu.VMEM((rows + HALF, width), BF16)],
        name="medium",
    )
    last = lax.dynamic_index_in_dim(bpd, stretch_id(), 0, keepdims=False)[-1]
    q_tail = lax.dynamic_index_in_dim(q_in, last, 0, keepdims=False)[BLK - TAIL :]
    q_halo = passed_along(q_tail)

    pieces = [None, None]
    for half in (1, 0):
        (copies,) = call(
            functools.partial(hidden_kernel, half),
            [shape((nx, HALF, width))],
            [smem(), smem()] + [vmem()] * 4,
            (bpd, doc_lengths, q_in, q_halo if half == 0 else q_tail, short_filters, medium),
            10**7,
            scratch=[pltpu.VMEM((HALF + TAIL, width), F32)],
            name=f"hidden{half}",
        )
        own = lax.all_to_all(copies, "x", split_axis=0, concat_axis=0, tiled=True)
        own = own.reshape(nx * HALF, width)
        other = lax.ppermute(own, "core", swap)
        (partial,) = call(
            project_kernel,
            [shape((nz, nx * HALF, 128))],
            [vmem()] * 3,
            (own, other, weight),
            2 * nx * HALF * 2 * width * nz * 128,
            name=f"project{half}",
        )
        parts = lax.all_to_all(partial, "z", split_axis=0, concat_axis=0, tiled=True)
        total = jnp.sum(parts.astype(F32), axis=0).astype(BF16)
        mine = lax.all_to_all(
            total.reshape(nx, HALF, 128), "x", split_axis=0, concat_axis=0, tiled=True
        )
        pieces[half] = mine
    both = jnp.concatenate(pieces, axis=1)
    return both.transpose(1, 0, 2).reshape(rows, nx * 128)


def solution(mesh):
    ctx, mp = CTX, ("z", "core")
    mesh4 = Mesh(mesh.devices.reshape(SHAPE4), ctx + mp)
    return jax.shard_map(
        on_device,
        mesh=mesh4,
        in_specs=(
            P(ctx, None, mp),
            P(None, None, mp),
            P(None, mp),
            P(mp),
            P(mp, ctx),
            P(),
            P(),
        ),
        out_specs=P(ctx, mp),
        check_vma=False,
    )
```

time: 224 us -> 216 us (0.964)
  the two profiles are of different devices: /device:TPU:4 before, /device:TPU:2 now
where the time goes in v1:
time: 216 us; the launch traced here: 215 us
  waiting for transfers between devices  83.2 us (39%)
  starting transfers between devices  57 us (26%)
  Pallas kernels  29.7 us (14%)
  blocking collectives  20.9 us (10%)
  between operations  15.3 us (7%)
  local copies, waits for them, and re-layouts  6.67 us (3%)
  other arithmetic  2.45 us (1%)
    all_to_all x2, waiting for transfers between devices, on_device(): lax.all_to_all(partial, 'z', split_axis=0, concat_axis=0, tiled=True)  47.9 us
    pallas_call x8, Pallas kernels, call(): pl.pallas_call(body, out_shape=outs, in_specs=ins, out_specs=[vmem()] * l...  29.7 us
    all_to_all x1, waiting for transfers between devices, on_device(): kv_in = lax.all_to_all(kv_out, CTX, split_axis=0, concat_axis=0, tiled=True)  15.9 us
    all_to_all x2, starting transfers between devices, on_device(): lax.all_to_all(partial, 'z', split_axis=0, concat_axis=0, tiled=True)  15.1 us
    all_to_all x1, blocking collectives, on_device(): own = lax.all_to_all(copies, 'x', split_axis=0, concat_axis=0, tiled=True)  12.5 us
    all_to_all x1, starting transfers between devices, on_device(): kv_in = lax.all_to_all(kv_out, CTX, split_axis=0, concat_axis=0, tiled=True)  10.4 us
    all_to_all x1, blocking collectives, on_device(): lax.all_to_all(total.reshape(nx, HALF, 128), 'x', split_axis=0, concat_ax...  8.35 us
    ppermute x2, starting transfers between devices, passed_along(): return lax.ppermute(block, CTX, [(i, i + 1) for i in range(n - 1)])  6.55 us
  transfers between devices with their start and end apart: 13, of which 9 were waited for; matrix products, arithmetic and copies ran while one was open for 2% of the time, Pallas kernels for 12%

profile of v1, /device:TPU:2, one launch (start us, length us, event | category | flops | bytes accessed | tf_op | source)
XLA Modules:
  0.0 215.1 jit_solution(8696175184986293833)
XLA Ops:
  6.5 1.4 copy.18.bpd
  7.9 3.4 %pack.1 = (bf16[32,2,16,512]{3,2,1,0:T(8,128)(2,1)}, bf16[32,16,512]{2,1,0:T(8,128)(2,1)}) custom-call(s32[32,16]{1,0:T(8,128)} %copy.18.bpd, bf16[3,512,512]{2,1,0:T(8,128)(2,1)} %bitcast.17), custom_call_target="tpu_custom_call" | custom-call | flops 1000000 | bytes 3147776 | tf_op jit(solution)/shard_map/pack/pallas_call | solution.py:33
  11.3 10.4 %all-to-all-start.1 = ((bf16[32,2,16,512]{3,2,1,0:T(8,128)(2,1)}), bf16[32,2,16,512]{3,2,1,0:T(8,128)(2,1)S(1)}, u32[]{:S(2)}, u32[]{:S(2)}) async-start(bf16[32,2,16,512]{3,2,1,0:T(8,128)(2,1)} %get-tuple-element.13), calls=%async_computation.1 | async-start | bytes 2097152 | tf_op jit(solution)/shard_map/all_to_all | solution.py:248
  21.7 0.0 all-gather.2.cloned.1.call-start
  21.8 3.4 %collective-permute-start.3 = (bf16[512,128]{1,0:T(8,128)(2,1)S(1)}, bf16[512,128]{1,0:T(8,128)(2,1)S(1)}, u32[]{:S(2)}, u32[]{:S(2)}) collective-permute-start(bf16[512,128]{1,0:T(8,128)(2,1)S(1)} %get-tuple-element.21), channel_id=1, source_target_pairs={{0,0},{1,16},{16,32},{17,48},{32,1},{33,17},{48,33},{49,49},{2,2},... | collective-permute-start | bytes 393224 | tf_op jit(solution)/shard_map/ppermute | solution.py:215
  25.2 2.5 %collective-permute-start.4 = (bf16[512,128]{1,0:T(8,128)(2,1)S(1)}, bf16[512,128]{1,0:T(8,128)(2,1)S(1)}, u32[]{:S(2)}, u32[]{:S(2)}) collective-permute-start(bf16[512,128]{1,0:T(8,128)(2,1)S(1)} %get-tuple-element.22), channel_id=1, source_target_pairs={{0,16},{1,0},{16,48},{17,32},{32,17},{33,1},{48,49},{49,33},{2,18}... | collective-permute-start | bytes 393224 | tf_op jit(solution)/shard_map/ppermute | solution.py:216
  27.7 2.4 %collective-permute-done.3 = bf16[512,128]{1,0:T(8,128)(2,1)S(1)} collective-permute-done((bf16[512,128]{1,0:T(8,128)(2,1)S(1)}, bf16[512,128]{1,0:T(8,128)(2,1)S(1)}, u32[]{:S(2)}, u32[]{:S(2)}) %collective-permute-start.3) | collective-permute-done | bytes 131104 | tf_op jit(solution)/shard_map/ppermute | solution.py:215
  30.2 2.9 %collective-permute-done.4 = bf16[512,128]{1,0:T(8,128)(2,1)S(1)} collective-permute-done((bf16[512,128]{1,0:T(8,128)(2,1)S(1)}, bf16[512,128]{1,0:T(8,128)(2,1)S(1)}, u32[]{:S(2)}, u32[]{:S(2)}) %collective-permute-start.4) | collective-permute-done | bytes 131104 | tf_op jit(solution)/shard_map/ppermute | solution.py:216
  33.1 0.7 pad_maximum_fusion
  33.8 0.0 all-gather.2.cloned.1.call-update
  33.8 15.9 %all-to-all-done.1.kv = bf16[32,2,16,512]{3,2,1,0:T(8,128)(2,1)S(1)} async-done(((bf16[32,2,16,512]{3,2,1,0:T(8,128)(2,1)}), bf16[32,2,16,512]{3,2,1,0:T(8,128)(2,1)S(1)}, u32[]{:S(2)}, u32[]{:S(2)}) %all-to-all-start.1) | async-done | bytes 1048608 | tf_op jit(solution)/shard_map/all_to_all | solution.py:248
  49.8 5.6 %all-to-all-start = ((bf16[32,16,512]{2,1,0:T(8,128)(2,1)}), bf16[32,16,512]{2,1,0:T(8,128)(2,1)S(1)}, u32[]{:S(2)}, u32[]{:S(2)}) async-start(bf16[32,16,512]{2,1,0:T(8,128)(2,1)} %get-tuple-element.12), calls=%async_computation | async-start | bytes 1048576 | tf_op jit(solution)/shard_map/all_to_all | solution.py:249
  55.4 0.1 rev.3
  55.4 0.7 pad_convert_fusion.line
  56.1 4.9 %bands.1 = bf16[32,128,256]{2,1,0:T(8,128)(2,1)} custom-call(f32[32,256]{1,0:T(8,128)} %pad_convert_fusion.line), custom_call_target="tpu_custom_call" | custom-call | flops 100000000 | bytes 2129920 | tf_op jit(solution)/shard_map/bands/pallas_call | solution.py:33
  61.0 3.7 %gated.1 = (bf16[256,512]{1,0:T(8,128)(2,1)}, bf16[144,512]{1,0:T(8,128)(2,1)}, bf16[16,512]{1,0:T(8,128)(2,1)}) custom-call(s32[32,16]{1,0:T(8,128)} %copy.18.bpd, s32[8]{0:T(128)} %lengths.7, bf16[32,2,16,512]{3,2,1,0:T(8,128)(2,1)} %copy-done.1, bf16[3,7,512]{2,1,0:T(8,128)(2,1)} %taps.7), custom_call_target="tpu_custom_call" | custom-call | flops 10000000 | bytes 1498144 | tf_op jit(solution)/shard_map/gated/pallas_call | solution.py:33
  64.7 3.4 %collective-permute-start.1 = (bf16[144,512]{1,0:T(8,128)(2,1)}, bf16[144,512]{1,0:T(8,128)(2,1)S(1)}, u32[]{:S(2)}, u32[]{:S(2)}) collective-permute-start(bf16[144,512]{1,0:T(8,128)(2,1)} %get-tuple-element.16), channel_id=1, source_target_pairs={{0,16},{16,32},{32,48},{48,64},{64,80},{80,96},{96,112},{112,128},... | collective-permute-start | bytes 442376 | tf_op jit(solution)/shard_map/ppermute | solution.py:202
  68.1 1.3 dynamic-slice
  71.1 3.9 %all-to-all-done.q = bf16[32,16,512]{2,1,0:T(8,128)(2,1)S(1)} async-done(((bf16[32,16,512]{2,1,0:T(8,128)(2,1)}), bf16[32,16,512]{2,1,0:T(8,128)(2,1)S(1)}, u32[]{:S(2)}, u32[]{:S(2)}) %all-to-all-start) | async-done | bytes 524320 | tf_op jit(solution)/shard_map/all_to_all | solution.py:249
  75.0 3.2 %collective-permute-start = (bf16[8,512]{1,0:T(8,128)(2,1)S(1)}, bf16[8,512]{1,0:T(8,128)(2,1)S(1)}, u32[]{:S(2)}, u32[]{:S(2)}) collective-permute-start(bf16[8,512]{1,0:T(8,128)(2,1)S(1)} %dynamic-slice_bitcast_fusion.halo), channel_id=1, source_target_pairs={{0,16},{16,32},{32,48},{48,64},{64,80},{80,96},{96,112},{112,128},... | collective-permute-start | bytes 24584 | tf_op jit(solution)/shard_map/ppermute | solution.py:202
  78.2 0.0 collective-permute-done.1.recv
  78.2 0.7 copy-done.10
  78.9 4.0 %medium.1 = f32[256,512]{1,0:T(8,128)} custom-call(s32[8]{0:T(128)} %lengths.7, bf16[256,512]{1,0:T(8,128)(2,1)} %get-tuple-element.15.z, bf16[144,512]{1,0:T(8,128)(2,1)} %copy-done.10, bf16[16,512]{1,0:T(8,128)(2,1)} %get-tuple-element.17.head, bf16[3,7,512]{2,1,0:T(8,128)(2,1)} %taps.7, bf16[32,128,256]{2,1,0:T(8,128)(2,1)} %bands.1, f32[1,512]{1,0:T(1,128)} %bitcast.21), custom_call_target="tpu_custom_call" | custom-call | flops 1000000000 | bytes 3071008 | tf_op jit(solution)/shard_map/medium/pallas_call | solution.py:33
  82.8 0.0 copy-start.8
  82.8 0.6 copy-done.8
  83.4 2.5 %hidden0.1 = bf16[4,128,512]{2,1,0:T(8,128)(2,1)} custom-call(s32[32,16]{1,0:T(8,128)} %copy.18.bpd, s32[8]{0:T(128)} %lengths.7, bf16[32,16,512]{2,1,0:T(8,128)(2,1)} %copy-done, bf16[8,512]{1,0:T(8,128)(2,1)} %copy-done.8, bf16[3,7,512]{2,1,0:T(8,128)(2,1)} %taps.7, f32[256,512]{1,0:T(8,128)} %medium.1), custom_call_target="tpu_custom_call" | custom-call | flops 10000000 | bytes 1604640 | tf_op jit(solution)/shard_map/hidden0/pallas_call | solution.py:33
  86.0 12.5 %all_to_all.40 = bf16[4,128,512]{2,1,0:T(8,128)(2,1)S(1)} all-to-all(bf16[4,128,512]{2,1,0:T(8,128)(2,1)} %hidden0.1), channel_id=1, replica_groups=mesh['y'=8,'x'=4,'z'=8,'core'=2] {'x'}, dimensions={0} | all-to-all | bytes 1048576 | tf_op jit(solution)/shard_map/all_to_all | solution.py:299
  98.5 1.9 collective-permute-start.2
  100.4 2.6 %hidden1.1 = bf16[4,128,512]{2,1,0:T(8,128)(2,1)} custom-call(s32[32,16]{1,0:T(8,128)} %copy.18.bpd, s32[8]{0:T(128)} %lengths.7, bf16[32,16,512]{2,1,0:T(8,128)(2,1)} %copy-done, bf16[8,512]{1,0:T(8,128)(2,1)} %copy-done.7, bf16[3,7,512]{2,1,0:T(8,128)(2,1)} %taps.7, f32[256,512]{1,0:T(8,128)} %medium.1), custom_call_target="tpu_custom_call" | custom-call | flops 10000000 | bytes 1604640 | tf_op jit(solution)/shard_map/hidden1/pallas_call | solution.py:33
  103.0 4.9 %all-to-all-start.5 = ((bf16[4,128,512]{2,1,0:T(8,128)(2,1)}), bf16[4,128,512]{2,1,0:T(8,128)(2,1)S(1)}, u32[]{:S(2)}, u32[]{:S(2)}) async-start(bf16[4,128,512]{2,1,0:T(8,128)(2,1)} %hidden1.1), calls=%async_computation.5 | async-start | bytes 1048576 | tf_op jit(solution)/shard_map/all_to_all | solution.py:299
  107.9 0.8 copy-done.4
  108.7 4.3 %project0.1 = bf16[8,512,128]{2,1,0:T(8,128)(2,1)} custom-call(bf16[512,512]{1,0:T(8,128)(2,1)} %bitcast.16, bf16[512,512]{1,0:T(8,128)(2,1)} %copy-done.4, bf16[1024,1024]{1,0:T(8,128)(2,1)} %all-gather.2.cloned.1.call-done.weight), custom_call_target="tpu_custom_call" | custom-call | flops 1073741824 | bytes 4194304 | tf_op jit(solution)/shard_map/project0/pallas_call | solution.py:33
  113.0 3.8 %all-to-all-done.5 = bf16[4,128,512]{2,1,0:T(8,128)(2,1)S(1)} async-done(((bf16[4,128,512]{2,1,0:T(8,128)(2,1)}), bf16[4,128,512]{2,1,0:T(8,128)(2,1)S(1)}, u32[]{:S(2)}, u32[]{:S(2)}) %all-to-all-start.5) | async-done | bytes 524320 | tf_op jit(solution)/shard_map/all_to_all | solution.py:299
  116.8 11.5 %all-to-all-start.3 = ((bf16[8,512,128]{2,1,0:T(8,128)(2,1)}), bf16[8,512,128]{2,1,0:T(8,128)(2,1)S(1)}, u32[]{:S(2)}, u32[]{:S(2)}) async-start(bf16[8,512,128]{2,1,0:T(8,128)(2,1)} %project0.1), calls=%async_computation.3 | async-start | bytes 2097152 | tf_op jit(solution)/shard_map/all_to_all | solution.py:310
  128.4 1.9 collective-permute-start.5
  130.3 1.9 collective-permute-done.5.other
  132.2 0.8 copy-done.5
  133.0 4.3 %project1.1 = bf16[8,512,128]{2,1,0:T(8,128)(2,1)} custom-call(bf16[512,512]{1,0:T(8,128)(2,1)} %bitcast.14, bf16[512,512]{1,0:T(8,128)(2,1)} %copy-done.5, bf16[1024,1024]{1,0:T(8,128)(2,1)} %all-gather.2.cloned.1.call-done.weight), custom_call_target="tpu_custom_call" | custom-call | flops 1073741824 | bytes 4194304 | tf_op jit(solution)/shard_map/project1/pallas_call | solution.py:33
  137.3 19.6 %all-to-all-done.3 = bf16[8,512,128]{2,1,0:T(8,128)(2,1)S(1)} async-done(((bf16[8,512,128]{2,1,0:T(8,128)(2,1)}), bf16[8,512,128]{2,1,0:T(8,128)(2,1)S(1)}, u32[]{:S(2)}, u32[]{:S(2)}) %all-to-all-start.3) | async-done | bytes 1048608 | tf_op jit(solution)/shard_map/all_to_all | solution.py:310
  156.9 3.6 %all-to-all-start.6 = ((bf16[8,512,128]{2,1,0:T(8,128)(2,1)}), bf16[8,512,128]{2,1,0:T(8,128)(2,1)S(1)}, u32[]{:S(2)}, u32[]{:S(2)}) async-start(bf16[8,512,128]{2,1,0:T(8,128)(2,1)} %project1.1), calls=%async_computation.6 | async-start | bytes 2097152 | tf_op jit(solution)/shard_map/all_to_all | solution.py:310
  160.5 0.8 reduce_sum.24
  161.3 28.3 %all-to-all-done.6 = bf16[8,512,128]{2,1,0:T(8,128)(2,1)S(1)} async-done(((bf16[8,512,128]{2,1,0:T(8,128)(2,1)}), bf16[8,512,128]{2,1,0:T(8,128)(2,1)S(1)}, u32[]{:S(2)}, u32[]{:S(2)}) %all-to-all-start.6) | async-done | bytes 1048608 | tf_op jit(solution)/shard_map/all_to_all | solution.py:310
  189.6 4.8 %all-to-all-start.4 = ((bf16[4,128,128]{2,1,0:T(8,128)(2,1)}), bf16[4,128,128]{2,1,0:T(8,128)(2,1)S(1)}, u32[]{:S(2)}, u32[]{:S(2)}) async-start(bf16[4,128,128]{2,1,0:T(8,128)(2,1)} %bitcast.6), calls=%async_computation.4 | async-start | bytes 262144 | tf_op jit(solution)/shard_map/all_to_all | solution.py:312
  194.4 0.1 reduce_sum.25
  194.5 4.4 %all-to-all-done.4 = bf16[4,128,128]{2,1,0:T(8,128)(2,1)S(1)} async-done(((bf16[4,128,128]{2,1,0:T(8,128)(2,1)}), bf16[4,128,128]{2,1,0:T(8,128)(2,1)S(1)}, u32[]{:S(2)}, u32[]{:S(2)}) %all-to-all-start.4) | async-done | bytes 131104 | tf_op jit(solution)/shard_map/all_to_all | solution.py:312
  198.9 8.3 %all_to_all.41 = bf16[4,128,128]{2,1,0:T(8,128)(2,1)S(1)} all-to-all(bf16[4,128,128]{2,1,0:T(8,128)(2,1)S(1)} %bitcast.19), channel_id=1, replica_groups=mesh['y'=8,'x'=4,'z'=8,'core'=2] {'x'}, dimensions={0} | all-to-all | bytes 262144 | tf_op jit(solution)/shard_map/all_to_all | solution.py:312
  207.3 0.1 copy.20
  207.4 0.8 copy.21
  (24 shorter events, 0.1 us)
Async XLA Ops:
  6.5 15.2 %copy-start.6 = (bf16[512,256]{1,0:T(8,128)(2,1)S(1)}, bf16[512,256]{1,0:T(8,128)(2,1)}, u32[]{:S(2)}) copy-start(bf16[512,256]{1,0:T(8,128)(2,1)} %param.11) | copy-start | bytes 786436
  11.3 44.0 %copy-start.9 = (bf16[128,32]{0,1:T(8,128)(2,1)S(1)}, bf16[128,32]{0,1:T(8,128)(2,1)}, u32[]{:S(2)}) copy-start(bf16[128,32]{0,1:T(8,128)(2,1)} %param.9) | copy-start | bytes 24580
  11.3 38.5 %all-to-all-start.1 = ((bf16[32,2,16,512]{3,2,1,0:T(8,128)(2,1)}), bf16[32,2,16,512]{3,2,1,0:T(8,128)(2,1)S(1)}, u32[]{:S(2)}, u32[]{:S(2)}) async-start(bf16[32,2,16,512]{3,2,1,0:T(8,128)(2,1)} %get-tuple-element.13), calls=%async_computation.1 | async-start | bytes 2097152 | tf_op jit(solution)/shard_map/all_to_all | solution.py:248
  21.7 86.2 %all-gather.2.cloned.1.call-start = ((), (), s32[]{:S(2)}) async-start(), calls=%async_computation.8 | async-start | bytes 2359296 | tf_op jit(solution)/shard_map/all_gather | solution.py:221
  21.8 8.4 %collective-permute-start.3 = (bf16[512,128]{1,0:T(8,128)(2,1)S(1)}, bf16[512,128]{1,0:T(8,128)(2,1)S(1)}, u32[]{:S(2)}, u32[]{:S(2)}) collective-permute-start(bf16[512,128]{1,0:T(8,128)(2,1)S(1)} %get-tuple-element.21), channel_id=1, source_target_pairs={{0,0},{1,16},{16,32},{17,48},{32,1},{33,17},{48,33},{49,49},{2,2},... | collective-permute-start | bytes 393224 | tf_op jit(solution)/shard_map/ppermute | solution.py:215
  25.2 7.9 %collective-permute-start.4 = (bf16[512,128]{1,0:T(8,128)(2,1)S(1)}, bf16[512,128]{1,0:T(8,128)(2,1)S(1)}, u32[]{:S(2)}, u32[]{:S(2)}) collective-permute-start(bf16[512,128]{1,0:T(8,128)(2,1)S(1)} %get-tuple-element.22), channel_id=1, source_target_pairs={{0,16},{1,0},{16,48},{17,32},{32,17},{33,1},{48,49},{49,33},{2,18}... | collective-permute-start | bytes 393224 | tf_op jit(solution)/shard_map/ppermute | solution.py:216
  49.8 11.3 %copy-start.1 = (bf16[32,2,16,512]{3,2,1,0:T(8,128)(2,1)}, bf16[32,2,16,512]{3,2,1,0:T(8,128)(2,1)S(1)}, u32[]{:S(2)}) copy-start(bf16[32,2,16,512]{3,2,1,0:T(8,128)(2,1)S(1)} %all-to-all-done.1.kv) | copy-start | bytes 3145732
  49.8 25.2 %all-to-all-start = ((bf16[32,16,512]{2,1,0:T(8,128)(2,1)}), bf16[32,16,512]{2,1,0:T(8,128)(2,1)S(1)}, u32[]{:S(2)}, u32[]{:S(2)}) async-start(bf16[32,16,512]{2,1,0:T(8,128)(2,1)} %get-tuple-element.12), calls=%async_computation | async-start | bytes 1048576 | tf_op jit(solution)/shard_map/all_to_all | solution.py:249
  64.7 13.4 %collective-permute-start.1 = (bf16[144,512]{1,0:T(8,128)(2,1)}, bf16[144,512]{1,0:T(8,128)(2,1)S(1)}, u32[]{:S(2)}, u32[]{:S(2)}) collective-permute-start(bf16[144,512]{1,0:T(8,128)(2,1)} %get-tuple-element.16), channel_id=1, source_target_pairs={{0,16},{16,32},{32,48},{48,64},{64,80},{80,96},{96,112},{112,128},... | collective-permute-start | bytes 442376 | tf_op jit(solution)/shard_map/ppermute | solution.py:202
  75.0 7.8 %copy-start = (bf16[32,16,512]{2,1,0:T(8,128)(2,1)}, bf16[32,16,512]{2,1,0:T(8,128)(2,1)S(1)}, u32[]{:S(2)}) copy-start(bf16[32,16,512]{2,1,0:T(8,128)(2,1)S(1)} %all-to-all-done.q) | copy-start | bytes 1572868
  75.0 11.0 %copy-start.7 = (bf16[8,512]{1,0:T(8,128)(2,1)}, bf16[8,512]{1,0:T(8,128)(2,1)S(1)}, u32[]{:S(2)}) copy-start(bf16[8,512]{1,0:T(8,128)(2,1)S(1)} %dynamic-slice_bitcast_fusion.halo) | copy-start | bytes 24580
  75.0 7.8 %collective-permute-start = (bf16[8,512]{1,0:T(8,128)(2,1)S(1)}, bf16[8,512]{1,0:T(8,128)(2,1)S(1)}, u32[]{:S(2)}, u32[]{:S(2)}) collective-permute-start(bf16[8,512]{1,0:T(8,128)(2,1)S(1)} %dynamic-slice_bitcast_fusion.halo), channel_id=1, source_target_pairs={{0,16},{16,32},{32,48},{48,64},{64,80},{80,96},{96,112},{112,128},... | collective-permute-start | bytes 24584 | tf_op jit(solution)/shard_map/ppermute | solution.py:202
  78.2 0.7 copy-start.10
  82.8 0.6 copy-start.8
  98.5 9.4 %copy-start.3 = (bf16[4,128,512]{2,1,0:T(8,128)(2,1)}, bf16[4,128,512]{2,1,0:T(8,128)(2,1)S(1)}, u32[]{:S(2)}) copy-start(bf16[4,128,512]{2,1,0:T(8,128)(2,1)S(1)} %all_to_all.40) | copy-start | bytes 1572868
  98.5 9.4 %collective-permute-start.2 = (bf16[512,512]{1,0:T(8,128)(2,1)S(1)}, bf16[512,512]{1,0:T(8,128)(2,1)S(1)}, u32[]{:S(2)}, u32[]{:S(2)}) collective-permute-start(bf16[512,512]{1,0:T(8,128)(2,1)S(1)} %bitcast.15), channel_id=1, source_target_pairs={{0,1},{1,0},{2,3},{3,2},{4,5},{5,4},{6,7},{7,6},{8,9},{9,8},{10,11... | collective-permute-start | bytes 1572872 | tf_op jit(solution)/shard_map/ppermute | solution.py:301
  103.0 13.9 %all-to-all-start.5 = ((bf16[4,128,512]{2,1,0:T(8,128)(2,1)}), bf16[4,128,512]{2,1,0:T(8,128)(2,1)S(1)}, u32[]{:S(2)}, u32[]{:S(2)}) async-start(bf16[4,128,512]{2,1,0:T(8,128)(2,1)} %hidden1.1), calls=%async_computation.5 | async-start | bytes 1048576 | tf_op jit(solution)/shard_map/all_to_all | solution.py:299
  107.9 0.8 copy-start.4
  116.8 15.3 %copy-start.2 = (bf16[4,128,512]{2,1,0:T(8,128)(2,1)}, bf16[4,128,512]{2,1,0:T(8,128)(2,1)S(1)}, u32[]{:S(2)}) copy-start(bf16[4,128,512]{2,1,0:T(8,128)(2,1)S(1)} %all-to-all-done.5) | copy-start | bytes 1572868
  116.8 40.1 %all-to-all-start.3 = ((bf16[8,512,128]{2,1,0:T(8,128)(2,1)}), bf16[8,512,128]{2,1,0:T(8,128)(2,1)S(1)}, u32[]{:S(2)}, u32[]{:S(2)}) async-start(bf16[8,512,128]{2,1,0:T(8,128)(2,1)} %project0.1), calls=%async_computation.3 | async-start | bytes 2097152 | tf_op jit(solution)/shard_map/all_to_all | solution.py:310
  128.4 3.8 %collective-permute-start.5 = (bf16[512,512]{1,0:T(8,128)(2,1)S(1)}, bf16[512,512]{1,0:T(8,128)(2,1)S(1)}, u32[]{:S(2)}, u32[]{:S(2)}) collective-permute-start(bf16[512,512]{1,0:T(8,128)(2,1)S(1)} %bitcast.13), channel_id=1, source_target_pairs={{0,1},{1,0},{2,3},{3,2},{4,5},{5,4},{6,7},{7,6},{8,9},{9,8},{10,11... | collective-permute-start | bytes 1572872 | tf_op jit(solution)/shard_map/ppermute | solution.py:301
  132.2 0.8 copy-start.5
  156.9 32.7 %all-to-all-start.6 = ((bf16[8,512,128]{2,1,0:T(8,128)(2,1)}), bf16[8,512,128]{2,1,0:T(8,128)(2,1)S(1)}, u32[]{:S(2)}, u32[]{:S(2)}) async-start(bf16[8,512,128]{2,1,0:T(8,128)(2,1)} %project1.1), calls=%async_computation.6 | async-start | bytes 2097152 | tf_op jit(solution)/shard_map/all_to_all | solution.py:310
  189.6 9.3 %all-to-all-start.4 = ((bf16[4,128,128]{2,1,0:T(8,128)(2,1)}), bf16[4,128,128]{2,1,0:T(8,128)(2,1)S(1)}, u32[]{:S(2)}, u32[]{:S(2)}) async-start(bf16[4,128,128]{2,1,0:T(8,128)(2,1)} %bitcast.6), calls=%async_computation.4 | async-start | bytes 262144 | tf_op jit(solution)/shard_map/all_to_all | solution.py:312
Sparse Core Ops, SparseCore 0:
  33.9 61.9 all-gather.1

commit v2 on v1

--- a/solution.py
+++ b/solution.py
@@ -1,5 +1,3 @@
-import functools
-
 import jax
 import jax.numpy as jnp
 from jax import lax
@@ -66,15 +64,15 @@
 
     def one(c, slot):
         mine = jnp.int32(0)
-        for k in range(bpd.shape[1]):
-            mine = mine | (bpd[c, k] == me).astype(jnp.int32)
+        for k in range(bpd.shape[0]):
+            mine = mine | (bpd[k, c] == me).astype(jnp.int32)
         rows = pl.ds(pl.multiple_of(slot * BLK, BLK), BLK)
         kv[c, 0] = src[1, rows, :]
         kv[c, 1] = src[2, rows, :]
         q[c] = src[0, rows, :]
         return slot + mine
 
-    lax.fori_loop(0, bpd.shape[0], one, jnp.int32(0))
+    lax.fori_loop(0, bpd.shape[1], one, jnp.int32(0))
 
 
 def toeplitz_kernel(line, out):
@@ -92,7 +90,7 @@
     for i in range(2):
         buf[i, 0:TAIL, :] = jnp.zeros((TAIL, width), F32)
     for k in range(rows // BLK):
-        s = bpd[me, k]
+        s = bpd[k, me]
         for i in range(2):
             buf[i, TAIL + k * BLK : TAIL + (k + 1) * BLK, :] = kv[s, i].astype(F32)
 
@@ -147,50 +145,80 @@
             out[b * HALF : (b + 1) * HALF, cols] = total + gain[:, cols] * zs
 
 
-def hidden_kernel(half, bpd, lengths, q, halo, taps, medium, out, buf):
+def hidden_kernel(bpd, lengths, q, halo, taps, medium, out, buf):
     me = stretch_id()
-    width = medium.shape[1]
-    rows = medium.shape[0]
-    if half == 0:
-        buf[0:TAIL, :] = halo[...].astype(F32)
-    else:
-        s = bpd[me, half * HALF // BLK - 1]
-        buf[0:TAIL, :] = q[s].astype(F32)[BLK - TAIL :]
-    for k in range(HALF // BLK):
-        s = bpd[me, half * HALF // BLK + k]
-        buf[TAIL + k * BLK : TAIL + (k + 1) * BLK, :] = q[s].astype(F32)
+    rows, width = medium.shape
+    buf[0:TAIL, :] = halo[...].astype(F32)
+    for k in range(rows // BLK):
+        buf[TAIL + k * BLK : TAIL + (k + 1) * BLK, :] = q[bpd[k, me]].astype(F32)
     step = 32
 
     def chunk(r, carry):
         at = pl.multiple_of(r * step, step)
-        first = half * HALF + at
-        back = reach_back(lengths, me * rows + first, (step, width))
+        back = reach_back(lengths, me * rows + at, (step, width))
         query = short_rows(buf[pl.ds(at, step + TAIL), :], taps, 0, back)
-        value = (query * medium[pl.ds(pl.multiple_of(first, step), step), :]).astype(BF16)
+        value = (query * medium[pl.ds(at, step), :]).astype(BF16)
         for copy in range(out.shape[0]):
             out[copy, pl.ds(at, step), :] = value
         return carry
 
-    lax.fori_loop(0, HALF // step, chunk, 0)
+    lax.fori_loop(0, rows // step, chunk, 0)
 
 
 def project_kernel(own, other, weight, out):
     k = own.shape[1]
     lane = out.shape[2]
-    step = 256
-
-    def rows(r, carry):
-        at = pl.ds(pl.multiple_of(r * step, step), step)
-        for pair in range(out.shape[0] // 2):
-            cols = slice(pair * 2 * lane, (pair + 1) * 2 * lane)
-            got = jnp.dot(own[at, :], weight[0:k, cols], preferred_element_type=F32)
-            got = got + jnp.dot(other[at, :], weight[k:, cols], preferred_element_type=F32)
-            got = got.astype(BF16)
-            out[2 * pair, at, :] = got[:, :lane]
-            out[2 * pair + 1, at, :] = got[:, lane:]
-        return carry
-
-    lax.fori_loop(0, own.shape[0] // step, rows, 0)
+    for pair in range(out.shape[0] // 2):
+        cols = slice(pair * 2 * lane, (pair + 1) * 2 * lane)
+        got = jnp.dot(own[...], weight[0:k, cols], preferred_element_type=F32)
+        got = got + jnp.dot(other[...], weight[k:, cols], preferred_element_type=F32)
+        got = got.astype(BF16)
+        out[2 * pair] = got[:, :lane]
+        out[2 * pair + 1] = got[:, lane:]
+
+
+def project(own, other, weight, nx, nz):
+    rows = own.shape[0] // nx
+    k = own.shape[1]
+    cols = weight.shape[1]
+    lane = cols // nz
+    return pl.pallas_call(
+        project_kernel,
+        grid=(nx,),
+        in_specs=[
+            pl.BlockSpec((rows, k), lambda i: (i, 0)),
+            pl.BlockSpec((rows, k), lambda i: (i, 0)),
+            pl.BlockSpec((2 * k, cols), lambda i: (0, 0)),
+        ],
+        out_specs=pl.BlockSpec((nz, None, rows, lane), lambda i: (0, i, 0, 0)),
+        out_shape=shape((nz, nx, rows, lane)),
+        cost_estimate=pl.CostEstimate(
+            flops=4 * nx * rows * k * cols, bytes_accessed=8 << 20, transcendentals=0
+        ),
+        name="project",
+    )(own, other, weight)
+
+
+def sum_kernel(parts, out):
+    total = parts[0].astype(F32)
+    for i in range(1, parts.shape[0]):
+        total = total + parts[i].astype(F32)
+    out[...] = total.astype(BF16)
+
+
+def summed(parts):
+    nz, nx, rows, lane = parts.shape
+    return pl.pallas_call(
+        sum_kernel,
+        grid=(nx,),
+        in_specs=[pl.BlockSpec((nz, None, rows, lane), lambda i: (0, i, 0, 0))],
+        out_specs=pl.BlockSpec((rows, lane), lambda i: (0, i)),
+        out_shape=shape((rows, nx * lane)),
+        cost_estimate=pl.CostEstimate(
+            flops=parts.size, bytes_accessed=2 * parts.size, transcendentals=0
+        ),
+        name="total",
+    )(parts)
 
 
 def shape(dims, dtype=BF16):
@@ -234,8 +262,7 @@
     stretches = ny * nx
     width = source_rows.shape[2]
     rows = block_packing_device.shape[1] * BLK
-    bpd = block_packing_device
-    swap = [(0, 1), (1, 0)]
+    bpd = block_packing_device.T
 
     kv_out, q_out = call(
         pack_kernel,
@@ -281,40 +308,26 @@
         scratch=[pltpu.VMEM((rows + HALF, width), BF16)],
         name="medium",
     )
-    last = lax.dynamic_index_in_dim(bpd, stretch_id(), 0, keepdims=False)[-1]
+    medium, q_in = lax.optimization_barrier((medium, q_in))
+    last = lax.dynamic_index_in_dim(bpd[-1], stretch_id(), 0, keepdims=False)
     q_tail = lax.dynamic_index_in_dim(q_in, last, 0, keepdims=False)[BLK - TAIL :]
     q_halo = passed_along(q_tail)
-
-    pieces = [None, None]
-    for half in (1, 0):
-        (copies,) = call(
-            functools.partial(hidden_kernel, half),
-            [shape((nx, HALF, width))],
-            [smem(), smem()] + [vmem()] * 4,
-            (bpd, doc_lengths, q_in, q_halo if half == 0 else q_tail, short_filters, medium),
-            10**7,
-            scratch=[pltpu.VMEM((HALF + TAIL, width), F32)],
-            name=f"hidden{half}",
-        )
-        own = lax.all_to_all(copies, "x", split_axis=0, concat_axis=0, tiled=True)
-        own = own.reshape(nx * HALF, width)
-        other = lax.ppermute(own, "core", swap)
-        (partial,) = call(
-            project_kernel,
-            [shape((nz, nx * HALF, 128))],
-            [vmem()] * 3,
-            (own, other, weight),
-            2 * nx * HALF * 2 * width * nz * 128,
-            name=f"project{half}",
-        )
-        parts = lax.all_to_all(partial, "z", split_axis=0, concat_axis=0, tiled=True)
-        total = jnp.sum(parts.astype(F32), axis=0).astype(BF16)
-        mine = lax.all_to_all(
-            total.reshape(nx, HALF, 128), "x", split_axis=0, concat_axis=0, tiled=True
-        )
-        pieces[half] = mine
-    both = jnp.concatenate(pieces, axis=1)
-    return both.transpose(1, 0, 2).reshape(rows, nx * 128)
+    (copies,) = call(
+        hidden_kernel,
+        [shape((nx, rows, width))],
+        [smem(), smem()] + [vmem()] * 4,
+        (bpd, doc_lengths, q_in, q_halo, short_filters, medium),
+        10**7,
+        scratch=[pltpu.VMEM((rows + TAIL, width), F32)],
+        name="hidden",
+    )
+    own = lax.all_to_all(copies, "x", split_axis=0, concat_axis=0, tiled=True)
+    own = own.reshape(nx * rows, width)
+    other = lax.ppermute(own, "core", [(0, 1), (1, 0)])
+    partial = project(own, other, weight, nx, nz)
+    flat = partial.reshape(nz * nx, rows, partial.shape[3])
+    parts = lax.all_to_all(flat, ("z", "x"), split_axis=0, concat_axis=0, tiled=True)
+    return summed(parts.reshape(partial.shape))
 
 
 def solution(mesh):

time: 216 us -> 196 us (0.907)
  the two profiles are of different devices: /device:TPU:2 before, /device:TPU:34 now
where the time goes in v2:
time: 196 us
  blocking collectives  84.6 us (43%)
  starting transfers between devices  34 us (17%)
  Pallas kernels  28.8 us (15%)
  waiting for transfers between devices  27.8 us (14%)
  between operations  15.2 us (8%)
  local copies, waits for them, and re-layouts  3.62 us (2%)
    all_to_all x1, blocking collectives, on_device(): lax.all_to_all(flat, ('z', 'x'), split_axis=0, concat_axis=0, tiled=True)  63.5 us
    all_to_all x1, blocking collectives, on_device(): own = lax.all_to_all(copies, 'x', split_axis=0, concat_axis=0, tiled=True)  21.1 us
    pallas_call x5, Pallas kernels, call(): pl.pallas_call(body, out_shape=outs, in_specs=ins, out_specs=[vmem()] * l...  19.3 us
    all_to_all x1, waiting for transfers between devices, on_device(): kv_in = lax.all_to_all(kv_out, CTX, split_axis=0, concat_axis=0, tiled=True)  11.9 us
    all_to_all x1, starting transfers between devices, on_device(): kv_in = lax.all_to_all(kv_out, CTX, split_axis=0, concat_axis=0, tiled=True)  9.93 us
    all_to_all x1, starting transfers between devices, on_device(): q_in = lax.all_to_all(q_out, CTX, split_axis=0, concat_axis=0, tiled=True)  9.48 us
    ppermute x2, waiting for transfers between devices, passed_along(): return lax.ppermute(block, CTX, [(i, i + 1) for i in range(n - 1)])  7.82 us
    ppermute x2, starting transfers between devices, passed_along(): return lax.ppermute(block, CTX, [(i, i + 1) for i in range(n - 1)])  6.73 us
  transfers between devices with their start and end apart: 8, of which 6 were waited for; matrix products, arithmetic and copies ran while one was open for 1% of the time, Pallas kernels for 8%

profile of v2, /device:TPU:34, one launch (start us, length us, event | category | flops | bytes accessed | tf_op | source)
XLA Modules:
  0.0 195.5 jit_solution(4708937343159149047)
XLA Ops:
  6.5 0.0 copy-start.3
  6.5 3.6 %pack.1 = (bf16[32,2,16,512]{3,2,1,0:T(8,128)(2,1)}, bf16[32,16,512]{2,1,0:T(8,128)(2,1)}) custom-call(s32[16,32]{1,0:T(8,128)} %bitcast.15, bf16[3,512,512]{2,1,0:T(8,128)(2,1)} %bitcast.12), custom_call_target="tpu_custom_call" | custom-call | flops 1000000 | bytes 3147776 | tf_op jit(solution)/shard_map/pack/pallas_call | solution.py:31
  10.1 0.0 copy-start.5
  10.1 9.9 %all-to-all-start = ((bf16[32,2,16,512]{3,2,1,0:T(8,128)(2,1)}), bf16[32,2,16,512]{3,2,1,0:T(8,128)(2,1)S(1)}, u32[]{:S(2)}, u32[]{:S(2)}) async-start(bf16[32,2,16,512]{3,2,1,0:T(8,128)(2,1)} %get-tuple-element.14), calls=%async_computation | async-start | bytes 2097152 | tf_op jit(solution)/shard_map/all_to_all | solution.py:275
  20.1 0.0 all-gather.2.cloned.1.call-start
  20.1 0.0 copy-done.3
  20.2 3.4 %collective-permute-start.3 = (bf16[512,128]{1,0:T(8,128)(2,1)S(1)}, bf16[512,128]{1,0:T(8,128)(2,1)S(1)}, u32[]{:S(2)}, u32[]{:S(2)}) collective-permute-start(bf16[512,128]{1,0:T(8,128)(2,1)S(1)} %get-tuple-element.25), channel_id=1, source_target_pairs={{0,0},{1,16},{16,32},{17,48},{32,1},{33,17},{48,33},{49,49},{2,2},... | collective-permute-start | bytes 393224 | tf_op jit(solution)/shard_map/ppermute | solution.py:243
  23.5 2.5 %collective-permute-start.4 = (bf16[512,128]{1,0:T(8,128)(2,1)S(1)}, bf16[512,128]{1,0:T(8,128)(2,1)S(1)}, u32[]{:S(2)}, u32[]{:S(2)}) collective-permute-start(bf16[512,128]{1,0:T(8,128)(2,1)S(1)} %get-tuple-element.26), channel_id=1, source_target_pairs={{0,16},{1,0},{16,48},{17,32},{32,17},{33,1},{48,49},{49,33},{2,18}... | collective-permute-start | bytes 393224 | tf_op jit(solution)/shard_map/ppermute | solution.py:244
  26.1 3.7 %collective-permute-done.3 = bf16[512,128]{1,0:T(8,128)(2,1)S(1)} collective-permute-done((bf16[512,128]{1,0:T(8,128)(2,1)S(1)}, bf16[512,128]{1,0:T(8,128)(2,1)S(1)}, u32[]{:S(2)}, u32[]{:S(2)}) %collective-permute-start.3) | collective-permute-done | bytes 131104 | tf_op jit(solution)/shard_map/ppermute | solution.py:243
  29.8 1.8 collective-permute-done.4
  31.6 0.7 pad_maximum_fusion
  32.3 0.0 all-gather.2.cloned.1.call-update
  32.3 11.9 %all-to-all-done.kv = bf16[32,2,16,512]{3,2,1,0:T(8,128)(2,1)S(1)} async-done(((bf16[32,2,16,512]{3,2,1,0:T(8,128)(2,1)}), bf16[32,2,16,512]{3,2,1,0:T(8,128)(2,1)S(1)}, u32[]{:S(2)}, u32[]{:S(2)}) %all-to-all-start) | async-done | bytes 1048608 | tf_op jit(solution)/shard_map/all_to_all | solution.py:275
  44.2 0.0 copy-start
  44.2 9.5 %all-to-all-start.1 = ((bf16[32,16,512]{2,1,0:T(8,128)(2,1)}), bf16[32,16,512]{2,1,0:T(8,128)(2,1)S(1)}, u32[]{:S(2)}, u32[]{:S(2)}) async-start(bf16[32,16,512]{2,1,0:T(8,128)(2,1)} %get-tuple-element.20), calls=%async_computation.1 | async-start | bytes 1048576 | tf_op jit(solution)/shard_map/all_to_all | solution.py:276
  53.7 0.0 copy-done.5
  53.7 0.1 rev.3
  53.8 0.7 pad_convert_fusion.line
  54.5 4.9 %bands.1 = bf16[32,128,256]{2,1,0:T(8,128)(2,1)} custom-call(f32[32,256]{1,0:T(8,128)} %pad_convert_fusion.line), custom_call_target="tpu_custom_call" | custom-call | flops 100000000 | bytes 2129920 | tf_op jit(solution)/shard_map/bands/pallas_call | solution.py:31
  59.4 0.0 copy-done
  59.4 3.7 %gated.1 = (bf16[256,512]{1,0:T(8,128)(2,1)}, bf16[144,512]{1,0:T(8,128)(2,1)}, bf16[16,512]{1,0:T(8,128)(2,1)}) custom-call(s32[16,32]{1,0:T(8,128)} %bitcast.16, s32[8]{0:T(128)} %lengths.5, bf16[32,2,16,512]{3,2,1,0:T(8,128)(2,1)} %copy-done, bf16[3,7,512]{2,1,0:T(8,128)(2,1)} %taps.5), custom_call_target="tpu_custom_call" | custom-call | flops 10000000 | bytes 1498144 | tf_op jit(solution)/shard_map/gated/pallas_call | solution.py:31
  63.1 3.4 %collective-permute-start = (bf16[144,512]{1,0:T(8,128)(2,1)}, bf16[144,512]{1,0:T(8,128)(2,1)S(1)}, u32[]{:S(2)}, u32[]{:S(2)}) collective-permute-start(bf16[144,512]{1,0:T(8,128)(2,1)} %get-tuple-element.17), channel_id=1, source_target_pairs={{0,16},{16,32},{32,48},{48,64},{64,80},{80,96},{96,112},{112,128},... | collective-permute-start | bytes 442376 | tf_op jit(solution)/shard_map/ppermute | solution.py:230
  66.5 0.7 slice.20
  67.2 0.6 constant_dynamic-slice_fusion
  69.4 0.9 collective-permute-done.recv
  70.3 0.0 copy-start.7
  70.3 0.7 copy-done.7
  71.0 3.9 %medium.1 = f32[256,512]{1,0:T(8,128)} custom-call(s32[8]{0:T(128)} %lengths.5, bf16[256,512]{1,0:T(8,128)(2,1)} %get-tuple-element.16.z, bf16[144,512]{1,0:T(8,128)(2,1)} %copy-done.7, bf16[16,512]{1,0:T(8,128)(2,1)} %get-tuple-element.18.head, bf16[3,7,512]{2,1,0:T(8,128)(2,1)} %taps.5, bf16[32,128,256]{2,1,0:T(8,128)(2,1)} %bands.1, f32[1,512]{1,0:T(1,128)} %bitcast.20), custom_call_target="tpu_custom_call" | custom-call | flops 1000000000 | bytes 3071008 | tf_op jit(solution)/shard_map/medium/pallas_call | solution.py:31
  74.9 0.0 all-to-all-done.1.q
  74.9 0.0 copy-start.1
  75.0 3.4 %collective-permute-start.1 = (bf16[8,512]{1,0:T(8,128)(2,1)S(1)}, bf16[8,512]{1,0:T(8,128)(2,1)S(1)}, u32[]{:S(2)}, u32[]{:S(2)}) collective-permute-start(bf16[8,512]{1,0:T(8,128)(2,1)S(1)} %dynamic-slice_bitcast_fusion), channel_id=1, source_target_pairs={{0,16},{16,32},{32,48},{48,64},{64,80},{80,96},{96,112},{112,128},... | collective-permute-start | bytes 24584 | tf_op jit(solution)/shard_map/ppermute | solution.py:230
  78.3 6.9 %collective-permute-done.1.halo = bf16[8,512]{1,0:T(8,128)(2,1)S(1)} collective-permute-done((bf16[8,512]{1,0:T(8,128)(2,1)S(1)}, bf16[8,512]{1,0:T(8,128)(2,1)S(1)}, u32[]{:S(2)}, u32[]{:S(2)}) %collective-permute-start.1) | collective-permute-done | bytes 8224 | tf_op jit(solution)/shard_map/ppermute | solution.py:230
  85.2 0.0 copy-done.1
  85.3 0.0 copy-start.4
  85.3 0.6 copy-done.4
  85.9 3.2 %hidden.1 = bf16[4,256,512]{2,1,0:T(8,128)(2,1)} custom-call(s32[16,32]{1,0:T(8,128)} %bitcast.18, s32[8]{0:T(128)} %lengths.5, bf16[32,16,512]{2,1,0:T(8,128)(2,1)} %copy-done.1, bf16[8,512]{1,0:T(8,128)(2,1)} %copy-done.4, bf16[3,7,512]{2,1,0:T(8,128)(2,1)} %taps.5, f32[256,512]{1,0:T(8,128)} %medium.1), custom_call_target="tpu_custom_call" | custom-call | flops 10000000 | bytes 2128928 | tf_op jit(solution)/shard_map/hidden/pallas_call | solution.py:31
  89.1 21.1 %all_to_all.20 = bf16[4,256,512]{2,1,0:T(8,128)(2,1)S(1)} all-to-all(bf16[4,256,512]{2,1,0:T(8,128)(2,1)} %hidden.1), channel_id=1, replica_groups=mesh['y'=8,'x'=4,'z'=8,'core'=2] {'x'}, dimensions={0} | all-to-all | bytes 2097152 | tf_op jit(solution)/shard_map/all_to_all | solution.py:324
  110.2 0.0 copy-start.2
  110.2 1.9 collective-permute-start.2
  112.1 0.0 all-gather.2.cloned.1.call-done.weight
  112.1 2.6 %collective-permute-done.2.other = bf16[1024,512]{1,0:T(8,128)(2,1)S(1)} collective-permute-done((bf16[1024,512]{1,0:T(8,128)(2,1)S(1)}, bf16[1024,512]{1,0:T(8,128)(2,1)S(1)}, u32[]{:S(2)}, u32[]{:S(2)}) %collective-permute-start.2) | collective-permute-done | bytes 1048608 | tf_op jit(solution)/shard_map/ppermute | solution.py:326
  114.7 0.0 copy-done.2
  114.7 0.0 copy-start.6
  114.7 1.0 copy-done.6
  115.7 6.0 %project.1 = bf16[8,4,256,128]{3,2,1,0:T(8,128)(2,1)} custom-call(bf16[1024,512]{1,0:T(8,128)(2,1)} %bitcast.14, bf16[1024,512]{1,0:T(8,128)(2,1)} %copy-done.6, bf16[1024,1024]{1,0:T(8,128)(2,1)} %all-gather.2.cloned.1.call-done.weight), custom_call_target="tpu_custom_call" | custom-call | flops 2147483648 | bytes 8388608 | tf_op jit(solution)/shard_map/project/pallas_call | solution.py:185
  121.7 63.5 %all_to_all.21 = bf16[32,256,128]{2,1,0:T(8,128)(2,1)} all-to-all(bf16[32,256,128]{2,1,0:T(8,128)(2,1)} %bitcast.11), channel_id=1, replica_groups=mesh['y'=8,'x'=4,'z'=8,'core'=2] {'z','x'}, dimensions={0} | all-to-all | bytes 4194304 | tf_op jit(solution)/shard_map/all_to_all | solution.py:329
  185.1 3.5 %total.1 = bf16[256,512]{1,0:T(8,128)(2,1)} custom-call(bf16[8,4,256,128]{3,2,1,0:T(8,128)(2,1)} %bitcast.10), custom_call_target="tpu_custom_call" | custom-call | flops 1048576 | bytes 2097152 | tf_op jit(solution)/shard_map/total/pallas_call | solution.py:211
  (3 shorter events, 0.1 us)
Async XLA Ops:
  6.5 13.6 %copy-start.3 = (bf16[512,256]{1,0:T(8,128)(2,1)S(1)}, bf16[512,256]{1,0:T(8,128)(2,1)}, u32[]{:S(2)}) copy-start(bf16[512,256]{1,0:T(8,128)(2,1)} %param.11) | copy-start | bytes 786436
  10.1 43.6 %copy-start.5 = (bf16[128,32]{0,1:T(8,128)(2,1)S(1)}, bf16[128,32]{0,1:T(8,128)(2,1)}, u32[]{:S(2)}) copy-start(bf16[128,32]{0,1:T(8,128)(2,1)} %param.9) | copy-start | bytes 24580
  10.1 34.1 %all-to-all-start = ((bf16[32,2,16,512]{3,2,1,0:T(8,128)(2,1)}), bf16[32,2,16,512]{3,2,1,0:T(8,128)(2,1)S(1)}, u32[]{:S(2)}, u32[]{:S(2)}) async-start(bf16[32,2,16,512]{3,2,1,0:T(8,128)(2,1)} %get-tuple-element.14), calls=%async_computation | async-start | bytes 2097152 | tf_op jit(solution)/shard_map/all_to_all | solution.py:275
  20.1 92.0 %all-gather.2.cloned.1.call-start = ((), (), s32[]{:S(2)}) async-start(), calls=%async_computation.4 | async-start | bytes 2359296 | tf_op jit(solution)/shard_map/all_gather | solution.py:249
  20.2 9.6 %collective-permute-start.3 = (bf16[512,128]{1,0:T(8,128)(2,1)S(1)}, bf16[512,128]{1,0:T(8,128)(2,1)S(1)}, u32[]{:S(2)}, u32[]{:S(2)}) collective-permute-start(bf16[512,128]{1,0:T(8,128)(2,1)S(1)} %get-tuple-element.25), channel_id=1, source_target_pairs={{0,0},{1,16},{16,32},{17,48},{32,1},{33,17},{48,33},{49,49},{2,2},... | collective-permute-start | bytes 393224 | tf_op jit(solution)/shard_map/ppermute | solution.py:243
  23.5 8.0 %collective-permute-start.4 = (bf16[512,128]{1,0:T(8,128)(2,1)S(1)}, bf16[512,128]{1,0:T(8,128)(2,1)S(1)}, u32[]{:S(2)}, u32[]{:S(2)}) collective-permute-start(bf16[512,128]{1,0:T(8,128)(2,1)S(1)} %get-tuple-element.26), channel_id=1, source_target_pairs={{0,16},{1,0},{16,48},{17,32},{32,17},{33,1},{48,49},{49,33},{2,18}... | collective-permute-start | bytes 393224 | tf_op jit(solution)/shard_map/ppermute | solution.py:244
  44.2 15.2 %copy-start = (bf16[32,2,16,512]{3,2,1,0:T(8,128)(2,1)}, bf16[32,2,16,512]{3,2,1,0:T(8,128)(2,1)S(1)}, u32[]{:S(2)}) copy-start(bf16[32,2,16,512]{3,2,1,0:T(8,128)(2,1)S(1)} %all-to-all-done.kv) | copy-start | bytes 3145732
  44.2 30.7 %all-to-all-start.1 = ((bf16[32,16,512]{2,1,0:T(8,128)(2,1)}), bf16[32,16,512]{2,1,0:T(8,128)(2,1)S(1)}, u32[]{:S(2)}, u32[]{:S(2)}) async-start(bf16[32,16,512]{2,1,0:T(8,128)(2,1)} %get-tuple-element.20), calls=%async_computation.1 | async-start | bytes 1048576 | tf_op jit(solution)/shard_map/all_to_all | solution.py:276
  63.1 7.2 %collective-permute-start = (bf16[144,512]{1,0:T(8,128)(2,1)}, bf16[144,512]{1,0:T(8,128)(2,1)S(1)}, u32[]{:S(2)}, u32[]{:S(2)}) collective-permute-start(bf16[144,512]{1,0:T(8,128)(2,1)} %get-tuple-element.17), channel_id=1, source_target_pairs={{0,16},{16,32},{32,48},{48,64},{64,80},{80,96},{96,112},{112,128},... | collective-permute-start | bytes 442376 | tf_op jit(solution)/shard_map/ppermute | solution.py:230
  70.3 0.7 copy-start.7
  74.9 10.3 %copy-start.1 = (bf16[32,16,512]{2,1,0:T(8,128)(2,1)}, bf16[32,16,512]{2,1,0:T(8,128)(2,1)S(1)}, u32[]{:S(2)}) copy-start(bf16[32,16,512]{2,1,0:T(8,128)(2,1)S(1)} %all-to-all-done.1.q) | copy-start | bytes 1572868
  75.0 10.3 %collective-permute-start.1 = (bf16[8,512]{1,0:T(8,128)(2,1)S(1)}, bf16[8,512]{1,0:T(8,128)(2,1)S(1)}, u32[]{:S(2)}, u32[]{:S(2)}) collective-permute-start(bf16[8,512]{1,0:T(8,128)(2,1)S(1)} %dynamic-slice_bitcast_fusion), channel_id=1, source_target_pairs={{0,16},{16,32},{32,48},{48,64},{64,80},{80,96},{96,112},{112,128},... | collective-permute-start | bytes 24584 | tf_op jit(solution)/shard_map/ppermute | solution.py:230
  85.3 0.6 copy-start.4
  110.2 4.5 %copy-start.2 = (bf16[4,256,512]{2,1,0:T(8,128)(2,1)}, bf16[4,256,512]{2,1,0:T(8,128)(2,1)S(1)}, u32[]{:S(2)}) copy-start(bf16[4,256,512]{2,1,0:T(8,128)(2,1)S(1)} %all_to_all.20) | copy-start | bytes 3145732
  110.2 4.5 %collective-permute-start.2 = (bf16[1024,512]{1,0:T(8,128)(2,1)S(1)}, bf16[1024,512]{1,0:T(8,128)(2,1)S(1)}, u32[]{:S(2)}, u32[]{:S(2)}) collective-permute-start(bf16[1024,512]{1,0:T(8,128)(2,1)S(1)} %bitcast.13), channel_id=1, source_target_pairs={{0,1},{1,0},{2,3},{3,2},{4,5},{5,4},{6,7},{7,6},{8,9},{9,8},{10,11... | collective-permute-start | bytes 3145736 | tf_op jit(solution)/shard_map/ppermute | solution.py:326
  114.7 1.0 copy-start.6
Sparse Core Ops, SparseCore 0:
  32.4 58.6 all-gather.1

commit v3 on v2

--- a/solution.py
+++ b/solution.py
@@ -1,3 +1,5 @@
+import functools
+
 import jax
 import jax.numpy as jnp
 from jax import lax
@@ -5,6 +7,7 @@
 from jax.experimental.pallas import tpu as pltpu
 from jax.sharding import Mesh, PartitionSpec as P
 
+
 CTX = ("y", "x")
 SHAPE4 = (8, 4, 8, 2)
 BLK = 16
@@ -25,7 +28,7 @@
     return lax.axis_index("y") * lax.axis_size("x") + lax.axis_index("x")
 
 
-def call(body, outs, ins, args, flops, scratch=(), name=None):
+def call(body, outs, ins, args, flops, scratch=()):
     moved = sum(a.size * a.dtype.itemsize for a in args)
     moved += sum(o.size * o.dtype.itemsize for o in outs)
     return pl.pallas_call(
@@ -35,7 +38,6 @@
         out_specs=[vmem()] * len(outs),
         scratch_shapes=list(scratch),
         cost_estimate=pl.CostEstimate(flops=flops, bytes_accessed=moved, transcendentals=0),
-        name=name,
     )(*args)
 
 
@@ -59,20 +61,48 @@
     return total
 
 
-def pack_kernel(bpd, src, kv, q):
-    me = stretch_id()
-
-    def one(c, slot):
-        mine = jnp.int32(0)
-        for k in range(bpd.shape[0]):
-            mine = mine | (bpd[k, c] == me).astype(jnp.int32)
-        rows = pl.ds(pl.multiple_of(slot * BLK, BLK), BLK)
+def pack_kernel(bpd, src, kv, q, slots):
+    @pl.when(pl.program_id(0) == 0)
+    def _():
+        me = stretch_id()
+
+        def count(c, slot):
+            mine = bpd[0, c] == me
+            for k in range(1, bpd.shape[0]):
+                mine = mine | (bpd[k, c] == me)
+            slots[c] = slot
+            return slot + mine.astype(jnp.int32)
+
+        lax.fori_loop(0, bpd.shape[1], count, jnp.int32(0))
+
+    def one(c, carry):
+        rows = pl.ds(pl.multiple_of(slots[c] * BLK, BLK), BLK)
         kv[c, 0] = src[1, rows, :]
         kv[c, 1] = src[2, rows, :]
         q[c] = src[0, rows, :]
-        return slot + mine
-
-    lax.fori_loop(0, bpd.shape[1], one, jnp.int32(0))
+        return carry
+
+    lax.fori_loop(0, bpd.shape[1], one, 0, unroll=4)
+
+
+def packed_blocks(bpd, src, stretches):
+    width = src.shape[2]
+    lane = width // 4
+    return pl.pallas_call(
+        pack_kernel,
+        grid=(width // lane,),
+        in_specs=[smem(), pl.BlockSpec((3, src.shape[1], lane), lambda i: (0, 0, i))],
+        out_specs=[
+            pl.BlockSpec((stretches, 2, BLK, lane), lambda i: (0, 0, 0, i)),
+            pl.BlockSpec((stretches, BLK, lane), lambda i: (0, 0, i)),
+        ],
+        out_shape=[shape((stretches, 2, BLK, width)), shape((stretches, BLK, width))],
+        scratch_shapes=[pltpu.SMEM((stretches,), jnp.int32)],
+        cost_estimate=pl.CostEstimate(
+            flops=10**6, bytes_accessed=4 * src.size, transcendentals=0
+        ),
+        name="pack",
+    )(bpd, src)
 
 
 def toeplitz_kernel(line, out):
@@ -165,60 +195,52 @@
     lax.fori_loop(0, rows // step, chunk, 0)
 
 
-def project_kernel(own, other, weight, out):
+def project_kernel(offsets, own, other, *refs):
+    weights, out = refs[:-1], refs[-1]
     k = own.shape[1]
-    lane = out.shape[2]
-    for pair in range(out.shape[0] // 2):
-        cols = slice(pair * 2 * lane, (pair + 1) * 2 * lane)
-        got = jnp.dot(own[...], weight[0:k, cols], preferred_element_type=F32)
-        got = got + jnp.dot(other[...], weight[k:, cols], preferred_element_type=F32)
+    lane = out.shape[3]
+    n = out.shape[0]
+    y = lax.axis_index("y")
+    for pair in range(0, n, 2):
+        wide = jnp.concatenate([weights[pair][...], weights[pair + 1][...]], axis=1)
+        got = jnp.dot(own[...], wide[:k], preferred_element_type=F32)
+        got = got + jnp.dot(other[...], wide[k:], preferred_element_type=F32)
         got = got.astype(BF16)
-        out[2 * pair] = got[:, :lane]
-        out[2 * pair + 1] = got[:, lane:]
-
-
-def project(own, other, weight, nx, nz):
+        for i in range(2):
+            at = lax.rem(y - offsets[pair + i] + n, n)
+            for s in range(out.shape[1]):
+                piece = got[s * out.shape[2] : (s + 1) * out.shape[2]]
+                out[at, s] = piece[:, i * lane : (i + 1) * lane]
+
+
+def project(own, other, weights, nx):
+    offsets = tuple(w[0] for w in weights)
+    blocks = [w[1] for w in weights]
+    n = len(blocks)
     rows = own.shape[0] // nx
+    two = 2
     k = own.shape[1]
-    cols = weight.shape[1]
-    lane = cols // nz
+    lane = blocks[0].shape[1]
     return pl.pallas_call(
-        project_kernel,
-        grid=(nx,),
+        functools.partial(project_kernel, offsets),
+        grid=(nx // two,),
         in_specs=[
-            pl.BlockSpec((rows, k), lambda i: (i, 0)),
-            pl.BlockSpec((rows, k), lambda i: (i, 0)),
-            pl.BlockSpec((2 * k, cols), lambda i: (0, 0)),
-        ],
-        out_specs=pl.BlockSpec((nz, None, rows, lane), lambda i: (0, i, 0, 0)),
-        out_shape=shape((nz, nx, rows, lane)),
+            pl.BlockSpec((two * rows, k), lambda i: (i, 0)),
+            pl.BlockSpec((two * rows, k), lambda i: (i, 0)),
+        ]
+        + [pl.BlockSpec((2 * k, lane), lambda i: (0, 0)) for _ in blocks],
+        out_specs=pl.BlockSpec((n, two, rows, lane), lambda i: (0, i, 0, 0)),
+        out_shape=shape((n, nx, rows, lane)),
         cost_estimate=pl.CostEstimate(
-            flops=4 * nx * rows * k * cols, bytes_accessed=8 << 20, transcendentals=0
+            flops=4 * nx * rows * k * n * lane, bytes_accessed=8 << 20, transcendentals=0
         ),
         name="project",
-    )(own, other, weight)
-
-
-def sum_kernel(parts, out):
-    total = parts[0].astype(F32)
-    for i in range(1, parts.shape[0]):
-        total = total + parts[i].astype(F32)
-    out[...] = total.astype(BF16)
+    )(own, other, *blocks)
 
 
 def summed(parts):
-    nz, nx, rows, lane = parts.shape
-    return pl.pallas_call(
-        sum_kernel,
-        grid=(nx,),
-        in_specs=[pl.BlockSpec((nz, None, rows, lane), lambda i: (0, i, 0, 0))],
-        out_specs=pl.BlockSpec((rows, lane), lambda i: (0, i)),
-        out_shape=shape((rows, nx * lane)),
-        cost_estimate=pl.CostEstimate(
-            flops=parts.size, bytes_accessed=2 * parts.size, transcendentals=0
-        ),
-        name="total",
-    )(parts)
+    columns = [jnp.sum(parts[:, x].astype(F32), axis=0) for x in range(parts.shape[1])]
+    return jnp.concatenate(columns, axis=1).astype(BF16)
 
 
 def shape(dims, dtype=BF16):
@@ -245,11 +267,15 @@
     straight = lax.axis_index("x") % 2 == core
     own = jnp.where(straight, a, b)
     other = jnp.where(straight, b, a)
-    both = jnp.concatenate([own, other], axis=0)
-    return lax.all_gather(both, "y", axis=1, tiled=True)
-
-
-def on_device(
+    return jnp.concatenate([own, other], axis=0)
+
+
+def around(block, distance):
+    n = lax.axis_size("y")
+    return lax.ppermute(block, "y", [(i, (i + distance) % n) for i in range(n)])
+
+
+def operator(
     source_rows,
     short_filters,
     medium_filters,
@@ -264,30 +290,19 @@
     rows = block_packing_device.shape[1] * BLK
     bpd = block_packing_device.T
 
-    kv_out, q_out = call(
-        pack_kernel,
-        [shape((stretches, 2, BLK, width)), shape((stretches, BLK, width))],
-        [smem(), vmem()],
-        (bpd, source_rows.transpose(1, 0, 2)),
-        10**6,
-        name="pack",
-    )
+    kv_out, q_out = packed_blocks(bpd, source_rows.transpose(1, 0, 2), stretches)
     kv_in = lax.all_to_all(kv_out, CTX, split_axis=0, concat_axis=0, tiled=True)
     q_in = lax.all_to_all(q_out, CTX, split_axis=0, concat_axis=0, tiled=True)
-
-    weight = weight_columns(out_weight)
+    block = weight_columns(out_weight)
 
     groups = medium_filters.shape[1]
     line = jnp.pad(medium_filters[::-1].T.astype(F32), ((0, 0), (1, HALF - 1)))
-    (bands,) = call(
-        toeplitz_kernel,
-        [shape((groups, HALF, 2 * HALF))],
-        [vmem()],
-        (line,),
-        10**8,
-        name="bands",
-    )
-    bands, kv_in = lax.optimization_barrier((bands, kv_in))
+    (bands,) = call(toeplitz_kernel, [shape((groups, HALF, 2 * HALF))], [vmem()], (line,), 10**8)
+    weights = [(0, block)]
+    up = down = block
+    for d in (1, 2):
+        up, down = around(up, 1), around(down, -1)
+        weights += [(d, up), (-d, down)]
 
     z, send, head = call(
         z_kernel,
@@ -296,7 +311,6 @@
         (bpd, doc_lengths, kv_in, short_filters),
         10**7,
         scratch=[pltpu.VMEM((2, rows + TAIL, width), F32)],
-        name="gated",
     )
     recv = passed_along(send)
     (medium,) = call(
@@ -306,10 +320,12 @@
         (doc_lengths, z, recv, head, short_filters, bands, skip_gain.reshape(1, width)),
         10**9,
         scratch=[pltpu.VMEM((rows + HALF, width), BF16)],
-        name="medium",
     )
     medium, q_in = lax.optimization_barrier((medium, q_in))
-    last = lax.dynamic_index_in_dim(bpd[-1], stretch_id(), 0, keepdims=False)
+    up, down = around(up, 1), around(down, -1)
+    weights += [(3, up), (-3, down), (4, around(up, 1))]
+    mine = jnp.arange(stretches, dtype=jnp.int32) == stretch_id()
+    last = jnp.sum(jnp.where(mine, bpd[-1], 0))
     q_tail = lax.dynamic_index_in_dim(q_in, last, 0, keepdims=False)[BLK - TAIL :]
     q_halo = passed_along(q_tail)
     (copies,) = call(
@@ -319,12 +335,11 @@
         (bpd, doc_lengths, q_in, q_halo, short_filters, medium),
         10**7,
         scratch=[pltpu.VMEM((rows + TAIL, width), F32)],
-        name="hidden",
     )
     own = lax.all_to_all(copies, "x", split_axis=0, concat_axis=0, tiled=True)
     own = own.reshape(nx * rows, width)
     other = lax.ppermute(own, "core", [(0, 1), (1, 0)])
-    partial = project(own, other, weight, nx, nz)
+    partial = project(own, other, weights, nx)
     flat = partial.reshape(nz * nx, rows, partial.shape[3])
     parts = lax.all_to_all(flat, ("z", "x"), split_axis=0, concat_axis=0, tiled=True)
     return summed(parts.reshape(partial.shape))
@@ -334,7 +349,7 @@
     ctx, mp = CTX, ("z", "core")
     mesh4 = Mesh(mesh.devices.reshape(SHAPE4), ctx + mp)
     return jax.shard_map(
-        on_device,
+        operator,
         mesh=mesh4,
         in_specs=(
             P(ctx, None, mp),

time: 196 us -> 213 us (1.087)
  starting transfers between devices: 34 us -> 55.9 us
  between operations: 15.2 us -> 2.37 us
  blocking collectives: 84.6 us -> 94.5 us
  Pallas kernels: 28.8 us -> 25.9 us
    ppermute x1 -> x8, starting transfers between devices: 1.91 us -> 26.6 us  [the longest x7 23.8 us: around(): return lax.ppermute(block, 'y', [(i, (i + distance) % n) for i in range(n)])]
    ppermute x1 -> x8, waiting for transfers between devices: 2.6 us -> 17.3 us  [the longest x7 17.3 us: around(): return lax.ppermute(block, 'y', [(i, (i + distance) % n) for i in range(n)])]
    all_to_all x2, waiting for transfers between devices: 11.9 us -> 0.01 us  [the longest x1 0.01 us: operator(): q_in = lax.all_to_all(q_out, CTX, split_axis=0, concat_axis=0, tiled=True)]
    all_to_all x2, blocking collectives: 84.6 us -> 94.5 us  [the longest x1 60.3 us: operator(): lax.all_to_all(flat, ('z', 'x'), split_axis=0, concat_axis=0, tiled=True)]
    ppermute x2, waiting for transfers between devices: 7.82 us -> 2.46 us  [passed_along(): return lax.ppermute(block, CTX, [(i, i + 1) for i in range(n - 1)])]
    pallas_call x5 -> x4, Pallas kernels: 19.3 us -> 15.8 us  [call(): pl.pallas_call(body, out_shape=outs, in_specs=ins, out_specs=[vmem()] * l...]
    all_to_all x2, starting transfers between devices: 19.4 us -> 16.8 us  [the longest x1 9.48 us: operator(): q_in = lax.all_to_all(q_out, CTX, split_axis=0, concat_axis=0, tiled=True)]
    ppermute x1, waiting for transfers between devices: 3.7 us -> 6.25 us  [weight_columns(): a = lax.ppermute(same, ('x', 'core'), route(lambda i: i))]
  transfers between devices with their start and end apart: 8 -> 14, of which waited for: 6 -> 9; matrix products, arithmetic and copies ran while one was open for 1% -> 1% of each run, Pallas kernels for 8% -> 6%
where the time goes in v3:
time: 213 us; the launch traced here: 212 us
  blocking collectives  94.5 us (44%)
  starting transfers between devices  55.9 us (26%)
  waiting for transfers between devices  26.7 us (13%)
  Pallas kernels  25.9 us (12%)
  other arithmetic  3.2 us (2%)
  local copies, waits for them, and re-layouts  3.05 us (1%)
  between operations  2.37 us (1%)
    all_to_all x1, blocking collectives, operator(): lax.all_to_all(flat, ('z', 'x'), split_axis=0, concat_axis=0, tiled=True)  60.3 us
    all_to_all x1, blocking collectives, operator(): kv_in = lax.all_to_all(kv_out, CTX, split_axis=0, concat_axis=0, tiled=True)  34.2 us
    ppermute x7, starting transfers between devices, around(): return lax.ppermute(block, 'y', [(i, (i + distance) % n) for i in range(n)])  23.8 us
    ppermute x7, waiting for transfers between devices, around(): return lax.ppermute(block, 'y', [(i, (i + distance) % n) for i in range(n)])  17.3 us
    pallas_call x4, Pallas kernels, call(): pl.pallas_call(body, out_shape=outs, in_specs=ins, out_specs=[vmem()] * l...  15.8 us
    all_to_all x1, starting transfers between devices, operator(): q_in = lax.all_to_all(q_out, CTX, split_axis=0, concat_axis=0, tiled=True)  9.48 us
    all_to_all x1, starting transfers between devices, operator(): own = lax.all_to_all(copies, 'x', split_axis=0, concat_axis=0, tiled=True)  7.36 us
    ppermute x2, starting transfers between devices, passed_along(): return lax.ppermute(block, CTX, [(i, i + 1) for i in range(n - 1)])  6.57 us
  transfers between devices with their start and end apart: 14, of which 9 were waited for; matrix products, arithmetic and copies ran while one was open for 1% of the time, Pallas kernels for 6%

profile of v3, /device:TPU:34, one launch (start us, length us, event | category | flops | bytes accessed | tf_op | source)
XLA Modules:
  0.0 211.7 jit_solution(8708148903472911947)
XLA Ops:
  0.0 4.7 %pack.1 = (bf16[32,2,16,512]{3,2,1,0:T(8,128)(2,1)}, bf16[32,16,512]{2,1,0:T(8,128)(2,1)}) custom-call(s32[16,32]{1,0:T(8,128)} %bitcast.18, bf16[3,512,512]{2,1,0:T(8,128)(2,1)} %bitcast.15), custom_call_target="tpu_custom_call" | custom-call | flops 1000000 | bytes 3145728 | tf_op jit(solution)/shard_map/pack/pallas_call | solution.py:91
  4.7 34.2 %all_to_all.20.kv = bf16[32,2,16,512]{3,2,1,0:T(8,128)(2,1)} all-to-all(bf16[32,2,16,512]{3,2,1,0:T(8,128)(2,1)} %get-tuple-element.12), channel_id=1, replica_groups=mesh['y'=8,'x'=4,'z'=8,'core'=2] {'y','x'}, dimensions={0} | all-to-all | bytes 2097152 | tf_op jit(solution)/shard_map/all_to_all | solution.py:294
  38.9 9.5 %all-to-all-start.1 = ((bf16[32,16,512]{2,1,0:T(8,128)(2,1)}), bf16[32,16,512]{2,1,0:T(8,128)(2,1)S(1)}, u32[]{:S(2)}, u32[]{:S(2)}) async-start(bf16[32,16,512]{2,1,0:T(8,128)(2,1)} %get-tuple-element.16), calls=%async_computation.1 | async-start | bytes 1048576 | tf_op jit(solution)/shard_map/all_to_all | solution.py:295
  48.4 3.7 %shard_map.73 = (bf16[256,512]{1,0:T(8,128)(2,1)}, bf16[144,512]{1,0:T(8,128)(2,1)}, bf16[16,512]{1,0:T(8,128)(2,1)}) custom-call(s32[16,32]{1,0:T(8,128)} %bitcast.19, s32[8]{0:T(128)} %lengths.5, bf16[32,2,16,512]{3,2,1,0:T(8,128)(2,1)} %all_to_all.20.kv, bf16[3,7,512]{2,1,0:T(8,128)(2,1)} %taps.5), custom_call_target="tpu_custom_call" | custom-call | flops 10000000 | bytes 1498144 | tf_op jit(solution)/shard_map/pallas_call | solution.py:34
  52.1 3.4 %collective-permute-start = (bf16[144,512]{1,0:T(8,128)(2,1)}, bf16[144,512]{1,0:T(8,128)(2,1)S(1)}, u32[]{:S(2)}, u32[]{:S(2)}) collective-permute-start(bf16[144,512]{1,0:T(8,128)(2,1)} %get-tuple-element.14), channel_id=1, source_target_pairs={{0,16},{16,32},{32,48},{48,64},{64,80},{80,96},{96,112},{112,128},... | collective-permute-start | bytes 442376 | tf_op jit(solution)/shard_map/ppermute | solution.py:252
  55.5 1.4 fusion
  58.3 0.1 rev.3
  59.0 0.7 pad_convert_fusion.line
  59.7 4.9 %shard_map.74.bands = bf16[32,128,256]{2,1,0:T(8,128)(2,1)} custom-call(f32[32,256]{1,0:T(8,128)} %pad_convert_fusion.line), custom_call_target="tpu_custom_call" | custom-call | flops 100000000 | bytes 2129920 | tf_op jit(solution)/shard_map/pallas_call | solution.py:34
  64.7 0.0 collective-permute-done.recv
  64.7 0.7 copy-done.14
  65.3 3.9 %shard_map.75.medium = f32[256,512]{1,0:T(8,128)} custom-call(s32[8]{0:T(128)} %lengths.5, bf16[256,512]{1,0:T(8,128)(2,1)} %get-tuple-element.13.z, bf16[144,512]{1,0:T(8,128)(2,1)} %copy-done.14, bf16[16,512]{1,0:T(8,128)(2,1)} %get-tuple-element.15.head, bf16[3,7,512]{2,1,0:T(8,128)(2,1)} %taps.5, bf16[32,128,256]{2,1,0:T(8,128)(2,1)} %shard_map.74.bands, ...), custom_call_target="tpu_custom_call" | custom-call | flops 1000000000 | bytes 3071008 | tf_op jit(solution)/shard_map/pallas_call | solution.py:34
  69.3 0.0 all-to-all-done.1.q
  69.3 0.0 copy-start.2
  69.3 3.2 %collective-permute-start.1 = (bf16[8,512]{1,0:T(8,128)(2,1)S(1)}, bf16[8,512]{1,0:T(8,128)(2,1)S(1)}, u32[]{:S(2)}, u32[]{:S(2)}) collective-permute-start(bf16[8,512]{1,0:T(8,128)(2,1)S(1)} %dynamic-slice_bitcast_fusion), channel_id=1, source_target_pairs={{0,16},{16,32},{32,48},{48,64},{64,80},{80,96},{96,112},{112,128},... | collective-permute-start | bytes 24584 | tf_op jit(solution)/shard_map/ppermute | solution.py:252
  72.5 2.5 %collective-permute-done.1.halo = bf16[8,512]{1,0:T(8,128)(2,1)S(1)} collective-permute-done((bf16[8,512]{1,0:T(8,128)(2,1)S(1)}, bf16[8,512]{1,0:T(8,128)(2,1)S(1)}, u32[]{:S(2)}, u32[]{:S(2)}) %collective-permute-start.1) | collective-permute-done | bytes 8224 | tf_op jit(solution)/shard_map/ppermute | solution.py:252
  75.0 0.6 copy-done.4
  75.6 3.2 %shard_map.76 = bf16[4,256,512]{2,1,0:T(8,128)(2,1)} custom-call(s32[16,32]{1,0:T(8,128)} %bitcast.21, s32[8]{0:T(128)} %lengths.5, bf16[32,16,512]{2,1,0:T(8,128)(2,1)} %copy-done, bf16[8,512]{1,0:T(8,128)(2,1)} %copy-done.4, bf16[3,7,512]{2,1,0:T(8,128)(2,1)} %taps.5, f32[256,512]{1,0:T(8,128)} %shard_map.75.medium), custom_call_target="tpu_custom_call" | custom-call | flops 10000000 | bytes 2128928 | tf_op jit(solution)/shard_map/pallas_call | solution.py:34
  78.8 7.4 %all-to-all-start.2 = ((bf16[4,256,512]{2,1,0:T(8,128)(2,1)}), bf16[4,256,512]{2,1,0:T(8,128)(2,1)S(1)}, u32[]{:S(2)}, u32[]{:S(2)}) async-start(bf16[4,256,512]{2,1,0:T(8,128)(2,1)} %shard_map.76), calls=%async_computation.2 | async-start | bytes 2097152 | tf_op jit(solution)/shard_map/all_to_all | solution.py:339
  86.2 3.4 %collective-permute-start.3 = (bf16[512,128]{1,0:T(8,128)(2,1)S(1)}, bf16[512,128]{1,0:T(8,128)(2,1)S(1)}, u32[]{:S(2)}, u32[]{:S(2)}) collective-permute-start(bf16[512,128]{1,0:T(8,128)(2,1)S(1)} %get-tuple-element.25), channel_id=1, source_target_pairs={{0,0},{1,16},{16,32},{17,48},{32,1},{33,17},{48,33},{49,49},{2,2},... | collective-permute-start | bytes 393224 | tf_op jit(solution)/shard_map/ppermute | solution.py:265
  89.5 2.5 %collective-permute-start.4 = (bf16[512,128]{1,0:T(8,128)(2,1)S(1)}, bf16[512,128]{1,0:T(8,128)(2,1)S(1)}, u32[]{:S(2)}, u32[]{:S(2)}) collective-permute-start(bf16[512,128]{1,0:T(8,128)(2,1)S(1)} %get-tuple-element.26), channel_id=1, source_target_pairs={{0,16},{1,0},{16,48},{17,32},{32,17},{33,1},{48,49},{49,33},{2,18}... | collective-permute-start | bytes 393224 | tf_op jit(solution)/shard_map/ppermute | solution.py:266
  92.1 6.2 %collective-permute-done.3 = bf16[512,128]{1,0:T(8,128)(2,1)S(1)} collective-permute-done((bf16[512,128]{1,0:T(8,128)(2,1)S(1)}, bf16[512,128]{1,0:T(8,128)(2,1)S(1)}, u32[]{:S(2)}, u32[]{:S(2)}) %collective-permute-start.3) | collective-permute-done | bytes 131104 | tf_op jit(solution)/shard_map/ppermute | solution.py:265
  98.3 0.7 collective-permute-done.4
  99.1 0.0 copy-start.3
  99.1 2.0 collective-permute-start.5
  101.2 0.0 all-to-all-done.2
  101.2 2.8 %collective-permute-start.2 = (bf16[1024,512]{1,0:T(8,128)(2,1)S(1)}, bf16[1024,512]{1,0:T(8,128)(2,1)S(1)}, u32[]{:S(2)}, u32[]{:S(2)}) collective-permute-start(bf16[1024,512]{1,0:T(8,128)(2,1)S(1)} %bitcast.16), channel_id=1, source_target_pairs={{0,1},{1,0},{2,3},{3,2},{4,5},{5,4},{6,7},{7,6},{8,9},{9,8},{10,11... | collective-permute-start | bytes 3145736 | tf_op jit(solution)/shard_map/ppermute | solution.py:341
  104.0 4.9 %collective-permute-start.6 = (bf16[1024,128]{1,0:T(8,128)(2,1)S(1)}, bf16[1024,128]{1,0:T(8,128)(2,1)S(1)}, u32[]{:S(2)}, u32[]{:S(2)}) collective-permute-start(bf16[1024,128]{1,0:T(8,128)(2,1)S(1)} %pad_maximum_fusion.refs_0_), channel_id=1, source_target_pairs={{0,448},{64,0},{128,64},{192,128},{256,192},{320,256},{384,320},{4... | collective-permute-start | bytes 786440 | tf_op jit(solution)/shard_map/ppermute | solution.py:275
  108.9 2.5 %collective-permute-done.5.refs_1_ = bf16[1024,128]{1,0:T(8,128)(2,1)S(1)} collective-permute-done((bf16[1024,128]{1,0:T(8,128)(2,1)S(1)}, bf16[1024,128]{1,0:T(8,128)(2,1)S(1)}, u32[]{:S(2)}, u32[]{:S(2)}) %collective-permute-start.5) | collective-permute-done | bytes 262176 | tf_op jit(solution)/shard_map/ppermute | solution.py:275
  111.4 1.9 collective-permute-start.7
  113.3 1.3 collective-permute-done.6.refs_2_
  114.6 5.6 %collective-permute-start.8 = (bf16[1024,128]{1,0:T(8,128)(2,1)S(1)}, bf16[1024,128]{1,0:T(8,128)(2,1)S(1)}, u32[]{:S(2)}, u32[]{:S(2)}) collective-permute-start(bf16[1024,128]{1,0:T(8,128)(2,1)S(1)} %collective-permute-done.6.refs_2_), channel_id=1, source_target_pairs={{0,448},{64,0},{128,64},{192,128},{256,192},{320,256},{384,320},{4... | collective-permute-start | bytes 786440 | tf_op jit(solution)/shard_map/ppermute | solution.py:275
  120.2 2.7 %collective-permute-done.7.refs_3_ = bf16[1024,128]{1,0:T(8,128)(2,1)S(1)} collective-permute-done((bf16[1024,128]{1,0:T(8,128)(2,1)S(1)}, bf16[1024,128]{1,0:T(8,128)(2,1)S(1)}, u32[]{:S(2)}, u32[]{:S(2)}) %collective-permute-start.7) | collective-permute-done | bytes 262176 | tf_op jit(solution)/shard_map/ppermute | solution.py:275
  122.8 1.9 collective-permute-start.9
  124.8 0.3 collective-permute-done.8.refs_4_
  125.0 5.6 %collective-permute-start.10 = (bf16[1024,128]{1,0:T(8,128)(2,1)S(1)}, bf16[1024,128]{1,0:T(8,128)(2,1)S(1)}, u32[]{:S(2)}, u32[]{:S(2)}) collective-permute-start(bf16[1024,128]{1,0:T(8,128)(2,1)S(1)} %collective-permute-done.8.refs_4_), channel_id=1, source_target_pairs={{0,448},{64,0},{128,64},{192,128},{256,192},{320,256},{384,320},{4... | collective-permute-start | bytes 786440 | tf_op jit(solution)/shard_map/ppermute | solution.py:275
  130.6 2.8 %collective-permute-done.9.refs_5_ = bf16[1024,128]{1,0:T(8,128)(2,1)S(1)} collective-permute-done((bf16[1024,128]{1,0:T(8,128)(2,1)S(1)}, bf16[1024,128]{1,0:T(8,128)(2,1)S(1)}, u32[]{:S(2)}, u32[]{:S(2)}) %collective-permute-start.9) | collective-permute-done | bytes 262176 | tf_op jit(solution)/shard_map/ppermute | solution.py:275
  133.4 1.9 collective-permute-start.11
  135.3 0.0 collective-permute-done.10.refs_6_
  135.3 7.8 %collective-permute-done.11.refs_7_ = bf16[1024,128]{1,0:T(8,128)(2,1)S(1)} collective-permute-done((bf16[1024,128]{1,0:T(8,128)(2,1)S(1)}, bf16[1024,128]{1,0:T(8,128)(2,1)S(1)}, u32[]{:S(2)}, u32[]{:S(2)}) %collective-permute-start.11) | collective-permute-done | bytes 262176 | tf_op jit(solution)/shard_map/ppermute | solution.py:275
  143.1 0.0 copy-done.12
  143.1 0.7 copy-done.13
  143.8 0.0 collective-permute-done.2.other
  143.9 1.0 copy-done.6
  144.8 5.5 %project.1 = bf16[8,4,256,128]{3,2,1,0:T(8,128)(2,1)} custom-call(bf16[1024,512]{1,0:T(8,128)(2,1)} %bitcast.17, bf16[1024,512]{1,0:T(8,128)(2,1)} %copy-done.6, bf16[1024,128]{1,0:T(8,128)(2,1)} %copy-done.3, bf16[1024,128]{1,0:T(8,128)(2,1)} %copy-done.7, bf16[1024,128]{1,0:T(8,128)(2,1)} %copy-done.8, bf16[1024,128]{1,0:T(8,128)(2,1)} %copy-done.9, ...), custom_call_target="tpu_custom_call" | custom-call | flops 2147483648 | bytes 8388608 | tf_op jit(solution)/shard_map/project/pallas_call | solution.py:224
  150.3 60.3 %all_to_all.21 = bf16[32,256,128]{2,1,0:T(8,128)(2,1)S(1)} all-to-all(bf16[32,256,128]{2,1,0:T(8,128)(2,1)} %bitcast.14), channel_id=1, replica_groups=mesh['y'=8,'x'=4,'z'=8,'core'=2] {'z','x'}, dimensions={0} | all-to-all | bytes 4194304 | tf_op jit(solution)/shard_map/all_to_all | solution.py:344
  210.6 0.3 slice_reduce_fusion.3
  210.9 0.7 pad_maximum_fusion.1
  (27 shorter events, 0.1 us)
Async XLA Ops:
  4.7 53.6 %copy-start.5 = (bf16[128,32]{0,1:T(8,128)(2,1)S(1)}, bf16[128,32]{0,1:T(8,128)(2,1)}, u32[]{:S(2)}) copy-start(bf16[128,32]{0,1:T(8,128)(2,1)} %param.9) | copy-start | bytes 24580
  38.9 30.4 %all-to-all-start.1 = ((bf16[32,16,512]{2,1,0:T(8,128)(2,1)}), bf16[32,16,512]{2,1,0:T(8,128)(2,1)S(1)}, u32[]{:S(2)}, u32[]{:S(2)}) async-start(bf16[32,16,512]{2,1,0:T(8,128)(2,1)} %get-tuple-element.16), calls=%async_computation.1 | async-start | bytes 1048576 | tf_op jit(solution)/shard_map/all_to_all | solution.py:295
  52.1 12.6 %collective-permute-start = (bf16[144,512]{1,0:T(8,128)(2,1)}, bf16[144,512]{1,0:T(8,128)(2,1)S(1)}, u32[]{:S(2)}, u32[]{:S(2)}) collective-permute-start(bf16[144,512]{1,0:T(8,128)(2,1)} %get-tuple-element.14), channel_id=1, source_target_pairs={{0,16},{16,32},{32,48},{48,64},{64,80},{80,96},{96,112},{112,128},... | collective-permute-start | bytes 442376 | tf_op jit(solution)/shard_map/ppermute | solution.py:252
  64.7 0.7 copy-start.14
  69.3 5.7 %copy-start = (bf16[32,16,512]{2,1,0:T(8,128)(2,1)}, bf16[32,16,512]{2,1,0:T(8,128)(2,1)S(1)}, u32[]{:S(2)}) copy-start(bf16[32,16,512]{2,1,0:T(8,128)(2,1)S(1)} %all-to-all-done.1.q) | copy-start | bytes 1572868
  69.3 16.9 %copy-start.2 = (bf16[512,256]{1,0:T(8,128)(2,1)S(1)}, bf16[512,256]{1,0:T(8,128)(2,1)}, u32[]{:S(2)}) copy-start(bf16[512,256]{1,0:T(8,128)(2,1)} %param.11) | copy-start | bytes 786436
  69.3 5.7 %collective-permute-start.1 = (bf16[8,512]{1,0:T(8,128)(2,1)S(1)}, bf16[8,512]{1,0:T(8,128)(2,1)S(1)}, u32[]{:S(2)}, u32[]{:S(2)}) collective-permute-start(bf16[8,512]{1,0:T(8,128)(2,1)S(1)} %dynamic-slice_bitcast_fusion), channel_id=1, source_target_pairs={{0,16},{16,32},{32,48},{48,64},{64,80},{80,96},{96,112},{112,128},... | collective-permute-start | bytes 24584 | tf_op jit(solution)/shard_map/ppermute | solution.py:252
  75.0 0.6 copy-start.4
  78.8 22.4 %all-to-all-start.2 = ((bf16[4,256,512]{2,1,0:T(8,128)(2,1)}), bf16[4,256,512]{2,1,0:T(8,128)(2,1)S(1)}, u32[]{:S(2)}, u32[]{:S(2)}) async-start(bf16[4,256,512]{2,1,0:T(8,128)(2,1)} %shard_map.76), calls=%async_computation.2 | async-start | bytes 2097152 | tf_op jit(solution)/shard_map/all_to_all | solution.py:339
  86.2 12.2 %collective-permute-start.3 = (bf16[512,128]{1,0:T(8,128)(2,1)S(1)}, bf16[512,128]{1,0:T(8,128)(2,1)S(1)}, u32[]{:S(2)}, u32[]{:S(2)}) collective-permute-start(bf16[512,128]{1,0:T(8,128)(2,1)S(1)} %get-tuple-element.25), channel_id=1, source_target_pairs={{0,0},{1,16},{16,32},{17,48},{32,1},{33,17},{48,33},{49,49},{2,2},... | collective-permute-start | bytes 393224 | tf_op jit(solution)/shard_map/ppermute | solution.py:265
  89.5 9.5 %collective-permute-start.4 = (bf16[512,128]{1,0:T(8,128)(2,1)S(1)}, bf16[512,128]{1,0:T(8,128)(2,1)S(1)}, u32[]{:S(2)}, u32[]{:S(2)}) collective-permute-start(bf16[512,128]{1,0:T(8,128)(2,1)S(1)} %get-tuple-element.26), channel_id=1, source_target_pairs={{0,16},{1,0},{16,48},{17,32},{32,17},{33,1},{48,49},{49,33},{2,18}... | collective-permute-start | bytes 393224 | tf_op jit(solution)/shard_map/ppermute | solution.py:266
  99.1 44.7 %copy-start.3 = (bf16[1024,128]{1,0:T(8,128)(2,1)}, bf16[1024,128]{1,0:T(8,128)(2,1)S(1)}, u32[]{:S(2)}) copy-start(bf16[1024,128]{1,0:T(8,128)(2,1)S(1)} %pad_maximum_fusion.refs_0_) | copy-start | bytes 786436
  99.1 12.3 %collective-permute-start.5 = (bf16[1024,128]{1,0:T(8,128)(2,1)S(1)}, bf16[1024,128]{1,0:T(8,128)(2,1)S(1)}, u32[]{:S(2)}, u32[]{:S(2)}) collective-permute-start(bf16[1024,128]{1,0:T(8,128)(2,1)S(1)} %pad_maximum_fusion.refs_0_), channel_id=1, source_target_pairs={{0,64},{64,128},{128,192},{192,256},{256,320},{320,384},{384,448},... | collective-permute-start | bytes 786440 | tf_op jit(solution)/shard_map/ppermute | solution.py:275
  101.2 42.6 %copy-start.1 = (bf16[4,256,512]{2,1,0:T(8,128)(2,1)}, bf16[4,256,512]{2,1,0:T(8,128)(2,1)S(1)}, u32[]{:S(2)}) copy-start(bf16[4,256,512]{2,1,0:T(8,128)(2,1)S(1)} %all-to-all-done.2) | copy-start | bytes 3145732
  101.2 42.6 %collective-permute-start.2 = (bf16[1024,512]{1,0:T(8,128)(2,1)S(1)}, bf16[1024,512]{1,0:T(8,128)(2,1)S(1)}, u32[]{:S(2)}, u32[]{:S(2)}) collective-permute-start(bf16[1024,512]{1,0:T(8,128)(2,1)S(1)} %bitcast.16), channel_id=1, source_target_pairs={{0,1},{1,0},{2,3},{3,2},{4,5},{5,4},{6,7},{7,6},{8,9},{9,8},{10,11... | collective-permute-start | bytes 3145736 | tf_op jit(solution)/shard_map/ppermute | solution.py:341
  104.0 10.6 %collective-permute-start.6 = (bf16[1024,128]{1,0:T(8,128)(2,1)S(1)}, bf16[1024,128]{1,0:T(8,128)(2,1)S(1)}, u32[]{:S(2)}, u32[]{:S(2)}) collective-permute-start(bf16[1024,128]{1,0:T(8,128)(2,1)S(1)} %pad_maximum_fusion.refs_0_), channel_id=1, source_target_pairs={{0,448},{64,0},{128,64},{192,128},{256,192},{320,256},{384,320},{4... | collective-permute-start | bytes 786440 | tf_op jit(solution)/shard_map/ppermute | solution.py:275
  111.4 32.4 %copy-start.7 = (bf16[1024,128]{1,0:T(8,128)(2,1)}, bf16[1024,128]{1,0:T(8,128)(2,1)S(1)}, u32[]{:S(2)}) copy-start(bf16[1024,128]{1,0:T(8,128)(2,1)S(1)} %collective-permute-done.5.refs_1_) | copy-start | bytes 786436
  111.4 11.4 %collective-permute-start.7 = (bf16[1024,128]{1,0:T(8,128)(2,1)S(1)}, bf16[1024,128]{1,0:T(8,128)(2,1)S(1)}, u32[]{:S(2)}, u32[]{:S(2)}) collective-permute-start(bf16[1024,128]{1,0:T(8,128)(2,1)S(1)} %collective-permute-done.5.refs_1_), channel_id=1, source_target_pairs={{0,64},{64,128},{128,192},{192,256},{256,320},{320,384},{384,448},... | collective-permute-start | bytes 786440 | tf_op jit(solution)/shard_map/ppermute | solution.py:275
  114.6 29.2 %copy-start.8 = (bf16[1024,128]{1,0:T(8,128)(2,1)}, bf16[1024,128]{1,0:T(8,128)(2,1)S(1)}, u32[]{:S(2)}) copy-start(bf16[1024,128]{1,0:T(8,128)(2,1)S(1)} %collective-permute-done.6.refs_2_) | copy-start | bytes 786436
  114.6 10.5 %collective-permute-start.8 = (bf16[1024,128]{1,0:T(8,128)(2,1)S(1)}, bf16[1024,128]{1,0:T(8,128)(2,1)S(1)}, u32[]{:S(2)}, u32[]{:S(2)}) collective-permute-start(bf16[1024,128]{1,0:T(8,128)(2,1)S(1)} %collective-permute-done.6.refs_2_), channel_id=1, source_target_pairs={{0,448},{64,0},{128,64},{192,128},{256,192},{320,256},{384,320},{4... | collective-permute-start | bytes 786440 | tf_op jit(solution)/shard_map/ppermute | solution.py:275
  122.8 21.0 %copy-start.9 = (bf16[1024,128]{1,0:T(8,128)(2,1)}, bf16[1024,128]{1,0:T(8,128)(2,1)S(1)}, u32[]{:S(2)}) copy-start(bf16[1024,128]{1,0:T(8,128)(2,1)S(1)} %collective-permute-done.7.refs_3_) | copy-start | bytes 786436
  122.8 10.6 %collective-permute-start.9 = (bf16[1024,128]{1,0:T(8,128)(2,1)S(1)}, bf16[1024,128]{1,0:T(8,128)(2,1)S(1)}, u32[]{:S(2)}, u32[]{:S(2)}) collective-permute-start(bf16[1024,128]{1,0:T(8,128)(2,1)S(1)} %collective-permute-done.7.refs_3_), channel_id=1, source_target_pairs={{0,64},{64,128},{128,192},{192,256},{256,320},{320,384},{384,448},... | collective-permute-start | bytes 786440 | tf_op jit(solution)/shard_map/ppermute | solution.py:275
  125.0 18.8 %copy-start.10 = (bf16[1024,128]{1,0:T(8,128)(2,1)}, bf16[1024,128]{1,0:T(8,128)(2,1)S(1)}, u32[]{:S(2)}) copy-start(bf16[1024,128]{1,0:T(8,128)(2,1)S(1)} %collective-permute-done.8.refs_4_) | copy-start | bytes 786436
  125.0 10.3 %collective-permute-start.10 = (bf16[1024,128]{1,0:T(8,128)(2,1)S(1)}, bf16[1024,128]{1,0:T(8,128)(2,1)S(1)}, u32[]{:S(2)}, u32[]{:S(2)}) collective-permute-start(bf16[1024,128]{1,0:T(8,128)(2,1)S(1)} %collective-permute-done.8.refs_4_), channel_id=1, source_target_pairs={{0,448},{64,0},{128,64},{192,128},{256,192},{320,256},{384,320},{4... | collective-permute-start | bytes 786440 | tf_op jit(solution)/shard_map/ppermute | solution.py:275
  133.4 1.9 copy-start.11
  133.4 9.7 %collective-permute-start.11 = (bf16[1024,128]{1,0:T(8,128)(2,1)S(1)}, bf16[1024,128]{1,0:T(8,128)(2,1)S(1)}, u32[]{:S(2)}, u32[]{:S(2)}) collective-permute-start(bf16[1024,128]{1,0:T(8,128)(2,1)S(1)} %collective-permute-done.9.refs_5_), channel_id=1, source_target_pairs={{0,64},{64,128},{128,192},{192,256},{256,320},{320,384},{384,448},... | collective-permute-start | bytes 786440 | tf_op jit(solution)/shard_map/ppermute | solution.py:275
  135.3 7.8 %copy-start.12 = (bf16[1024,128]{1,0:T(8,128)(2,1)}, bf16[1024,128]{1,0:T(8,128)(2,1)S(1)}, u32[]{:S(2)}) copy-start(bf16[1024,128]{1,0:T(8,128)(2,1)S(1)} %collective-permute-done.10.refs_6_) | copy-start | bytes 786436
  143.1 0.7 copy-start.13
  143.9 1.0 copy-start.6

commit v4 on v3

--- a/solution.py
+++ b/solution.py
@@ -61,43 +61,31 @@
     return total
 
 
-def pack_kernel(bpd, src, kv, q, slots):
-    @pl.when(pl.program_id(0) == 0)
-    def _():
-        me = stretch_id()
-
-        def count(c, slot):
-            mine = bpd[0, c] == me
-            for k in range(1, bpd.shape[0]):
-                mine = mine | (bpd[k, c] == me)
-            slots[c] = slot
-            return slot + mine.astype(jnp.int32)
-
-        lax.fori_loop(0, bpd.shape[1], count, jnp.int32(0))
-
-    def one(c, carry):
-        rows = pl.ds(pl.multiple_of(slots[c] * BLK, BLK), BLK)
-        kv[c, 0] = src[1, rows, :]
-        kv[c, 1] = src[2, rows, :]
-        q[c] = src[0, rows, :]
-        return carry
-
-    lax.fori_loop(0, bpd.shape[1], one, 0, unroll=4)
+def pack_kernel(bpd, src, kv, q, sems):
+    me = stretch_id()
+
+    def one(c, slot):
+        mine = bpd[0, c] == me
+        for k in range(1, bpd.shape[0]):
+            mine = mine | (bpd[k, c] == me)
+        rows = pl.ds(pl.multiple_of(slot * BLK, BLK), BLK)
+        pltpu.make_async_copy(src.at[pl.ds(1, 2), rows, :], kv.at[c], sems.at[0]).start()
+        pltpu.make_async_copy(src.at[0, rows, :], q.at[c], sems.at[1]).start()
+        return slot + mine.astype(jnp.int32)
+
+    lax.fori_loop(0, bpd.shape[1], one, jnp.int32(0), unroll=2)
+    pltpu.make_async_copy(kv, kv, sems.at[0]).wait()
+    pltpu.make_async_copy(q, q, sems.at[1]).wait()
 
 
 def packed_blocks(bpd, src, stretches):
     width = src.shape[2]
-    lane = width // 4
     return pl.pallas_call(
         pack_kernel,
-        grid=(width // lane,),
-        in_specs=[smem(), pl.BlockSpec((3, src.shape[1], lane), lambda i: (0, 0, i))],
-        out_specs=[
-            pl.BlockSpec((stretches, 2, BLK, lane), lambda i: (0, 0, 0, i)),
-            pl.BlockSpec((stretches, BLK, lane), lambda i: (0, 0, i)),
-        ],
+        in_specs=[smem(), vmem()],
+        out_specs=[pl.BlockSpec(memory_space=pl.ANY)] * 2,
         out_shape=[shape((stretches, 2, BLK, width)), shape((stretches, BLK, width))],
-        scratch_shapes=[pltpu.SMEM((stretches,), jnp.int32)],
+        scratch_shapes=[pltpu.SemaphoreType.DMA((2,))],
         cost_estimate=pl.CostEstimate(
             flops=10**6, bytes_accessed=4 * src.size, transcendentals=0
         ),
@@ -197,15 +185,13 @@
 
 def project_kernel(offsets, own, other, *refs):
     weights, out = refs[:-1], refs[-1]
-    k = own.shape[1]
     lane = out.shape[3]
     n = out.shape[0]
     y = lax.axis_index("y")
+    left = jnp.concatenate([own[...], other[...]], axis=1)
     for pair in range(0, n, 2):
         wide = jnp.concatenate([weights[pair][...], weights[pair + 1][...]], axis=1)
-        got = jnp.dot(own[...], wide[:k], preferred_element_type=F32)
-        got = got + jnp.dot(other[...], wide[k:], preferred_element_type=F32)
-        got = got.astype(BF16)
+        got = jnp.dot(left, wide, preferred_element_type=F32).astype(BF16)
         for i in range(2):
             at = lax.rem(y - offsets[pair + i] + n, n)
             for s in range(out.shape[1]):

time: 213 us -> 211 us (level)
  no operation moved by 1% of the time
where the time goes in v4:
time: 211 us; the launch traced here: 210 us
  blocking collectives  94.4 us (45%)
  starting transfers between devices  55.9 us (26%)
  waiting for transfers between devices  26.7 us (13%)
  Pallas kernels  24.2 us (11%)
  other arithmetic  3.2 us (2%)
  local copies, waits for them, and re-layouts  3.06 us (1%)
  between operations  2.38 us (1%)
    all_to_all x1, blocking collectives, operator(): lax.all_to_all(flat, ('z', 'x'), split_axis=0, concat_axis=0, tiled=True)  60.3 us
    all_to_all x1, blocking collectives, operator(): kv_in = lax.all_to_all(kv_out, CTX, split_axis=0, concat_axis=0, tiled=True)  34.1 us
    ppermute x7, starting transfers between devices, around(): return lax.ppermute(block, 'y', [(i, (i + distance) % n) for i in range(n)])  23.8 us
    ppermute x7, waiting for transfers between devices, around(): return lax.ppermute(block, 'y', [(i, (i + distance) % n) for i in range(n)])  17.3 us
    pallas_call x4, Pallas kernels, call(): pl.pallas_call(body, out_shape=outs, in_specs=ins, out_specs=[vmem()] * l...  15.8 us
    all_to_all x1, starting transfers between devices, operator(): q_in = lax.all_to_all(q_out, CTX, split_axis=0, concat_axis=0, tiled=True)  9.48 us
    all_to_all x1, starting transfers between devices, operator(): own = lax.all_to_all(copies, 'x', split_axis=0, concat_axis=0, tiled=True)  7.36 us
    ppermute x2, starting transfers between devices, passed_along(): return lax.ppermute(block, CTX, [(i, i + 1) for i in range(n - 1)])  6.57 us
  transfers between devices with their start and end apart: 14, of which 9 were waited for; matrix products, arithmetic and copies ran while one was open for 1% of the time, Pallas kernels for 6%

profile of v4, /device:TPU:34, one launch (start us, length us, event | category | flops | bytes accessed | tf_op | source)
XLA Modules:
  0.0 209.8 jit_solution(7939247787614960734)
XLA Ops:
  0.0 3.0 %pack.1 = (bf16[32,2,16,512]{3,2,1,0:T(8,128)(2,1)}, bf16[32,16,512]{2,1,0:T(8,128)(2,1)}) custom-call(s32[16,32]{1,0:T(8,128)} %bitcast.18, bf16[3,512,512]{2,1,0:T(8,128)(2,1)} %bitcast.15), custom_call_target="tpu_custom_call" | custom-call | flops 1000000 | bytes 3145728 | tf_op jit(solution)/shard_map/pack/pallas_call | solution.py:83
  3.0 0.0 copy-start.5
  3.0 34.1 %all_to_all.20.kv = bf16[32,2,16,512]{3,2,1,0:T(8,128)(2,1)} all-to-all(bf16[32,2,16,512]{3,2,1,0:T(8,128)(2,1)} %get-tuple-element.12), channel_id=1, replica_groups=mesh['y'=8,'x'=4,'z'=8,'core'=2] {'y','x'}, dimensions={0} | all-to-all | bytes 2097152 | tf_op jit(solution)/shard_map/all_to_all | solution.py:280
  37.0 9.5 %all-to-all-start.1 = ((bf16[32,16,512]{2,1,0:T(8,128)(2,1)}), bf16[32,16,512]{2,1,0:T(8,128)(2,1)S(1)}, u32[]{:S(2)}, u32[]{:S(2)}) async-start(bf16[32,16,512]{2,1,0:T(8,128)(2,1)} %get-tuple-element.16), calls=%async_computation.1 | async-start | bytes 1048576 | tf_op jit(solution)/shard_map/all_to_all | solution.py:281
  46.5 3.7 %shard_map.73 = (bf16[256,512]{1,0:T(8,128)(2,1)}, bf16[144,512]{1,0:T(8,128)(2,1)}, bf16[16,512]{1,0:T(8,128)(2,1)}) custom-call(s32[16,32]{1,0:T(8,128)} %bitcast.19, s32[8]{0:T(128)} %lengths.5, bf16[32,2,16,512]{3,2,1,0:T(8,128)(2,1)} %all_to_all.20.kv, bf16[3,7,512]{2,1,0:T(8,128)(2,1)} %taps.5), custom_call_target="tpu_custom_call" | custom-call | flops 10000000 | bytes 1498144 | tf_op jit(solution)/shard_map/pallas_call | solution.py:34
  50.3 3.4 %collective-permute-start = (bf16[144,512]{1,0:T(8,128)(2,1)}, bf16[144,512]{1,0:T(8,128)(2,1)S(1)}, u32[]{:S(2)}, u32[]{:S(2)}) collective-permute-start(bf16[144,512]{1,0:T(8,128)(2,1)} %get-tuple-element.14), channel_id=1, source_target_pairs={{0,16},{16,32},{32,48},{48,64},{64,80},{80,96},{96,112},{112,128},... | collective-permute-start | bytes 442376 | tf_op jit(solution)/shard_map/ppermute | solution.py:238
  53.6 1.4 fusion
  56.4 0.1 rev.3
  57.2 0.7 pad_convert_fusion.line
  57.9 4.9 %shard_map.74.bands = bf16[32,128,256]{2,1,0:T(8,128)(2,1)} custom-call(f32[32,256]{1,0:T(8,128)} %pad_convert_fusion.line), custom_call_target="tpu_custom_call" | custom-call | flops 100000000 | bytes 2129920 | tf_op jit(solution)/shard_map/pallas_call | solution.py:34
  62.8 0.0 collective-permute-done.recv
  62.8 0.7 copy-done.14
  63.5 3.9 %shard_map.75.medium = f32[256,512]{1,0:T(8,128)} custom-call(s32[8]{0:T(128)} %lengths.5, bf16[256,512]{1,0:T(8,128)(2,1)} %get-tuple-element.13.z, bf16[144,512]{1,0:T(8,128)(2,1)} %copy-done.14, bf16[16,512]{1,0:T(8,128)(2,1)} %get-tuple-element.15.head, bf16[3,7,512]{2,1,0:T(8,128)(2,1)} %taps.5, bf16[32,128,256]{2,1,0:T(8,128)(2,1)} %shard_map.74.bands, ...), custom_call_target="tpu_custom_call" | custom-call | flops 1000000000 | bytes 3071008 | tf_op jit(solution)/shard_map/pallas_call | solution.py:34
  67.4 0.0 all-to-all-done.1.q
  67.5 0.0 copy-start.2
  67.5 3.2 %collective-permute-start.1 = (bf16[8,512]{1,0:T(8,128)(2,1)S(1)}, bf16[8,512]{1,0:T(8,128)(2,1)S(1)}, u32[]{:S(2)}, u32[]{:S(2)}) collective-permute-start(bf16[8,512]{1,0:T(8,128)(2,1)S(1)} %dynamic-slice_bitcast_fusion), channel_id=1, source_target_pairs={{0,16},{16,32},{32,48},{48,64},{64,80},{80,96},{96,112},{112,128},... | collective-permute-start | bytes 24584 | tf_op jit(solution)/shard_map/ppermute | solution.py:238
  70.7 2.5 %collective-permute-done.1.halo = bf16[8,512]{1,0:T(8,128)(2,1)S(1)} collective-permute-done((bf16[8,512]{1,0:T(8,128)(2,1)S(1)}, bf16[8,512]{1,0:T(8,128)(2,1)S(1)}, u32[]{:S(2)}, u32[]{:S(2)}) %collective-permute-start.1) | collective-permute-done | bytes 8224 | tf_op jit(solution)/shard_map/ppermute | solution.py:238
  73.1 0.6 copy-done.4
  73.7 3.2 %shard_map.76 = bf16[4,256,512]{2,1,0:T(8,128)(2,1)} custom-call(s32[16,32]{1,0:T(8,128)} %bitcast.21, s32[8]{0:T(128)} %lengths.5, bf16[32,16,512]{2,1,0:T(8,128)(2,1)} %copy-done, bf16[8,512]{1,0:T(8,128)(2,1)} %copy-done.4, bf16[3,7,512]{2,1,0:T(8,128)(2,1)} %taps.5, f32[256,512]{1,0:T(8,128)} %shard_map.75.medium), custom_call_target="tpu_custom_call" | custom-call | flops 10000000 | bytes 2128928 | tf_op jit(solution)/shard_map/pallas_call | solution.py:34
  76.9 7.4 %all-to-all-start.2 = ((bf16[4,256,512]{2,1,0:T(8,128)(2,1)}), bf16[4,256,512]{2,1,0:T(8,128)(2,1)S(1)}, u32[]{:S(2)}, u32[]{:S(2)}) async-start(bf16[4,256,512]{2,1,0:T(8,128)(2,1)} %shard_map.76), calls=%async_computation.2 | async-start | bytes 2097152 | tf_op jit(solution)/shard_map/all_to_all | solution.py:325
  84.3 3.4 %collective-permute-start.3 = (bf16[512,128]{1,0:T(8,128)(2,1)S(1)}, bf16[512,128]{1,0:T(8,128)(2,1)S(1)}, u32[]{:S(2)}, u32[]{:S(2)}) collective-permute-start(bf16[512,128]{1,0:T(8,128)(2,1)S(1)} %get-tuple-element.25), channel_id=1, source_target_pairs={{0,0},{1,16},{16,32},{17,48},{32,1},{33,17},{48,33},{49,49},{2,2},... | collective-permute-start | bytes 393224 | tf_op jit(solution)/shard_map/ppermute | solution.py:251
  87.7 2.5 %collective-permute-start.4 = (bf16[512,128]{1,0:T(8,128)(2,1)S(1)}, bf16[512,128]{1,0:T(8,128)(2,1)S(1)}, u32[]{:S(2)}, u32[]{:S(2)}) collective-permute-start(bf16[512,128]{1,0:T(8,128)(2,1)S(1)} %get-tuple-element.26), channel_id=1, source_target_pairs={{0,16},{1,0},{16,48},{17,32},{32,17},{33,1},{48,49},{49,33},{2,18}... | collective-permute-start | bytes 393224 | tf_op jit(solution)/shard_map/ppermute | solution.py:252
  90.3 6.2 %collective-permute-done.3 = bf16[512,128]{1,0:T(8,128)(2,1)S(1)} collective-permute-done((bf16[512,128]{1,0:T(8,128)(2,1)S(1)}, bf16[512,128]{1,0:T(8,128)(2,1)S(1)}, u32[]{:S(2)}, u32[]{:S(2)}) %collective-permute-start.3) | collective-permute-done | bytes 131104 | tf_op jit(solution)/shard_map/ppermute | solution.py:251
  96.5 0.7 collective-permute-done.4
  97.3 0.0 copy-start.3
  97.3 2.0 collective-permute-start.5
  99.3 0.0 all-to-all-done.2
  99.3 2.8 %collective-permute-start.2 = (bf16[1024,512]{1,0:T(8,128)(2,1)S(1)}, bf16[1024,512]{1,0:T(8,128)(2,1)S(1)}, u32[]{:S(2)}, u32[]{:S(2)}) collective-permute-start(bf16[1024,512]{1,0:T(8,128)(2,1)S(1)} %bitcast.16), channel_id=1, source_target_pairs={{0,1},{1,0},{2,3},{3,2},{4,5},{5,4},{6,7},{7,6},{8,9},{9,8},{10,11... | collective-permute-start | bytes 3145736 | tf_op jit(solution)/shard_map/ppermute | solution.py:327
  102.2 4.9 %collective-permute-start.6 = (bf16[1024,128]{1,0:T(8,128)(2,1)S(1)}, bf16[1024,128]{1,0:T(8,128)(2,1)S(1)}, u32[]{:S(2)}, u32[]{:S(2)}) collective-permute-start(bf16[1024,128]{1,0:T(8,128)(2,1)S(1)} %pad_maximum_fusion.refs_0_), channel_id=1, source_target_pairs={{0,448},{64,0},{128,64},{192,128},{256,192},{320,256},{384,320},{4... | collective-permute-start | bytes 786440 | tf_op jit(solution)/shard_map/ppermute | solution.py:261
  107.0 2.5 %collective-permute-done.5.refs_1_ = bf16[1024,128]{1,0:T(8,128)(2,1)S(1)} collective-permute-done((bf16[1024,128]{1,0:T(8,128)(2,1)S(1)}, bf16[1024,128]{1,0:T(8,128)(2,1)S(1)}, u32[]{:S(2)}, u32[]{:S(2)}) %collective-permute-start.5) | collective-permute-done | bytes 262176 | tf_op jit(solution)/shard_map/ppermute | solution.py:261
  109.6 1.9 collective-permute-start.7
  111.5 1.3 collective-permute-done.6.refs_2_
  112.8 5.6 %collective-permute-start.8 = (bf16[1024,128]{1,0:T(8,128)(2,1)S(1)}, bf16[1024,128]{1,0:T(8,128)(2,1)S(1)}, u32[]{:S(2)}, u32[]{:S(2)}) collective-permute-start(bf16[1024,128]{1,0:T(8,128)(2,1)S(1)} %collective-permute-done.6.refs_2_), channel_id=1, source_target_pairs={{0,448},{64,0},{128,64},{192,128},{256,192},{320,256},{384,320},{4... | collective-permute-start | bytes 786440 | tf_op jit(solution)/shard_map/ppermute | solution.py:261
  118.4 2.7 %collective-permute-done.7.refs_3_ = bf16[1024,128]{1,0:T(8,128)(2,1)S(1)} collective-permute-done((bf16[1024,128]{1,0:T(8,128)(2,1)S(1)}, bf16[1024,128]{1,0:T(8,128)(2,1)S(1)}, u32[]{:S(2)}, u32[]{:S(2)}) %collective-permute-start.7) | collective-permute-done | bytes 262176 | tf_op jit(solution)/shard_map/ppermute | solution.py:261
  121.0 1.9 collective-permute-start.9
  122.9 0.3 collective-permute-done.8.refs_4_
  123.2 5.6 %collective-permute-start.10 = (bf16[1024,128]{1,0:T(8,128)(2,1)S(1)}, bf16[1024,128]{1,0:T(8,128)(2,1)S(1)}, u32[]{:S(2)}, u32[]{:S(2)}) collective-permute-start(bf16[1024,128]{1,0:T(8,128)(2,1)S(1)} %collective-permute-done.8.refs_4_), channel_id=1, source_target_pairs={{0,448},{64,0},{128,64},{192,128},{256,192},{320,256},{384,320},{4... | collective-permute-start | bytes 786440 | tf_op jit(solution)/shard_map/ppermute | solution.py:261
  128.8 2.8 %collective-permute-done.9.refs_5_ = bf16[1024,128]{1,0:T(8,128)(2,1)S(1)} collective-permute-done((bf16[1024,128]{1,0:T(8,128)(2,1)S(1)}, bf16[1024,128]{1,0:T(8,128)(2,1)S(1)}, u32[]{:S(2)}, u32[]{:S(2)}) %collective-permute-start.9) | collective-permute-done | bytes 262176 | tf_op jit(solution)/shard_map/ppermute | solution.py:261
  131.6 1.9 collective-permute-start.11
  133.5 0.0 collective-permute-done.10.refs_6_
  133.5 7.8 %collective-permute-done.11.refs_7_ = bf16[1024,128]{1,0:T(8,128)(2,1)S(1)} collective-permute-done((bf16[1024,128]{1,0:T(8,128)(2,1)S(1)}, bf16[1024,128]{1,0:T(8,128)(2,1)S(1)}, u32[]{:S(2)}, u32[]{:S(2)}) %collective-permute-start.11) | collective-permute-done | bytes 262176 | tf_op jit(solution)/shard_map/ppermute | solution.py:261
  141.3 0.7 copy-done.13
  142.0 0.0 collective-permute-done.2.other
  142.0 1.0 copy-done.6
  143.0 5.5 %project.1 = bf16[8,4,256,128]{3,2,1,0:T(8,128)(2,1)} custom-call(bf16[1024,512]{1,0:T(8,128)(2,1)} %bitcast.17, bf16[1024,512]{1,0:T(8,128)(2,1)} %copy-done.6, bf16[1024,128]{1,0:T(8,128)(2,1)} %copy-done.3, bf16[1024,128]{1,0:T(8,128)(2,1)} %copy-done.7, bf16[1024,128]{1,0:T(8,128)(2,1)} %copy-done.8, bf16[1024,128]{1,0:T(8,128)(2,1)} %copy-done.9, ...), custom_call_target="tpu_custom_call" | custom-call | flops 2147483648 | bytes 8388608 | tf_op jit(solution)/shard_map/project/pallas_call | solution.py:210
  148.5 60.3 %all_to_all.21 = bf16[32,256,128]{2,1,0:T(8,128)(2,1)S(1)} all-to-all(bf16[32,256,128]{2,1,0:T(8,128)(2,1)} %bitcast.14), channel_id=1, replica_groups=mesh['y'=8,'x'=4,'z'=8,'core'=2] {'z','x'}, dimensions={0} | all-to-all | bytes 4194304 | tf_op jit(solution)/shard_map/all_to_all | solution.py:330
  208.8 0.3 slice_reduce_fusion.3
  209.1 0.7 pad_maximum_fusion.1
  (27 shorter events, 0.1 us)
Async XLA Ops:
  3.0 53.4 %copy-start.5 = (bf16[128,32]{0,1:T(8,128)(2,1)S(1)}, bf16[128,32]{0,1:T(8,128)(2,1)}, u32[]{:S(2)}) copy-start(bf16[128,32]{0,1:T(8,128)(2,1)} %param.9) | copy-start | bytes 24580
  37.0 30.4 %all-to-all-start.1 = ((bf16[32,16,512]{2,1,0:T(8,128)(2,1)}), bf16[32,16,512]{2,1,0:T(8,128)(2,1)S(1)}, u32[]{:S(2)}, u32[]{:S(2)}) async-start(bf16[32,16,512]{2,1,0:T(8,128)(2,1)} %get-tuple-element.16), calls=%async_computation.1 | async-start | bytes 1048576 | tf_op jit(solution)/shard_map/all_to_all | solution.py:281
  50.3 12.6 %collective-permute-start = (bf16[144,512]{1,0:T(8,128)(2,1)}, bf16[144,512]{1,0:T(8,128)(2,1)S(1)}, u32[]{:S(2)}, u32[]{:S(2)}) collective-permute-start(bf16[144,512]{1,0:T(8,128)(2,1)} %get-tuple-element.14), channel_id=1, source_target_pairs={{0,16},{16,32},{32,48},{48,64},{64,80},{80,96},{96,112},{112,128},... | collective-permute-start | bytes 442376 | tf_op jit(solution)/shard_map/ppermute | solution.py:238
  62.8 0.7 copy-start.14
  67.4 5.7 %copy-start = (bf16[32,16,512]{2,1,0:T(8,128)(2,1)}, bf16[32,16,512]{2,1,0:T(8,128)(2,1)S(1)}, u32[]{:S(2)}) copy-start(bf16[32,16,512]{2,1,0:T(8,128)(2,1)S(1)} %all-to-all-done.1.q) | copy-start | bytes 1572868
  67.5 16.9 %copy-start.2 = (bf16[512,256]{1,0:T(8,128)(2,1)S(1)}, bf16[512,256]{1,0:T(8,128)(2,1)}, u32[]{:S(2)}) copy-start(bf16[512,256]{1,0:T(8,128)(2,1)} %param.11) | copy-start | bytes 786436
  67.5 5.7 %collective-permute-start.1 = (bf16[8,512]{1,0:T(8,128)(2,1)S(1)}, bf16[8,512]{1,0:T(8,128)(2,1)S(1)}, u32[]{:S(2)}, u32[]{:S(2)}) collective-permute-start(bf16[8,512]{1,0:T(8,128)(2,1)S(1)} %dynamic-slice_bitcast_fusion), channel_id=1, source_target_pairs={{0,16},{16,32},{32,48},{48,64},{64,80},{80,96},{96,112},{112,128},... | collective-permute-start | bytes 24584 | tf_op jit(solution)/shard_map/ppermute | solution.py:238
  73.1 0.6 copy-start.4
  76.9 22.4 %all-to-all-start.2 = ((bf16[4,256,512]{2,1,0:T(8,128)(2,1)}), bf16[4,256,512]{2,1,0:T(8,128)(2,1)S(1)}, u32[]{:S(2)}, u32[]{:S(2)}) async-start(bf16[4,256,512]{2,1,0:T(8,128)(2,1)} %shard_map.76), calls=%async_computation.2 | async-start | bytes 2097152 | tf_op jit(solution)/shard_map/all_to_all | solution.py:325
  84.3 12.2 %collective-permute-start.3 = (bf16[512,128]{1,0:T(8,128)(2,1)S(1)}, bf16[512,128]{1,0:T(8,128)(2,1)S(1)}, u32[]{:S(2)}, u32[]{:S(2)}) collective-permute-start(bf16[512,128]{1,0:T(8,128)(2,1)S(1)} %get-tuple-element.25), channel_id=1, source_target_pairs={{0,0},{1,16},{16,32},{17,48},{32,1},{33,17},{48,33},{49,49},{2,2},... | collective-permute-start | bytes 393224 | tf_op jit(solution)/shard_map/ppermute | solution.py:251
  87.7 9.5 %collective-permute-start.4 = (bf16[512,128]{1,0:T(8,128)(2,1)S(1)}, bf16[512,128]{1,0:T(8,128)(2,1)S(1)}, u32[]{:S(2)}, u32[]{:S(2)}) collective-permute-start(bf16[512,128]{1,0:T(8,128)(2,1)S(1)} %get-tuple-element.26), channel_id=1, source_target_pairs={{0,16},{1,0},{16,48},{17,32},{32,17},{33,1},{48,49},{49,33},{2,18}... | collective-permute-start | bytes 393224 | tf_op jit(solution)/shard_map/ppermute | solution.py:252
  97.3 44.7 %copy-start.3 = (bf16[1024,128]{1,0:T(8,128)(2,1)}, bf16[1024,128]{1,0:T(8,128)(2,1)S(1)}, u32[]{:S(2)}) copy-start(bf16[1024,128]{1,0:T(8,128)(2,1)S(1)} %pad_maximum_fusion.refs_0_) | copy-start | bytes 786436
  97.3 12.3 %collective-permute-start.5 = (bf16[1024,128]{1,0:T(8,128)(2,1)S(1)}, bf16[1024,128]{1,0:T(8,128)(2,1)S(1)}, u32[]{:S(2)}, u32[]{:S(2)}) collective-permute-start(bf16[1024,128]{1,0:T(8,128)(2,1)S(1)} %pad_maximum_fusion.refs_0_), channel_id=1, source_target_pairs={{0,64},{64,128},{128,192},{192,256},{256,320},{320,384},{384,448},... | collective-permute-start | bytes 786440 | tf_op jit(solution)/shard_map/ppermute | solution.py:261
  99.3 42.6 %copy-start.1 = (bf16[4,256,512]{2,1,0:T(8,128)(2,1)}, bf16[4,256,512]{2,1,0:T(8,128)(2,1)S(1)}, u32[]{:S(2)}) copy-start(bf16[4,256,512]{2,1,0:T(8,128)(2,1)S(1)} %all-to-all-done.2) | copy-start | bytes 3145732
  99.3 42.6 %collective-permute-start.2 = (bf16[1024,512]{1,0:T(8,128)(2,1)S(1)}, bf16[1024,512]{1,0:T(8,128)(2,1)S(1)}, u32[]{:S(2)}, u32[]{:S(2)}) collective-permute-start(bf16[1024,512]{1,0:T(8,128)(2,1)S(1)} %bitcast.16), channel_id=1, source_target_pairs={{0,1},{1,0},{2,3},{3,2},{4,5},{5,4},{6,7},{7,6},{8,9},{9,8},{10,11... | collective-permute-start | bytes 3145736 | tf_op jit(solution)/shard_map/ppermute | solution.py:327
  102.2 10.6 %collective-permute-start.6 = (bf16[1024,128]{1,0:T(8,128)(2,1)S(1)}, bf16[1024,128]{1,0:T(8,128)(2,1)S(1)}, u32[]{:S(2)}, u32[]{:S(2)}) collective-permute-start(bf16[1024,128]{1,0:T(8,128)(2,1)S(1)} %pad_maximum_fusion.refs_0_), channel_id=1, source_target_pairs={{0,448},{64,0},{128,64},{192,128},{256,192},{320,256},{384,320},{4... | collective-permute-start | bytes 786440 | tf_op jit(solution)/shard_map/ppermute | solution.py:261
  109.6 32.4 %copy-start.7 = (bf16[1024,128]{1,0:T(8,128)(2,1)}, bf16[1024,128]{1,0:T(8,128)(2,1)S(1)}, u32[]{:S(2)}) copy-start(bf16[1024,128]{1,0:T(8,128)(2,1)S(1)} %collective-permute-done.5.refs_1_) | copy-start | bytes 786436
  109.6 11.4 %collective-permute-start.7 = (bf16[1024,128]{1,0:T(8,128)(2,1)S(1)}, bf16[1024,128]{1,0:T(8,128)(2,1)S(1)}, u32[]{:S(2)}, u32[]{:S(2)}) collective-permute-start(bf16[1024,128]{1,0:T(8,128)(2,1)S(1)} %collective-permute-done.5.refs_1_), channel_id=1, source_target_pairs={{0,64},{64,128},{128,192},{192,256},{256,320},{320,384},{384,448},... | collective-permute-start | bytes 786440 | tf_op jit(solution)/shard_map/ppermute | solution.py:261
  112.8 29.2 %copy-start.8 = (bf16[1024,128]{1,0:T(8,128)(2,1)}, bf16[1024,128]{1,0:T(8,128)(2,1)S(1)}, u32[]{:S(2)}) copy-start(bf16[1024,128]{1,0:T(8,128)(2,1)S(1)} %collective-permute-done.6.refs_2_) | copy-start | bytes 786436
  112.8 10.5 %collective-permute-start.8 = (bf16[1024,128]{1,0:T(8,128)(2,1)S(1)}, bf16[1024,128]{1,0:T(8,128)(2,1)S(1)}, u32[]{:S(2)}, u32[]{:S(2)}) collective-permute-start(bf16[1024,128]{1,0:T(8,128)(2,1)S(1)} %collective-permute-done.6.refs_2_), channel_id=1, source_target_pairs={{0,448},{64,0},{128,64},{192,128},{256,192},{320,256},{384,320},{4... | collective-permute-start | bytes 786440 | tf_op jit(solution)/shard_map/ppermute | solution.py:261
  121.0 21.0 %copy-start.9 = (bf16[1024,128]{1,0:T(8,128)(2,1)}, bf16[1024,128]{1,0:T(8,128)(2,1)S(1)}, u32[]{:S(2)}) copy-start(bf16[1024,128]{1,0:T(8,128)(2,1)S(1)} %collective-permute-done.7.refs_3_) | copy-start | bytes 786436
  121.0 10.6 %collective-permute-start.9 = (bf16[1024,128]{1,0:T(8,128)(2,1)S(1)}, bf16[1024,128]{1,0:T(8,128)(2,1)S(1)}, u32[]{:S(2)}, u32[]{:S(2)}) collective-permute-start(bf16[1024,128]{1,0:T(8,128)(2,1)S(1)} %collective-permute-done.7.refs_3_), channel_id=1, source_target_pairs={{0,64},{64,128},{128,192},{192,256},{256,320},{320,384},{384,448},... | collective-permute-start | bytes 786440 | tf_op jit(solution)/shard_map/ppermute | solution.py:261
  123.2 18.8 %copy-start.10 = (bf16[1024,128]{1,0:T(8,128)(2,1)}, bf16[1024,128]{1,0:T(8,128)(2,1)S(1)}, u32[]{:S(2)}) copy-start(bf16[1024,128]{1,0:T(8,128)(2,1)S(1)} %collective-permute-done.8.refs_4_) | copy-start | bytes 786436
  123.2 10.3 %collective-permute-start.10 = (bf16[1024,128]{1,0:T(8,128)(2,1)S(1)}, bf16[1024,128]{1,0:T(8,128)(2,1)S(1)}, u32[]{:S(2)}, u32[]{:S(2)}) collective-permute-start(bf16[1024,128]{1,0:T(8,128)(2,1)S(1)} %collective-permute-done.8.refs_4_), channel_id=1, source_target_pairs={{0,448},{64,0},{128,64},{192,128},{256,192},{320,256},{384,320},{4... | collective-permute-start | bytes 786440 | tf_op jit(solution)/shard_map/ppermute | solution.py:261
  131.6 1.9 copy-start.11
  131.6 9.7 %collective-permute-start.11 = (bf16[1024,128]{1,0:T(8,128)(2,1)S(1)}, bf16[1024,128]{1,0:T(8,128)(2,1)S(1)}, u32[]{:S(2)}, u32[]{:S(2)}) collective-permute-start(bf16[1024,128]{1,0:T(8,128)(2,1)S(1)} %collective-permute-done.9.refs_5_), channel_id=1, source_target_pairs={{0,64},{64,128},{128,192},{192,256},{256,320},{320,384},{384,448},... | collective-permute-start | bytes 786440 | tf_op jit(solution)/shard_map/ppermute | solution.py:261
  133.5 7.8 %copy-start.12 = (bf16[1024,128]{1,0:T(8,128)(2,1)}, bf16[1024,128]{1,0:T(8,128)(2,1)S(1)}, u32[]{:S(2)}) copy-start(bf16[1024,128]{1,0:T(8,128)(2,1)S(1)} %collective-permute-done.10.refs_6_) | copy-start | bytes 786436
  141.3 0.7 copy-start.13
  142.0 1.0 copy-start.6

commit v5 on v4

--- a/solution.py
+++ b/solution.py
@@ -61,7 +61,7 @@
     return total
 
 
-def pack_kernel(bpd, src, kv, q, sems):
+def pack_kernel(bpd, src, out, sem):
     me = stretch_id()
 
     def one(c, slot):
@@ -69,23 +69,20 @@
         for k in range(1, bpd.shape[0]):
             mine = mine | (bpd[k, c] == me)
         rows = pl.ds(pl.multiple_of(slot * BLK, BLK), BLK)
-        pltpu.make_async_copy(src.at[pl.ds(1, 2), rows, :], kv.at[c], sems.at[0]).start()
-        pltpu.make_async_copy(src.at[0, rows, :], q.at[c], sems.at[1]).start()
+        pltpu.make_async_copy(src.at[:, rows, :], out.at[c], sem).start()
         return slot + mine.astype(jnp.int32)
 
     lax.fori_loop(0, bpd.shape[1], one, jnp.int32(0), unroll=2)
-    pltpu.make_async_copy(kv, kv, sems.at[0]).wait()
-    pltpu.make_async_copy(q, q, sems.at[1]).wait()
+    pltpu.make_async_copy(out, out, sem).wait()
 
 
 def packed_blocks(bpd, src, stretches):
-    width = src.shape[2]
     return pl.pallas_call(
         pack_kernel,
         in_specs=[smem(), vmem()],
-        out_specs=[pl.BlockSpec(memory_space=pl.ANY)] * 2,
-        out_shape=[shape((stretches, 2, BLK, width)), shape((stretches, BLK, width))],
-        scratch_shapes=[pltpu.SemaphoreType.DMA((2,))],
+        out_specs=pl.BlockSpec(memory_space=pl.ANY),
+        out_shape=shape((stretches, 3, BLK, src.shape[2])),
+        scratch_shapes=[pltpu.SemaphoreType.DMA],
         cost_estimate=pl.CostEstimate(
             flops=10**6, bytes_accessed=4 * src.size, transcendentals=0
         ),
@@ -99,51 +96,75 @@
         out[g] = pltpu.roll(row, 0, 1, stride=1, stride_axis=0).astype(BF16)
         return carry
 
-    lax.fori_loop(0, out.shape[0], one, 0)
-
-
-def z_kernel(bpd, lengths, kv, taps, z, send, head, buf):
+    lax.fori_loop(0, out.shape[0], one, 0, unroll=4)
+
+
+def gather_rows(bpd, blocks, which, buf):
+    me = stretch_id()
+    buf[0:TAIL, :] = jnp.zeros((TAIL, buf.shape[1]), F32)
+    for k in range((buf.shape[0] - TAIL) // BLK):
+        buf[TAIL + k * BLK : TAIL + (k + 1) * BLK, :] = blocks[bpd[k, me], which].astype(F32)
+
+
+STEP = 32
+
+
+def gated_kernel(bpd, lengths, blocks, taps, z, send, head, buf):
     me = stretch_id()
     rows, width = z.shape
     for i in range(2):
-        buf[i, 0:TAIL, :] = jnp.zeros((TAIL, width), F32)
-    for k in range(rows // BLK):
-        s = bpd[k, me]
-        for i in range(2):
-            buf[i, TAIL + k * BLK : TAIL + (k + 1) * BLK, :] = kv[s, i].astype(F32)
-
-    step = 32
+        gather_rows(bpd, blocks, 1 + i, buf.at[i])
 
     def chunk(r, carry):
-        at = pl.multiple_of(r * step, step)
-        back = reach_back(lengths, me * rows + at, (step, width))
-        wide = pl.ds(at, step + TAIL)
+        at = pl.multiple_of(r * STEP, STEP)
+        back = reach_back(lengths, me * rows + at, (STEP, width))
+        wide = pl.ds(at, STEP + TAIL)
         keyed = short_rows(buf[0, wide, :], taps, 1, back)
         valued = short_rows(buf[1, wide, :], taps, 2, back)
-        z[pl.ds(at, step), :] = (keyed * valued).astype(BF16)
+        z[pl.ds(at, STEP), :] = (keyed * valued).astype(BF16)
         return carry
 
-    lax.fori_loop(0, rows // step, chunk, 0)
+    lax.fori_loop(0, rows // STEP, chunk, 0)
     send[0:HALF, :] = z[rows - HALF :, :]
-    for i in range(2):
-        send[HALF + i * TAIL : HALF + (i + 1) * TAIL, :] = buf[i, rows : rows + TAIL, :].astype(BF16)
-        head[i * TAIL : (i + 1) * TAIL, :] = buf[i, TAIL : 2 * TAIL, :].astype(BF16)
-
-
-def medium_kernel(lengths, z, recv, head, taps, bands, gain, out, ext):
+    q_last = blocks[bpd[rows // BLK - 1, me], 0].astype(F32)[BLK - TAIL :]
+    q_first = blocks[bpd[0, me], 0].astype(F32)[:TAIL]
+    tails = [q_last] + [buf[i, rows : rows + TAIL, :] for i in range(2)]
+    heads = [q_first] + [buf[i, TAIL : 2 * TAIL, :] for i in range(2)]
+    for i in range(3):
+        send[HALF + i * TAIL : HALF + (i + 1) * TAIL, :] = tails[i].astype(BF16)
+        head[i * TAIL : (i + 1) * TAIL, :] = heads[i].astype(BF16)
+
+
+def query_kernel(bpd, lengths, blocks, taps, out, buf):
+    me = stretch_id()
+    rows, width = out.shape
+    gather_rows(bpd, blocks, 0, buf)
+
+    def chunk(r, carry):
+        at = pl.multiple_of(r * STEP, STEP)
+        back = reach_back(lengths, me * rows + at, (STEP, width))
+        out[pl.ds(at, STEP), :] = short_rows(buf[pl.ds(at, STEP + TAIL), :], taps, 0, back)
+        return carry
+
+    lax.fori_loop(0, rows // STEP, chunk, 0)
+
+
+def hidden_kernel(lengths, z, query, recv, head, taps, bands, gain, out, ext, first_q):
     me = stretch_id()
     rows, width = z.shape
     back = reach_back(lengths, me * rows, (TAIL, width))
     fixed = []
-    for i in range(2):
+    for i in range(3):
         tail = recv[HALF + i * TAIL : HALF + (i + 1) * TAIL, :].astype(F32)
         mine = head[i * TAIL : (i + 1) * TAIL, :].astype(F32)
-        fixed.append(short_rows(jnp.concatenate([tail, mine], axis=0), taps, 1 + i, back))
-    first = (fixed[0] * fixed[1]).astype(BF16).astype(F32)
+        fixed.append(short_rows(jnp.concatenate([tail, mine], axis=0), taps, i, back))
+    first = (fixed[1] * fixed[2]).astype(BF16).astype(F32)
     ext[0:HALF, :] = recv[0:HALF, :]
     ext[HALF:, :] = z[...]
     later = z[TAIL : 2 * TAIL, :].astype(F32)
     ext[HALF : HALF + 2 * TAIL, :] = jnp.concatenate([first, later], axis=0).astype(BF16)
+    first_q[0:TAIL, :] = fixed[0]
+    first_q[TAIL:, :] = query[TAIL:HALF, :]
     lane = 128
     per = lane // (width // bands.shape[0])
     group = lax.broadcasted_iota(jnp.int32, (HALF, lane), 1) // (lane // per)
@@ -160,27 +181,15 @@
                 got = jnp.dot(bands[t * per + g] * keep, right, preferred_element_type=F32)
                 total = jnp.where(group == g, got, total)
             zs = ext[(b + 1) * HALF : (b + 2) * HALF, cols].astype(F32)
-            out[b * HALF : (b + 1) * HALF, cols] = total + gain[:, cols] * zs
-
-
-def hidden_kernel(bpd, lengths, q, halo, taps, medium, out, buf):
-    me = stretch_id()
-    rows, width = medium.shape
-    buf[0:TAIL, :] = halo[...].astype(F32)
-    for k in range(rows // BLK):
-        buf[TAIL + k * BLK : TAIL + (k + 1) * BLK, :] = q[bpd[k, me]].astype(F32)
-    step = 32
-
-    def chunk(r, carry):
-        at = pl.multiple_of(r * step, step)
-        back = reach_back(lengths, me * rows + at, (step, width))
-        query = short_rows(buf[pl.ds(at, step + TAIL), :], taps, 0, back)
-        value = (query * medium[pl.ds(at, step), :]).astype(BF16)
-        for copy in range(out.shape[0]):
-            out[copy, pl.ds(at, step), :] = value
-        return carry
-
-    lax.fori_loop(0, rows // step, chunk, 0)
+            q = first_q[:, cols] if b == 0 else query[b * HALF : (b + 1) * HALF, cols]
+            value = (q * (total + gain[:, cols] * zs)).astype(BF16)
+            for copy in range(out.shape[0]):
+                out[copy, b * HALF : (b + 1) * HALF, cols] = value
+
+
+def relay_kernel(up, down, up_out, down_out):
+    up_out[...] = up[...]
+    down_out[...] = down[...]
 
 
 def project_kernel(offsets, own, other, *refs):
@@ -276,51 +285,49 @@
     rows = block_packing_device.shape[1] * BLK
     bpd = block_packing_device.T
 
-    kv_out, q_out = packed_blocks(bpd, source_rows.transpose(1, 0, 2), stretches)
-    kv_in = lax.all_to_all(kv_out, CTX, split_axis=0, concat_axis=0, tiled=True)
-    q_in = lax.all_to_all(q_out, CTX, split_axis=0, concat_axis=0, tiled=True)
+    packed = packed_blocks(bpd, source_rows.transpose(1, 0, 2), stretches)
+    blocks = lax.all_to_all(packed, CTX, split_axis=0, concat_axis=0, tiled=True)
+
     block = weight_columns(out_weight)
+    weights = [(0, block)]
+    up = down = block
+    for d in (1, 2, 3, 4):
+        up = around(up, 1)
+        down = around(down, -1) if d < 4 else None
+        if d == 3:
+            both = [shape(up.shape)] * 2
+            up, down = call(relay_kernel, both, [vmem()] * 2, (up, down), 0)
+        weights += [(d, up)] if down is None else [(d, up), (-d, down)]
 
     groups = medium_filters.shape[1]
     line = jnp.pad(medium_filters[::-1].T.astype(F32), ((0, 0), (1, HALF - 1)))
     (bands,) = call(toeplitz_kernel, [shape((groups, HALF, 2 * HALF))], [vmem()], (line,), 10**8)
-    weights = [(0, block)]
-    up = down = block
-    for d in (1, 2):
-        up, down = around(up, 1), around(down, -1)
-        weights += [(d, up), (-d, down)]
 
     z, send, head = call(
-        z_kernel,
-        [shape((rows, width)), shape((HALF + 2 * TAIL, width)), shape((2 * TAIL, width))],
+        gated_kernel,
+        [shape((rows, width)), shape((HALF + 3 * TAIL, width)), shape((3 * TAIL, width))],
         [smem(), smem(), vmem(), vmem()],
-        (bpd, doc_lengths, kv_in, short_filters),
+        (bpd, doc_lengths, blocks, short_filters),
         10**7,
         scratch=[pltpu.VMEM((2, rows + TAIL, width), F32)],
     )
     recv = passed_along(send)
-    (medium,) = call(
-        medium_kernel,
+    (query,) = call(
+        query_kernel,
         [shape((rows, width), F32)],
-        [smem()] + [vmem()] * 6,
-        (doc_lengths, z, recv, head, short_filters, bands, skip_gain.reshape(1, width)),
-        10**9,
-        scratch=[pltpu.VMEM((rows + HALF, width), BF16)],
+        [smem(), smem(), vmem(), vmem()],
+        (bpd, doc_lengths, blocks, short_filters),
+        10**7,
+        scratch=[pltpu.VMEM((rows + TAIL, width), F32)],
     )
-    medium, q_in = lax.optimization_barrier((medium, q_in))
-    up, down = around(up, 1), around(down, -1)
-    weights += [(3, up), (-3, down), (4, around(up, 1))]
-    mine = jnp.arange(stretches, dtype=jnp.int32) == stretch_id()
-    last = jnp.sum(jnp.where(mine, bpd[-1], 0))
-    q_tail = lax.dynamic_index_in_dim(q_in, last, 0, keepdims=False)[BLK - TAIL :]
-    q_halo = passed_along(q_tail)
+    gain = skip_gain.reshape(1, width)
     (copies,) = call(
         hidden_kernel,
         [shape((nx, rows, width))],
-        [smem(), smem()] + [vmem()] * 4,
-        (bpd, doc_lengths, q_in, q_halo, short_filters, medium),
-        10**7,
-        scratch=[pltpu.VMEM((rows + TAIL, width), F32)],
+        [smem()] + [vmem()] * 7,
+        (doc_lengths, z, query, recv, head, short_filters, bands, gain),
+        10**9,
+        scratch=[pltpu.VMEM((rows + HALF, width), BF16), pltpu.VMEM((HALF, width), F32)],
     )
     own = lax.all_to_all(copies, "x", split_axis=0, concat_axis=0, tiled=True)
     own = own.reshape(nx * rows, width)

time: 211 us -> 207 us (0.981)
  the two profiles are of different devices: /device:TPU:34 before, /device:TPU:2 now
where the time goes in v5:
time: 207 us; the launch traced here: 206 us
  blocking collectives  110 us (53%)
  starting transfers between devices  35.8 us (17%)
  waiting for transfers between devices  31.1 us (15%)
  Pallas kernels  24.7 us (12%)
  local copies, waits for them, and re-layouts  2.52 us (1%)
    all_to_all x1, blocking collectives, operator(): lax.all_to_all(flat, ('z', 'x'), split_axis=0, concat_axis=0, tiled=True)  60.2 us
    all_to_all x1, blocking collectives, operator(): lax.all_to_all(packed, CTX, split_axis=0, concat_axis=0, tiled=True)  49.7 us
    ppermute x7, waiting for transfers between devices, around(): return lax.ppermute(block, 'y', [(i, (i + distance) % n) for i in range(n)])  24.3 us
    ppermute x7, starting transfers between devices, around(): return lax.ppermute(block, 'y', [(i, (i + distance) % n) for i in range(n)])  19.3 us
    pallas_call x5, Pallas kernels, call(): pl.pallas_call(body, out_shape=outs, in_specs=ins, out_specs=[vmem()] * l...  16.3 us
    ppermute x1, waiting for transfers between devices, weight_columns(): a = lax.ppermute(same, ('x', 'core'), route(lambda i: i))  5.92 us
    pallas_call x1, Pallas kernels, project(): pl.pallas_call(functools.partial(project_kernel, offsets), grid=(nx // tw...  5.51 us
    all_to_all x1, starting transfers between devices, operator(): own = lax.all_to_all(copies, 'x', split_axis=0, concat_axis=0, tiled=True)  4.93 us
  transfers between devices with their start and end apart: 12, of which 9 were waited for; matrix products, arithmetic and copies ran while one was open for 0% of the time, Pallas kernels for 4%

profile of v5, /device:TPU:2, one launch (start us, length us, event | category | flops | bytes accessed | tf_op | source)
XLA Modules:
  0.0 206.0 jit_solution(17177832199605035176)
XLA Ops:
  0.0 2.9 %pack.1 = bf16[32,3,16,512]{3,2,1,0:T(8,128)(2,1)} custom-call(s32[16,32]{1,0:T(8,128)} %bitcast.12, bf16[3,512,512]{2,1,0:T(8,128)(2,1)} %bitcast.9), custom_call_target="tpu_custom_call" | custom-call | flops 1000000 | bytes 3145728 | tf_op jit(solution)/shard_map/pack/pallas_call | solution.py:80
  2.9 0.0 copy-start.6
  2.9 49.7 %all_to_all.15.blocks = bf16[32,3,16,512]{3,2,1,0:T(8,128)(2,1)} all-to-all(bf16[32,3,16,512]{3,2,1,0:T(8,128)(2,1)} %pack.1), channel_id=1, replica_groups=mesh['y'=8,'x'=4,'z'=8,'core'=2] {'y','x'}, dimensions={0} | all-to-all | bytes 3145728 | tf_op jit(solution)/shard_map/all_to_all | solution.py:289
  52.6 3.9 %shard_map.73 = (bf16[256,512]{1,0:T(8,128)(2,1)}, bf16[152,512]{1,0:T(8,128)(2,1)}, bf16[24,512]{1,0:T(8,128)(2,1)}) custom-call(s32[16,32]{1,0:T(8,128)} %bitcast.13, s32[8]{0:T(128)} %lengths.5, bf16[32,3,16,512]{3,2,1,0:T(8,128)(2,1)} %all_to_all.15.blocks, bf16[3,7,512]{2,1,0:T(8,128)(2,1)} %taps.5), custom_call_target="tpu_custom_call" | custom-call | flops 10000000 | bytes 2038816 | tf_op jit(solution)/shard_map/pallas_call | solution.py:34
  56.5 3.4 %collective-permute-start = (bf16[152,512]{1,0:T(8,128)(2,1)}, bf16[152,512]{1,0:T(8,128)(2,1)S(1)}, u32[]{:S(2)}, u32[]{:S(2)}) collective-permute-start(bf16[152,512]{1,0:T(8,128)(2,1)} %get-tuple-element.11), channel_id=1, source_target_pairs={{0,16},{16,32},{32,48},{48,64},{64,80},{80,96},{96,112},{112,128},... | collective-permute-start | bytes 466952 | tf_op jit(solution)/shard_map/ppermute | solution.py:247
  59.9 0.0 copy-done.6
  59.9 0.1 rev.3
  59.9 0.7 pad_convert_fusion.line
  60.6 3.2 %shard_map.75.bands = bf16[32,128,256]{2,1,0:T(8,128)(2,1)} custom-call(f32[32,256]{1,0:T(8,128)} %pad_convert_fusion.line), custom_call_target="tpu_custom_call" | custom-call | flops 100000000 | bytes 2129920 | tf_op jit(solution)/shard_map/pallas_call | solution.py:34
  63.8 3.1 %shard_map.74.query = f32[256,512]{1,0:T(8,128)} custom-call(s32[16,32]{1,0:T(8,128)} %bitcast.14, s32[8]{0:T(128)} %lengths.5, bf16[32,3,16,512]{3,2,1,0:T(8,128)(2,1)} %all_to_all.15.blocks, bf16[3,7,512]{2,1,0:T(8,128)(2,1)} %taps.5), custom_call_target="tpu_custom_call" | custom-call | flops 10000000 | bytes 2120736 | tf_op jit(solution)/shard_map/pallas_call | solution.py:34
  67.0 0.0 collective-permute-done.recv
  67.0 0.7 copy-done.5
  67.6 4.2 %shard_map.76 = bf16[4,256,512]{2,1,0:T(8,128)(2,1)} custom-call(s32[8]{0:T(128)} %lengths.5, bf16[256,512]{1,0:T(8,128)(2,1)} %get-tuple-element.10.z, f32[256,512]{1,0:T(8,128)} %shard_map.74.query, bf16[152,512]{1,0:T(8,128)(2,1)} %copy-done.5, bf16[24,512]{1,0:T(8,128)(2,1)} %get-tuple-element.12.head, bf16[3,7,512]{2,1,0:T(8,128)(2,1)} %taps.5, ...), custom_call_target="tpu_custom_call" | custom-call | flops 1000000000 | bytes 4135968 | tf_op jit(solution)/shard_map/pallas_call | solution.py:34
  71.8 4.9 %all-to-all-start.1 = ((bf16[4,256,512]{2,1,0:T(8,128)(2,1)}), bf16[4,256,512]{2,1,0:T(8,128)(2,1)S(1)}, u32[]{:S(2)}, u32[]{:S(2)}) async-start(bf16[4,256,512]{2,1,0:T(8,128)(2,1)} %shard_map.76), calls=%async_computation.1 | async-start | bytes 2097152 | tf_op jit(solution)/shard_map/all_to_all | solution.py:332
  76.7 0.0 copy-done.1
  76.8 3.4 %collective-permute-start.2 = (bf16[512,128]{1,0:T(8,128)(2,1)S(1)}, bf16[512,128]{1,0:T(8,128)(2,1)S(1)}, u32[]{:S(2)}, u32[]{:S(2)}) collective-permute-start(bf16[512,128]{1,0:T(8,128)(2,1)S(1)} %get-tuple-element.21), channel_id=1, source_target_pairs={{0,0},{1,16},{16,32},{17,48},{32,1},{33,17},{48,33},{49,49},{2,2},... | collective-permute-start | bytes 393224 | tf_op jit(solution)/shard_map/ppermute | solution.py:260
  80.1 2.5 %collective-permute-start.3 = (bf16[512,128]{1,0:T(8,128)(2,1)S(1)}, bf16[512,128]{1,0:T(8,128)(2,1)S(1)}, u32[]{:S(2)}, u32[]{:S(2)}) collective-permute-start(bf16[512,128]{1,0:T(8,128)(2,1)S(1)} %get-tuple-element.22), channel_id=1, source_target_pairs={{0,16},{1,0},{16,48},{17,32},{32,17},{33,1},{48,49},{49,33},{2,18}... | collective-permute-start | bytes 393224 | tf_op jit(solution)/shard_map/ppermute | solution.py:261
  82.7 5.9 %collective-permute-done.2 = bf16[512,128]{1,0:T(8,128)(2,1)S(1)} collective-permute-done((bf16[512,128]{1,0:T(8,128)(2,1)S(1)}, bf16[512,128]{1,0:T(8,128)(2,1)S(1)}, u32[]{:S(2)}, u32[]{:S(2)}) %collective-permute-start.2) | collective-permute-done | bytes 131104 | tf_op jit(solution)/shard_map/ppermute | solution.py:260
  88.6 0.8 collective-permute-done.3
  89.5 0.0 copy-start.2
  89.5 1.9 collective-permute-start.5
  91.5 3.9 %collective-permute-start.4 = (bf16[1024,128]{1,0:T(8,128)(2,1)S(1)}, bf16[1024,128]{1,0:T(8,128)(2,1)S(1)}, u32[]{:S(2)}, u32[]{:S(2)}) collective-permute-start(bf16[1024,128]{1,0:T(8,128)(2,1)S(1)} %pad_maximum_fusion.refs_0_), channel_id=1, source_target_pairs={{0,64},{64,128},{128,192},{192,256},{256,320},{320,384},{384,448},... | collective-permute-start | bytes 786440 | tf_op jit(solution)/shard_map/ppermute | solution.py:270
  95.4 0.0 all-to-all-done.1
  95.4 2.3 %collective-permute-start.1 = (bf16[1024,512]{1,0:T(8,128)(2,1)S(1)}, bf16[1024,512]{1,0:T(8,128)(2,1)S(1)}, u32[]{:S(2)}, u32[]{:S(2)}) collective-permute-start(bf16[1024,512]{1,0:T(8,128)(2,1)S(1)} %bitcast.10), channel_id=1, source_target_pairs={{0,1},{1,0},{2,3},{3,2},{4,5},{5,4},{6,7},{7,6},{8,9},{9,8},{10,11... | collective-permute-start | bytes 3145736 | tf_op jit(solution)/shard_map/ppermute | solution.py:334
  97.7 2.9 %collective-permute-done.5.refs_2_ = bf16[1024,128]{1,0:T(8,128)(2,1)S(1)} collective-permute-done((bf16[1024,128]{1,0:T(8,128)(2,1)S(1)}, bf16[1024,128]{1,0:T(8,128)(2,1)S(1)}, u32[]{:S(2)}, u32[]{:S(2)}) %collective-permute-start.5) | collective-permute-done | bytes 262176 | tf_op jit(solution)/shard_map/ppermute | solution.py:270
  100.6 2.9 %collective-permute-start.7 = (bf16[1024,128]{1,0:T(8,128)(2,1)S(1)}, bf16[1024,128]{1,0:T(8,128)(2,1)S(1)}, u32[]{:S(2)}, u32[]{:S(2)}) collective-permute-start(bf16[1024,128]{1,0:T(8,128)(2,1)S(1)} %collective-permute-done.5.refs_2_), channel_id=1, source_target_pairs={{0,448},{64,0},{128,64},{192,128},{256,192},{320,256},{384,320},{4... | collective-permute-start | bytes 786440 | tf_op jit(solution)/shard_map/ppermute | solution.py:270
  103.5 0.3 collective-permute-done.4.refs_1_
  103.7 2.7 %collective-permute-start.6 = (bf16[1024,128]{1,0:T(8,128)(2,1)S(1)}, bf16[1024,128]{1,0:T(8,128)(2,1)S(1)}, u32[]{:S(2)}, u32[]{:S(2)}) collective-permute-start(bf16[1024,128]{1,0:T(8,128)(2,1)S(1)} %collective-permute-done.4.refs_1_), channel_id=1, source_target_pairs={{0,64},{64,128},{128,192},{192,256},{256,320},{320,384},{384,448},... | collective-permute-start | bytes 786440 | tf_op jit(solution)/shard_map/ppermute | solution.py:270
  106.5 4.3 %collective-permute-done.7.refs_4_ = bf16[1024,128]{1,0:T(8,128)(2,1)S(1)} collective-permute-done((bf16[1024,128]{1,0:T(8,128)(2,1)S(1)}, bf16[1024,128]{1,0:T(8,128)(2,1)S(1)}, u32[]{:S(2)}, u32[]{:S(2)}) %collective-permute-start.7) | collective-permute-done | bytes 262176 | tf_op jit(solution)/shard_map/ppermute | solution.py:270
  110.8 4.1 %collective-permute-start.9 = (bf16[1024,128]{1,0:T(8,128)(2,1)S(1)}, bf16[1024,128]{1,0:T(8,128)(2,1)S(1)}, u32[]{:S(2)}, u32[]{:S(2)}) collective-permute-start(bf16[1024,128]{1,0:T(8,128)(2,1)S(1)} %collective-permute-done.7.refs_4_), channel_id=1, source_target_pairs={{0,448},{64,0},{128,64},{192,128},{256,192},{320,256},{384,320},{4... | collective-permute-start | bytes 786440 | tf_op jit(solution)/shard_map/ppermute | solution.py:270
  114.9 0.2 collective-permute-done.6.refs_3_
  115.1 1.9 collective-permute-start.8
  117.1 3.1 %collective-permute-done.9.down = bf16[1024,128]{1,0:T(8,128)(2,1)S(1)} collective-permute-done((bf16[1024,128]{1,0:T(8,128)(2,1)S(1)}, bf16[1024,128]{1,0:T(8,128)(2,1)S(1)}, u32[]{:S(2)}, u32[]{:S(2)}) %collective-permute-start.9) | collective-permute-done | bytes 262176 | tf_op jit(solution)/shard_map/ppermute | solution.py:270
  120.1 0.0 copy-done.10
  120.1 5.6 %collective-permute-done.8.up = bf16[1024,128]{1,0:T(8,128)(2,1)S(1)} collective-permute-done((bf16[1024,128]{1,0:T(8,128)(2,1)S(1)}, bf16[1024,128]{1,0:T(8,128)(2,1)S(1)}, u32[]{:S(2)}, u32[]{:S(2)}) %collective-permute-start.8) | collective-permute-done | bytes 262176 | tf_op jit(solution)/shard_map/ppermute | solution.py:270
  125.7 0.0 copy-done.3
  125.7 0.7 copy-done.4
  126.4 1.9 shard_map.77
  128.3 1.9 collective-permute-start.10
  130.2 8.0 %collective-permute-done.10.refs_7_ = bf16[1024,128]{1,0:T(8,128)(2,1)S(1)} collective-permute-done((bf16[1024,128]{1,0:T(8,128)(2,1)}, bf16[1024,128]{1,0:T(8,128)(2,1)S(1)}, u32[]{:S(2)}, u32[]{:S(2)}) %collective-permute-start.10) | collective-permute-done | bytes 262176 | tf_op jit(solution)/shard_map/ppermute | solution.py:270
  138.2 0.0 collective-permute-done.1.other
  138.2 0.0 copy-done.2
  138.2 0.7 copy-done.12
  138.9 0.4 copy-done.7
  139.3 5.5 %project.1 = bf16[8,4,256,128]{3,2,1,0:T(8,128)(2,1)} custom-call(bf16[1024,512]{1,0:T(8,128)(2,1)} %bitcast.11, bf16[1024,512]{1,0:T(8,128)(2,1)} %copy-done.7, bf16[1024,128]{1,0:T(8,128)(2,1)} %copy-done.2, bf16[1024,128]{1,0:T(8,128)(2,1)} %copy-done.9, bf16[1024,128]{1,0:T(8,128)(2,1)} %copy-done.8, bf16[1024,128]{1,0:T(8,128)(2,1)} %copy-done.11, ...), custom_call_target="tpu_custom_call" | custom-call | flops 2147483648 | bytes 8388608 | tf_op jit(solution)/shard_map/project/pallas_call | solution.py:219
  144.8 60.2 %all_to_all.16 = bf16[32,256,128]{2,1,0:T(8,128)(2,1)S(1)} all-to-all(bf16[32,256,128]{2,1,0:T(8,128)(2,1)} %bitcast.8), channel_id=1, replica_groups=mesh['y'=8,'x'=4,'z'=8,'core'=2] {'z','x'}, dimensions={0} | all-to-all | bytes 4194304 | tf_op jit(solution)/shard_map/all_to_all | solution.py:337
  204.9 0.3 slice_reduce_fusion.3
  205.2 0.7 pad_maximum_fusion.1
  (18 shorter events, 0.1 us)
Async XLA Ops:
  2.9 56.9 %copy-start.6 = (bf16[128,32]{0,1:T(8,128)(2,1)S(1)}, bf16[128,32]{0,1:T(8,128)(2,1)}, u32[]{:S(2)}) copy-start(bf16[128,32]{0,1:T(8,128)(2,1)} %param.9) | copy-start | bytes 24580
  56.5 10.5 %collective-permute-start = (bf16[152,512]{1,0:T(8,128)(2,1)}, bf16[152,512]{1,0:T(8,128)(2,1)S(1)}, u32[]{:S(2)}, u32[]{:S(2)}) collective-permute-start(bf16[152,512]{1,0:T(8,128)(2,1)} %get-tuple-element.11), channel_id=1, source_target_pairs={{0,16},{16,32},{32,48},{48,64},{64,80},{80,96},{96,112},{112,128},... | collective-permute-start | bytes 466952 | tf_op jit(solution)/shard_map/ppermute | solution.py:247
  67.0 0.7 copy-start.5
  67.6 9.1 %copy-start.1 = (bf16[512,256]{1,0:T(8,128)(2,1)S(1)}, bf16[512,256]{1,0:T(8,128)(2,1)}, u32[]{:S(2)}) copy-start(bf16[512,256]{1,0:T(8,128)(2,1)} %param.11) | copy-start | bytes 786436
  71.8 23.6 %all-to-all-start.1 = ((bf16[4,256,512]{2,1,0:T(8,128)(2,1)}), bf16[4,256,512]{2,1,0:T(8,128)(2,1)S(1)}, u32[]{:S(2)}, u32[]{:S(2)}) async-start(bf16[4,256,512]{2,1,0:T(8,128)(2,1)} %shard_map.76), calls=%async_computation.1 | async-start | bytes 2097152 | tf_op jit(solution)/shard_map/all_to_all | solution.py:332
  76.8 11.8 %collective-permute-start.2 = (bf16[512,128]{1,0:T(8,128)(2,1)S(1)}, bf16[512,128]{1,0:T(8,128)(2,1)S(1)}, u32[]{:S(2)}, u32[]{:S(2)}) collective-permute-start(bf16[512,128]{1,0:T(8,128)(2,1)S(1)} %get-tuple-element.21), channel_id=1, source_target_pairs={{0,0},{1,16},{16,32},{17,48},{32,1},{33,17},{48,33},{49,49},{2,2},... | collective-permute-start | bytes 393224 | tf_op jit(solution)/shard_map/ppermute | solution.py:260
  80.1 9.3 %collective-permute-start.3 = (bf16[512,128]{1,0:T(8,128)(2,1)S(1)}, bf16[512,128]{1,0:T(8,128)(2,1)S(1)}, u32[]{:S(2)}, u32[]{:S(2)}) collective-permute-start(bf16[512,128]{1,0:T(8,128)(2,1)S(1)} %get-tuple-element.22), channel_id=1, source_target_pairs={{0,16},{1,0},{16,48},{17,32},{32,17},{33,1},{48,49},{49,33},{2,18}... | collective-permute-start | bytes 393224 | tf_op jit(solution)/shard_map/ppermute | solution.py:261
  89.5 48.7 %copy-start.2 = (bf16[1024,128]{1,0:T(8,128)(2,1)}, bf16[1024,128]{1,0:T(8,128)(2,1)S(1)}, u32[]{:S(2)}) copy-start(bf16[1024,128]{1,0:T(8,128)(2,1)S(1)} %pad_maximum_fusion.refs_0_) | copy-start | bytes 786436
  89.5 11.1 %collective-permute-start.5 = (bf16[1024,128]{1,0:T(8,128)(2,1)S(1)}, bf16[1024,128]{1,0:T(8,128)(2,1)S(1)}, u32[]{:S(2)}, u32[]{:S(2)}) collective-permute-start(bf16[1024,128]{1,0:T(8,128)(2,1)S(1)} %pad_maximum_fusion.refs_0_), channel_id=1, source_target_pairs={{0,448},{64,0},{128,64},{192,128},{256,192},{320,256},{384,320},{4... | collective-permute-start | bytes 786440 | tf_op jit(solution)/shard_map/ppermute | solution.py:270
  91.5 12.3 %collective-permute-start.4 = (bf16[1024,128]{1,0:T(8,128)(2,1)S(1)}, bf16[1024,128]{1,0:T(8,128)(2,1)S(1)}, u32[]{:S(2)}, u32[]{:S(2)}) collective-permute-start(bf16[1024,128]{1,0:T(8,128)(2,1)S(1)} %pad_maximum_fusion.refs_0_), channel_id=1, source_target_pairs={{0,64},{64,128},{128,192},{192,256},{256,320},{320,384},{384,448},... | collective-permute-start | bytes 786440 | tf_op jit(solution)/shard_map/ppermute | solution.py:270
  95.4 42.8 %copy-start = (bf16[4,256,512]{2,1,0:T(8,128)(2,1)}, bf16[4,256,512]{2,1,0:T(8,128)(2,1)S(1)}, u32[]{:S(2)}) copy-start(bf16[4,256,512]{2,1,0:T(8,128)(2,1)S(1)} %all-to-all-done.1) | copy-start | bytes 3145732
  95.4 42.8 %collective-permute-start.1 = (bf16[1024,512]{1,0:T(8,128)(2,1)S(1)}, bf16[1024,512]{1,0:T(8,128)(2,1)S(1)}, u32[]{:S(2)}, u32[]{:S(2)}) collective-permute-start(bf16[1024,512]{1,0:T(8,128)(2,1)S(1)} %bitcast.10), channel_id=1, source_target_pairs={{0,1},{1,0},{2,3},{3,2},{4,5},{5,4},{6,7},{7,6},{8,9},{9,8},{10,11... | collective-permute-start | bytes 3145736 | tf_op jit(solution)/shard_map/ppermute | solution.py:334
  100.6 37.6 %copy-start.8 = (bf16[1024,128]{1,0:T(8,128)(2,1)}, bf16[1024,128]{1,0:T(8,128)(2,1)S(1)}, u32[]{:S(2)}) copy-start(bf16[1024,128]{1,0:T(8,128)(2,1)S(1)} %collective-permute-done.5.refs_2_) | copy-start | bytes 786436
  100.6 10.2 %collective-permute-start.7 = (bf16[1024,128]{1,0:T(8,128)(2,1)S(1)}, bf16[1024,128]{1,0:T(8,128)(2,1)S(1)}, u32[]{:S(2)}, u32[]{:S(2)}) collective-permute-start(bf16[1024,128]{1,0:T(8,128)(2,1)S(1)} %collective-permute-done.5.refs_2_), channel_id=1, source_target_pairs={{0,448},{64,0},{128,64},{192,128},{256,192},{320,256},{384,320},{4... | collective-permute-start | bytes 786440 | tf_op jit(solution)/shard_map/ppermute | solution.py:270
  103.7 34.5 %copy-start.9 = (bf16[1024,128]{1,0:T(8,128)(2,1)}, bf16[1024,128]{1,0:T(8,128)(2,1)S(1)}, u32[]{:S(2)}) copy-start(bf16[1024,128]{1,0:T(8,128)(2,1)S(1)} %collective-permute-done.4.refs_1_) | copy-start | bytes 786436
  103.7 11.4 %collective-permute-start.6 = (bf16[1024,128]{1,0:T(8,128)(2,1)S(1)}, bf16[1024,128]{1,0:T(8,128)(2,1)S(1)}, u32[]{:S(2)}, u32[]{:S(2)}) collective-permute-start(bf16[1024,128]{1,0:T(8,128)(2,1)S(1)} %collective-permute-done.4.refs_1_), channel_id=1, source_target_pairs={{0,64},{64,128},{128,192},{192,256},{256,320},{320,384},{384,448},... | collective-permute-start | bytes 786440 | tf_op jit(solution)/shard_map/ppermute | solution.py:270
  110.8 9.3 %copy-start.10 = (bf16[1024,128]{1,0:T(8,128)(2,1)}, bf16[1024,128]{1,0:T(8,128)(2,1)S(1)}, u32[]{:S(2)}) copy-start(bf16[1024,128]{1,0:T(8,128)(2,1)S(1)} %collective-permute-done.7.refs_4_) | copy-start | bytes 786436
  110.8 9.3 %collective-permute-start.9 = (bf16[1024,128]{1,0:T(8,128)(2,1)S(1)}, bf16[1024,128]{1,0:T(8,128)(2,1)S(1)}, u32[]{:S(2)}, u32[]{:S(2)}) collective-permute-start(bf16[1024,128]{1,0:T(8,128)(2,1)S(1)} %collective-permute-done.7.refs_4_), channel_id=1, source_target_pairs={{0,448},{64,0},{128,64},{192,128},{256,192},{320,256},{384,320},{4... | collective-permute-start | bytes 786440 | tf_op jit(solution)/shard_map/ppermute | solution.py:270
  115.1 5.0 %copy-start.11 = (bf16[1024,128]{1,0:T(8,128)(2,1)}, bf16[1024,128]{1,0:T(8,128)(2,1)S(1)}, u32[]{:S(2)}) copy-start(bf16[1024,128]{1,0:T(8,128)(2,1)S(1)} %collective-permute-done.6.refs_3_) | copy-start | bytes 786436
  115.1 10.5 %collective-permute-start.8 = (bf16[1024,128]{1,0:T(8,128)(2,1)S(1)}, bf16[1024,128]{1,0:T(8,128)(2,1)S(1)}, u32[]{:S(2)}, u32[]{:S(2)}) collective-permute-start(bf16[1024,128]{1,0:T(8,128)(2,1)S(1)} %collective-permute-done.6.refs_3_), channel_id=1, source_target_pairs={{0,64},{64,128},{128,192},{192,256},{256,320},{320,384},{384,448},... | collective-permute-start | bytes 786440 | tf_op jit(solution)/shard_map/ppermute | solution.py:270
  120.1 5.6 %copy-start.3 = (bf16[1024,128]{1,0:T(8,128)(2,1)}, bf16[1024,128]{1,0:T(8,128)(2,1)S(1)}, u32[]{:S(2)}) copy-start(bf16[1024,128]{1,0:T(8,128)(2,1)S(1)} %collective-permute-done.9.down) | copy-start | bytes 786436
  125.7 0.7 copy-start.4
  128.3 9.9 %collective-permute-start.10 = (bf16[1024,128]{1,0:T(8,128)(2,1)}, bf16[1024,128]{1,0:T(8,128)(2,1)S(1)}, u32[]{:S(2)}, u32[]{:S(2)}) collective-permute-start(bf16[1024,128]{1,0:T(8,128)(2,1)} %get-tuple-element.13.refs_5_), channel_id=1, source_target_pairs={{0,64},{64,128},{128,192},{192,256},{256,320},{320,384},{384,448},... | collective-permute-start | bytes 786440 | tf_op jit(solution)/shard_map/ppermute | solution.py:270
  138.2 0.7 copy-start.12
  138.2 1.1 copy-start.7

commit v6 on v5

--- a/solution.py
+++ b/solution.py
@@ -9,9 +9,10 @@
 
 
 CTX = ("y", "x")
-SHAPE4 = (8, 4, 8, 2)
+SHAPE5 = (8, 4, 4, 2, 2)
 BLK = 16
 TAIL = 8
+GRANT = 24 << 20
 HALF = 128
 F32, BF16 = jnp.float32, jnp.bfloat16
 
@@ -37,6 +38,7 @@
         in_specs=ins,
         out_specs=[vmem()] * len(outs),
         scratch_shapes=list(scratch),
+        compiler_params=pltpu.CompilerParams(vmem_limit_bytes=GRANT),
         cost_estimate=pl.CostEstimate(flops=flops, bytes_accessed=moved, transcendentals=0),
     )(*args)
 
@@ -86,6 +88,7 @@
         cost_estimate=pl.CostEstimate(
             flops=10**6, bytes_accessed=4 * src.size, transcendentals=0
         ),
+        compiler_params=pltpu.CompilerParams(vmem_limit_bytes=GRANT),
         name="pack",
     )(bpd, src)
 
@@ -192,45 +195,60 @@
     down_out[...] = down[...]
 
 
-def project_kernel(offsets, own, other, *refs):
-    weights, out = refs[:-1], refs[-1]
-    lane = out.shape[3]
-    n = out.shape[0]
+def project_kernel(offsets, part, own, other, *refs):
+    weights, (same, cross) = refs[:-2], refs[-2:]
+    count, rows, lane = same.shape[1:]
+    n = len(weights)
     y = lax.axis_index("y")
-    left = jnp.concatenate([own[...], other[...]], axis=1)
+    at = slice(part * count * rows, (part + 1) * count * rows)
+    left = jnp.concatenate([own[at, :], other[at, :]], axis=1)
     for pair in range(0, n, 2):
         wide = jnp.concatenate([weights[pair][...], weights[pair + 1][...]], axis=1)
         got = jnp.dot(left, wide, preferred_element_type=F32).astype(BF16)
         for i in range(2):
-            at = lax.rem(y - offsets[pair + i] + n, n)
-            for s in range(out.shape[1]):
-                piece = got[s * out.shape[2] : (s + 1) * out.shape[2]]
-                out[at, s] = piece[:, i * lane : (i + 1) * lane]
-
-
-def project(own, other, weights, nx):
-    offsets = tuple(w[0] for w in weights)
+            owner = lax.rem(y - offsets[pair + i] + n, n)
+            high = lax.div(owner, 2)
+            odd = lax.rem(owner + lax.axis_index("zl"), 2)
+            piece = got[:, i * lane : (i + 1) * lane].reshape(count, rows, lane)
+
+            @pl.when(odd == 0)
+            def _():
+                same[high] = piece
+
+            @pl.when(odd == 1)
+            def _():
+                cross[high] = piece
+
+
+def project(part, own, other, weights, nx):
+    rows = own.shape[0] // nx
     blocks = [w[1] for w in weights]
-    n = len(blocks)
-    rows = own.shape[0] // nx
-    two = 2
-    k = own.shape[1]
     lane = blocks[0].shape[1]
-    return pl.pallas_call(
-        functools.partial(project_kernel, offsets),
-        grid=(nx // two,),
-        in_specs=[
-            pl.BlockSpec((two * rows, k), lambda i: (i, 0)),
-            pl.BlockSpec((two * rows, k), lambda i: (i, 0)),
-        ]
-        + [pl.BlockSpec((2 * k, lane), lambda i: (0, 0)) for _ in blocks],
-        out_specs=pl.BlockSpec((n, two, rows, lane), lambda i: (0, i, 0, 0)),
-        out_shape=shape((n, nx, rows, lane)),
-        cost_estimate=pl.CostEstimate(
-            flops=4 * nx * rows * k * n * lane, bytes_accessed=8 << 20, transcendentals=0
-        ),
-        name="project",
-    )(own, other, *blocks)
+    return call(
+        functools.partial(project_kernel, tuple(w[0] for w in weights), part),
+        [shape((len(blocks) // 2, nx // 2, rows, lane))] * 2,
+        [vmem()] * (2 + len(blocks)),
+        (own, other, *blocks),
+        2 * own.size * len(blocks) * lane,
+    )
+
+
+def pair_kernel(own0, own1, got0, got1, out):
+    count = own0.shape[1]
+
+    def one(z, carry):
+        for i, (own, got) in enumerate(((own0, got0), (own1, got1))):
+            for s in range(count):
+                total = own[z, s].astype(F32) + got[z, s].astype(F32)
+                out[z, i * count + s] = total.astype(BF16)
+        return carry
+
+    lax.fori_loop(0, own0.shape[0], one, 0)
+
+
+def along_z(block, distance):
+    n = lax.axis_size(("zh", "zl"))
+    return lax.ppermute(block, ("zh", "zl"), [(i, (i + distance) % n) for i in range(n)])
 
 
 def summed(parts):
@@ -279,7 +297,7 @@
     doc_lengths,
     block_packing_device,
 ):
-    ny, nx, nz = lax.axis_size("y"), lax.axis_size("x"), lax.axis_size("z")
+    ny, nx = lax.axis_size("y"), lax.axis_size("x")
     stretches = ny * nx
     width = source_rows.shape[2]
     rows = block_packing_device.shape[1] * BLK
@@ -332,18 +350,24 @@
     own = lax.all_to_all(copies, "x", split_axis=0, concat_axis=0, tiled=True)
     own = own.reshape(nx * rows, width)
     other = lax.ppermute(own, "core", [(0, 1), (1, 0)])
-    partial = project(own, other, weights, nx)
-    flat = partial.reshape(nz * nx, rows, partial.shape[3])
-    parts = lax.all_to_all(flat, ("z", "x"), split_axis=0, concat_axis=0, tiled=True)
-    return summed(parts.reshape(partial.shape))
+    mine, got = [], []
+    for part, distance in ((0, 1), (1, -1)):
+        same, cross = project(part, own, other, weights, nx)
+        mine.append(same)
+        got.append(along_z(cross, distance))
+    nzh, _, _, lane = mine[0].shape
+    (pairs,) = call(pair_kernel, [shape((nzh, nx, rows, lane))], [vmem()] * 4, (*mine, *got), 10**6)
+    flat = pairs.reshape(nzh * nx, rows, lane)
+    parts = lax.all_to_all(flat, ("zh", "x"), split_axis=0, concat_axis=0, tiled=True)
+    return summed(parts.reshape(pairs.shape))
 
 
 def solution(mesh):
-    ctx, mp = CTX, ("z", "core")
-    mesh4 = Mesh(mesh.devices.reshape(SHAPE4), ctx + mp)
+    ctx, mp = CTX, ("zh", "zl", "core")
+    mesh5 = Mesh(mesh.devices.reshape(SHAPE5), ctx + mp)
     return jax.shard_map(
         operator,
-        mesh=mesh4,
+        mesh=mesh5,
         in_specs=(
             P(ctx, None, mp),
             P(None, None, mp),

time: 207 us -> 192 us (0.928)
  the two profiles are of different devices: /device:TPU:2 before, /device:TPU:24 now
where the time goes in v6:
time: 192 us; the launch traced here: 191 us
  blocking collectives  76.9 us (40%)
  starting transfers between devices  54.6 us (28%)
  waiting for transfers between devices  39.8 us (21%)
  Pallas kernels  16.3 us (8%)
  local copies, waits for them, and re-layouts  2.22 us (1%)
    all_to_all x1, blocking collectives, operator(): lax.all_to_all(packed, CTX, split_axis=0, concat_axis=0, tiled=True)  48.3 us
    all_to_all x1, blocking collectives, operator(): lax.all_to_all(flat, ('zh', 'x'), split_axis=0, concat_axis=0, tiled=True)  28.6 us
    ppermute x7, starting transfers between devices, around(): return lax.ppermute(block, 'y', [(i, (i + distance) % n) for i in range(n)])  23.5 us
    ppermute x7, waiting for transfers between devices, around(): return lax.ppermute(block, 'y', [(i, (i + distance) % n) for i in range(n)])  19.3 us
    pallas_call x8, Pallas kernels, call(): pl.pallas_call(body, out_shape=outs, in_specs=ins, out_specs=[vmem()] * l...  14.1 us
    ppermute x2, starting transfers between devices, along_z(): lax.ppermute(block, ('zh', 'zl'), [(i, (i + distance) % n) for i in range...  12.9 us
    ppermute x2, waiting for transfers between devices, along_z(): lax.ppermute(block, ('zh', 'zl'), [(i, (i + distance) % n) for i in range...  12.3 us
    ppermute x1, starting transfers between devices, weight_columns(): b = lax.ppermute(flip, ('x', 'core'), route(lambda i: 1 - i))  6.58 us
  transfers between devices with their start and end apart: 14, of which 8 were waited for; matrix products, arithmetic and copies ran while one was open for 0% of the time, Pallas kernels for 3%

profile of v6, /device:TPU:24, one launch (start us, length us, event | category | flops | bytes accessed | tf_op | source)
XLA Modules:
  0.0 191.1 jit_solution(7751685042895147808)
XLA Ops:
  0.0 1.4 copy-done
  1.4 0.7 copy-done.2
  2.1 2.2 %pack.1 = bf16[32,3,16,512]{3,2,1,0:T(8,128)(2,1)S(1)} custom-call(s32[16,32]{1,0:T(8,128)S(1)} %bitcast.12, bf16[3,512,512]{2,1,0:T(8,128)(2,1)S(1)} %bitcast.11), custom_call_target="tpu_custom_call" | custom-call | flops 1000000 | bytes 3145728 | tf_op jit(solution)/shard_map/pack/pallas_call | solution.py:82
  4.3 0.0 copy-start.1
  4.3 0.0 copy-start.4
  4.3 48.3 %all_to_all.15.blocks = bf16[32,3,16,512]{3,2,1,0:T(8,128)(2,1)S(1)} all-to-all(bf16[32,3,16,512]{3,2,1,0:T(8,128)(2,1)S(1)} %pack.1), channel_id=1, replica_groups=mesh['y'=8,'x'=4,'zh'=4,'zl'=2,'core'=2] {'y','x'}, dimensions={0} | all-to-all | bytes 3145728 | tf_op jit(solution)/shard_map/all_to_all | solution.py:307
  52.6 0.0 copy-done.1
  52.6 2.4 %shard_map.73 = (bf16[256,512]{1,0:T(8,128)(2,1)S(1)}, bf16[152,512]{1,0:T(8,128)(2,1)S(1)}, bf16[24,512]{1,0:T(8,128)(2,1)S(1)}) custom-call(s32[16,32]{1,0:T(8,128)S(1)} %bitcast.13, s32[8]{0:T(128)S(1)} %copy-done.4, bf16[32,3,16,512]{3,2,1,0:T(8,128)(2,1)S(1)} %all_to_all.15.blocks, bf16[3,7,512]{2,1,0:T(8,128)(2,1)S(1)} %copy-done.1), custom_call_target="tpu_custom_call" | custom-call | flops 10000000 | bytes 2038816 | tf_op jit(solution)/shard_map/pallas_call | solution.py:35
  55.1 2.2 %collective-permute-start = (bf16[152,512]{1,0:T(8,128)(2,1)S(1)}, bf16[152,512]{1,0:T(8,128)(2,1)S(1)}, u32[]{:S(2)}, u32[]{:S(2)}) collective-permute-start(bf16[152,512]{1,0:T(8,128)(2,1)S(1)} %get-tuple-element.15), channel_id=1, source_target_pairs={{0,16},{16,32},{32,48},{48,64},{64,80},{80,96},{96,112},{112,128},... | collective-permute-start | bytes 466952 | tf_op jit(solution)/shard_map/ppermute | solution.py:265
  57.3 0.1 rev.3
  57.4 0.1 pad_convert_fusion.line
  57.5 1.1 shard_map.75.bands
  58.6 0.0 copy-start.5
  58.6 1.6 shard_map.74.query
  60.2 4.1 %collective-permute-done.recv = bf16[152,512]{1,0:T(8,128)(2,1)S(1)} collective-permute-done((bf16[152,512]{1,0:T(8,128)(2,1)S(1)}, bf16[152,512]{1,0:T(8,128)(2,1)S(1)}, u32[]{:S(2)}, u32[]{:S(2)}) %collective-permute-start) | collective-permute-done | bytes 155680 | tf_op jit(solution)/shard_map/ppermute | solution.py:265
  64.3 2.9 %shard_map.76 = bf16[4,256,512]{2,1,0:T(8,128)(2,1)} custom-call(s32[8]{0:T(128)S(1)} %copy-done.4, bf16[256,512]{1,0:T(8,128)(2,1)S(1)} %get-tuple-element.14.z, f32[256,512]{1,0:T(8,128)S(1)} %shard_map.74.query, bf16[152,512]{1,0:T(8,128)(2,1)S(1)} %collective-permute-done.recv, bf16[24,512]{1,0:T(8,128)(2,1)S(1)} %get-tuple-element.16.head, ...), custom_call_target="tpu_custom_call" | custom-call | flops 1000000000 | bytes 4135968 | tf_op jit(solution)/shard_map/pallas_call | solution.py:35
  67.2 3.6 %all-to-all-start.1 = ((bf16[4,256,512]{2,1,0:T(8,128)(2,1)}), bf16[4,256,512]{2,1,0:T(8,128)(2,1)S(1)}, u32[]{:S(2)}, u32[]{:S(2)}) async-start(bf16[4,256,512]{2,1,0:T(8,128)(2,1)} %shard_map.76), calls=%async_computation.1 | async-start | bytes 2097152 | tf_op jit(solution)/shard_map/all_to_all | solution.py:350
  70.9 0.7 collective-permute-start.2
  71.6 6.6 %collective-permute-start.3 = (bf16[512,128]{1,0:T(8,128)(2,1)S(1)}, bf16[512,128]{1,0:T(8,128)(2,1)S(1)}, u32[]{:S(2)}, u32[]{:S(2)}) collective-permute-start(bf16[512,128]{1,0:T(8,128)(2,1)S(1)} %get-tuple-element.30), channel_id=1, source_target_pairs={{0,16},{1,0},{16,48},{17,32},{32,17},{33,1},{48,49},{49,33},{2,18}... | collective-permute-start | bytes 393224 | tf_op jit(solution)/shard_map/ppermute | solution.py:279
  78.2 0.0 collective-permute-done.2
  78.2 4.1 %collective-permute-done.3 = bf16[512,128]{1,0:T(8,128)(2,1)S(1)} collective-permute-done((bf16[512,128]{1,0:T(8,128)(2,1)S(1)}, bf16[512,128]{1,0:T(8,128)(2,1)S(1)}, u32[]{:S(2)}, u32[]{:S(2)}) %collective-permute-start.3) | collective-permute-done | bytes 131104 | tf_op jit(solution)/shard_map/ppermute | solution.py:279
  82.3 5.4 %collective-permute-start.4 = (bf16[1024,128]{1,0:T(8,128)(2,1)S(1)}, bf16[1024,128]{1,0:T(8,128)(2,1)S(1)}, u32[]{:S(2)}, u32[]{:S(2)}) collective-permute-start(bf16[1024,128]{1,0:T(8,128)(2,1)S(1)} %pad_maximum_fusion.refs_0_), channel_id=1, source_target_pairs={{0,64},{64,128},{128,192},{192,256},{256,320},{320,384},{384,448},... | collective-permute-start | bytes 786440 | tf_op jit(solution)/shard_map/ppermute | solution.py:288
  87.7 1.9 %collective-permute-start.5 = (bf16[1024,128]{1,0:T(8,128)(2,1)S(1)}, bf16[1024,128]{1,0:T(8,128)(2,1)S(1)}, u32[]{:S(2)}, u32[]{:S(2)}) collective-permute-start(bf16[1024,128]{1,0:T(8,128)(2,1)S(1)} %pad_maximum_fusion.refs_0_), channel_id=1, source_target_pairs={{0,448},{64,0},{128,64},{192,128},{256,192},{320,256},{384,320},{4... | collective-permute-start | bytes 786440 | tf_op jit(solution)/shard_map/ppermute | solution.py:288
  89.6 0.0 all-to-all-done.1
  89.6 5.1 %collective-permute-start.1 = (bf16[1024,512]{1,0:T(8,128)(2,1)S(1)}, bf16[1024,512]{1,0:T(8,128)(2,1)S(1)}, u32[]{:S(2)}, u32[]{:S(2)}) collective-permute-start(bf16[1024,512]{1,0:T(8,128)(2,1)S(1)} %bitcast.7), channel_id=1, source_target_pairs={{0,1},{1,0},{2,3},{3,2},{4,5},{5,4},{6,7},{7,6},{8,9},{9,8},{10,11... | collective-permute-start | bytes 3145736 | tf_op jit(solution)/shard_map/ppermute | solution.py:352
  94.7 0.0 collective-permute-done.4.refs_1_
  94.7 4.9 %collective-permute-start.6 = (bf16[1024,128]{1,0:T(8,128)(2,1)S(1)}, bf16[1024,128]{1,0:T(8,128)(2,1)S(1)}, u32[]{:S(2)}, u32[]{:S(2)}) collective-permute-start(bf16[1024,128]{1,0:T(8,128)(2,1)S(1)} %collective-permute-done.4.refs_1_), channel_id=1, source_target_pairs={{0,64},{64,128},{128,192},{192,256},{256,320},{320,384},{384,448},... | collective-permute-start | bytes 786440 | tf_op jit(solution)/shard_map/ppermute | solution.py:288
  99.6 0.0 collective-permute-done.5.refs_2_
  99.6 1.9 %collective-permute-start.7 = (bf16[1024,128]{1,0:T(8,128)(2,1)S(1)}, bf16[1024,128]{1,0:T(8,128)(2,1)S(1)}, u32[]{:S(2)}, u32[]{:S(2)}) collective-permute-start(bf16[1024,128]{1,0:T(8,128)(2,1)S(1)} %collective-permute-done.5.refs_2_), channel_id=1, source_target_pairs={{0,448},{64,0},{128,64},{192,128},{256,192},{320,256},{384,320},{4... | collective-permute-start | bytes 786440 | tf_op jit(solution)/shard_map/ppermute | solution.py:288
  101.5 3.9 %collective-permute-done.6.refs_3_ = bf16[1024,128]{1,0:T(8,128)(2,1)S(1)} collective-permute-done((bf16[1024,128]{1,0:T(8,128)(2,1)S(1)}, bf16[1024,128]{1,0:T(8,128)(2,1)S(1)}, u32[]{:S(2)}, u32[]{:S(2)}) %collective-permute-start.6) | collective-permute-done | bytes 262176 | tf_op jit(solution)/shard_map/ppermute | solution.py:288
  105.5 5.6 %collective-permute-start.8 = (bf16[1024,128]{1,0:T(8,128)(2,1)S(1)}, bf16[1024,128]{1,0:T(8,128)(2,1)S(1)}, u32[]{:S(2)}, u32[]{:S(2)}) collective-permute-start(bf16[1024,128]{1,0:T(8,128)(2,1)S(1)} %collective-permute-done.6.refs_3_), channel_id=1, source_target_pairs={{0,64},{64,128},{128,192},{192,256},{256,320},{320,384},{384,448},... | collective-permute-start | bytes 786440 | tf_op jit(solution)/shard_map/ppermute | solution.py:288
  111.1 0.0 collective-permute-done.7.refs_4_
  111.1 1.9 %collective-permute-start.9 = (bf16[1024,128]{1,0:T(8,128)(2,1)S(1)}, bf16[1024,128]{1,0:T(8,128)(2,1)S(1)}, u32[]{:S(2)}, u32[]{:S(2)}) collective-permute-start(bf16[1024,128]{1,0:T(8,128)(2,1)S(1)} %collective-permute-done.7.refs_4_), channel_id=1, source_target_pairs={{0,448},{64,0},{128,64},{192,128},{256,192},{320,256},{384,320},{4... | collective-permute-start | bytes 786440 | tf_op jit(solution)/shard_map/ppermute | solution.py:288
  113.0 3.1 %collective-permute-done.8.up = bf16[1024,128]{1,0:T(8,128)(2,1)S(1)} collective-permute-done((bf16[1024,128]{1,0:T(8,128)(2,1)S(1)}, bf16[1024,128]{1,0:T(8,128)(2,1)S(1)}, u32[]{:S(2)}, u32[]{:S(2)}) %collective-permute-start.8) | collective-permute-done | bytes 262176 | tf_op jit(solution)/shard_map/ppermute | solution.py:288
  116.1 5.6 %collective-permute-done.9.down = bf16[1024,128]{1,0:T(8,128)(2,1)S(1)} collective-permute-done((bf16[1024,128]{1,0:T(8,128)(2,1)S(1)}, bf16[1024,128]{1,0:T(8,128)(2,1)S(1)}, u32[]{:S(2)}, u32[]{:S(2)}) %collective-permute-start.9) | collective-permute-done | bytes 262176 | tf_op jit(solution)/shard_map/ppermute | solution.py:288
  121.8 1.9 %collective-permute-start.10 = (bf16[1024,128]{1,0:T(8,128)(2,1)S(1)}, bf16[1024,128]{1,0:T(8,128)(2,1)S(1)}, u32[]{:S(2)}, u32[]{:S(2)}) collective-permute-start(bf16[1024,128]{1,0:T(8,128)(2,1)S(1)} %get-tuple-element.17.refs_5_), channel_id=1, source_target_pairs={{0,64},{64,128},{128,192},{192,256},{256,320},{320,384},{384,448},... | collective-permute-start | bytes 786440 | tf_op jit(solution)/shard_map/ppermute | solution.py:288
  123.7 6.6 %collective-permute-done.10.refs_7_ = bf16[1024,128]{1,0:T(8,128)(2,1)S(1)} collective-permute-done((bf16[1024,128]{1,0:T(8,128)(2,1)S(1)}, bf16[1024,128]{1,0:T(8,128)(2,1)S(1)}, u32[]{:S(2)}, u32[]{:S(2)}) %collective-permute-start.10) | collective-permute-done | bytes 262176 | tf_op jit(solution)/shard_map/ppermute | solution.py:288
  130.3 0.0 collective-permute-done.1.other
  130.3 2.9 %shard_map.79 = (bf16[4,2,256,128]{3,2,1,0:T(8,128)(2,1)S(1)}, bf16[4,2,256,128]{3,2,1,0:T(8,128)(2,1)S(1)}) custom-call(bf16[1024,512]{1,0:T(8,128)(2,1)S(1)} %bitcast.8, bf16[1024,512]{1,0:T(8,128)(2,1)S(1)} %collective-permute-done.1.other, bf16[1024,128]{1,0:T(8,128)(2,1)S(1)} %pad_maximum_fusion.refs_0_, ...), custom_call_target="tpu_custom_call" | custom-call | flops 1073741824 | bytes 5242880 | tf_op jit(solution)/shard_map/pallas_call | solution.py:35
  133.2 10.9 %collective-permute-start.12 = (bf16[4,2,256,128]{3,2,1,0:T(8,128)(2,1)S(1)}, bf16[4,2,256,128]{3,2,1,0:T(8,128)(2,1)S(1)}, u32[]{:S(2)}, u32[]{:S(2)}) collective-permute-start(bf16[4,2,256,128]{3,2,1,0:T(8,128)(2,1)S(1)} %get-tuple-element.22), channel_id=1, source_target_pairs={{0,14},{2,0},{4,2},{6,4},{8,6},{10,8},{12,10},{14,12},{1,15},{3,1}... | collective-permute-start | bytes 1572872 | tf_op jit(solution)/shard_map/ppermute | solution.py:251
  144.2 2.9 %shard_map.78 = (bf16[4,2,256,128]{3,2,1,0:T(8,128)(2,1)S(1)}, bf16[4,2,256,128]{3,2,1,0:T(8,128)(2,1)S(1)}) custom-call(bf16[1024,512]{1,0:T(8,128)(2,1)S(1)} %bitcast.9, bf16[1024,512]{1,0:T(8,128)(2,1)S(1)} %collective-permute-done.1.other, bf16[1024,128]{1,0:T(8,128)(2,1)S(1)} %pad_maximum_fusion.refs_0_, ...), custom_call_target="tpu_custom_call" | custom-call | flops 1073741824 | bytes 5242880 | tf_op jit(solution)/shard_map/pallas_call | solution.py:35
  147.1 1.9 %collective-permute-start.11 = (bf16[4,2,256,128]{3,2,1,0:T(8,128)(2,1)S(1)}, bf16[4,2,256,128]{3,2,1,0:T(8,128)(2,1)S(1)}, u32[]{:S(2)}, u32[]{:S(2)}) collective-permute-start(bf16[4,2,256,128]{3,2,1,0:T(8,128)(2,1)S(1)} %get-tuple-element.21), channel_id=1, source_target_pairs={{0,2},{2,4},{4,6},{6,8},{8,10},{10,12},{12,14},{14,0},{1,3},{3,5},... | collective-permute-start | bytes 1572872 | tf_op jit(solution)/shard_map/ppermute | solution.py:251
  149.0 4.1 %collective-permute-done.12.got1 = bf16[4,2,256,128]{3,2,1,0:T(8,128)(2,1)S(1)} collective-permute-done((bf16[4,2,256,128]{3,2,1,0:T(8,128)(2,1)S(1)}, bf16[4,2,256,128]{3,2,1,0:T(8,128)(2,1)S(1)}, u32[]{:S(2)}, u32[]{:S(2)}) %collective-permute-start.12) | collective-permute-done | bytes 524320 | tf_op jit(solution)/shard_map/ppermute | solution.py:251
  153.1 8.2 %collective-permute-done.11.got0 = bf16[4,2,256,128]{3,2,1,0:T(8,128)(2,1)S(1)} collective-permute-done((bf16[4,2,256,128]{3,2,1,0:T(8,128)(2,1)S(1)}, bf16[4,2,256,128]{3,2,1,0:T(8,128)(2,1)S(1)}, u32[]{:S(2)}, u32[]{:S(2)}) %collective-permute-start.11) | collective-permute-done | bytes 524320 | tf_op jit(solution)/shard_map/ppermute | solution.py:251
  161.3 0.2 shard_map.80
  161.6 28.6 %all_to_all.16 = bf16[16,256,128]{2,1,0:T(8,128)(2,1)S(1)} all-to-all(bf16[16,256,128]{2,1,0:T(8,128)(2,1)S(1)} %bitcast.10), channel_id=1, replica_groups=mesh['y'=8,'x'=4,'zh'=4,'zl'=2,'core'=2] {'zh','x'}, dimensions={0} | all-to-all | bytes 2097152 | tf_op jit(solution)/shard_map/all_to_all | solution.py:361
  190.2 0.1 slice_reduce_fusion.3
  190.3 0.7 pad_maximum_fusion.1
  (14 shorter events, 0.1 us)
Async XLA Ops:
  0.0 1.4 copy-start
  1.4 0.7 copy-start.2
  4.3 48.3 %copy-start.1 = (bf16[3,7,512]{2,1,0:T(8,128)(2,1)S(1)}, bf16[3,7,512]{2,1,0:T(8,128)(2,1)}, u32[]{:S(2)}) copy-start(bf16[3,7,512]{2,1,0:T(8,128)(2,1)} %taps.5) | copy-start | bytes 64516
  4.3 48.3 %copy-start.4 = (s32[8]{0:T(128)S(1)}, s32[8]{0:T(128)}, u32[]{:S(2)}) copy-start(s32[8]{0:T(128)} %lengths.5) | copy-start | bytes 100
  52.6 4.6 %copy-start.7 = (bf16[128,32]{0,1:T(8,128)(2,1)S(1)}, bf16[128,32]{0,1:T(8,128)(2,1)}, u32[]{:S(2)}) copy-start(bf16[128,32]{0,1:T(8,128)(2,1)} %param.9) | copy-start | bytes 24580
  52.6 5.9 %copy-start.3 = (s32[32,16]{0,1:T(8,128)S(1)}, s32[32,16]{0,1:T(8,128)}, u32[]{:S(2)}) copy-start(s32[32,16]{0,1:T(8,128)} %param.13) | copy-start | bytes 6148
  55.1 9.2 %collective-permute-start = (bf16[152,512]{1,0:T(8,128)(2,1)S(1)}, bf16[152,512]{1,0:T(8,128)(2,1)S(1)}, u32[]{:S(2)}, u32[]{:S(2)}) collective-permute-start(bf16[152,512]{1,0:T(8,128)(2,1)S(1)} %get-tuple-element.15), channel_id=1, source_target_pairs={{0,16},{16,32},{32,48},{48,64},{64,80},{80,96},{96,112},{112,128},... | collective-permute-start | bytes 466952 | tf_op jit(solution)/shard_map/ppermute | solution.py:265
  58.6 5.7 %copy-start.5 = (f32[512]{0:T(512)S(1)}, f32[512]{0:T(512)}, u32[]{:S(2)}) copy-start(f32[512]{0:T(512)} %param.10) | copy-start | bytes 6148
  67.2 3.7 %copy-start.6 = (bf16[512,256]{1,0:T(8,128)(2,1)S(1)}, bf16[512,256]{1,0:T(8,128)(2,1)}, u32[]{:S(2)}) copy-start(bf16[512,256]{1,0:T(8,128)(2,1)} %param.11) | copy-start | bytes 786436
  67.2 22.4 %all-to-all-start.1 = ((bf16[4,256,512]{2,1,0:T(8,128)(2,1)}), bf16[4,256,512]{2,1,0:T(8,128)(2,1)S(1)}, u32[]{:S(2)}, u32[]{:S(2)}) async-start(bf16[4,256,512]{2,1,0:T(8,128)(2,1)} %shard_map.76), calls=%async_computation.1 | async-start | bytes 2097152 | tf_op jit(solution)/shard_map/all_to_all | solution.py:350
  70.9 7.3 %collective-permute-start.2 = (bf16[512,128]{1,0:T(8,128)(2,1)S(1)}, bf16[512,128]{1,0:T(8,128)(2,1)S(1)}, u32[]{:S(2)}, u32[]{:S(2)}) collective-permute-start(bf16[512,128]{1,0:T(8,128)(2,1)S(1)} %get-tuple-element.29), channel_id=1, source_target_pairs={{0,0},{1,16},{16,32},{17,48},{32,1},{33,17},{48,33},{49,49},{2,2},... | collective-permute-start | bytes 393224 | tf_op jit(solution)/shard_map/ppermute | solution.py:278
  71.6 10.7 %collective-permute-start.3 = (bf16[512,128]{1,0:T(8,128)(2,1)S(1)}, bf16[512,128]{1,0:T(8,128)(2,1)S(1)}, u32[]{:S(2)}, u32[]{:S(2)}) collective-permute-start(bf16[512,128]{1,0:T(8,128)(2,1)S(1)} %get-tuple-element.30), channel_id=1, source_target_pairs={{0,16},{1,0},{16,48},{17,32},{32,17},{33,1},{48,49},{49,33},{2,18}... | collective-permute-start | bytes 393224 | tf_op jit(solution)/shard_map/ppermute | solution.py:279
  82.3 12.4 %collective-permute-start.4 = (bf16[1024,128]{1,0:T(8,128)(2,1)S(1)}, bf16[1024,128]{1,0:T(8,128)(2,1)S(1)}, u32[]{:S(2)}, u32[]{:S(2)}) collective-permute-start(bf16[1024,128]{1,0:T(8,128)(2,1)S(1)} %pad_maximum_fusion.refs_0_), channel_id=1, source_target_pairs={{0,64},{64,128},{128,192},{192,256},{256,320},{320,384},{384,448},... | collective-permute-start | bytes 786440 | tf_op jit(solution)/shard_map/ppermute | solution.py:288
  87.7 11.9 %collective-permute-start.5 = (bf16[1024,128]{1,0:T(8,128)(2,1)S(1)}, bf16[1024,128]{1,0:T(8,128)(2,1)S(1)}, u32[]{:S(2)}, u32[]{:S(2)}) collective-permute-start(bf16[1024,128]{1,0:T(8,128)(2,1)S(1)} %pad_maximum_fusion.refs_0_), channel_id=1, source_target_pairs={{0,448},{64,0},{128,64},{192,128},{256,192},{320,256},{384,320},{4... | collective-permute-start | bytes 786440 | tf_op jit(solution)/shard_map/ppermute | solution.py:288
  89.6 40.7 %collective-permute-start.1 = (bf16[1024,512]{1,0:T(8,128)(2,1)S(1)}, bf16[1024,512]{1,0:T(8,128)(2,1)S(1)}, u32[]{:S(2)}, u32[]{:S(2)}) collective-permute-start(bf16[1024,512]{1,0:T(8,128)(2,1)S(1)} %bitcast.7), channel_id=1, source_target_pairs={{0,1},{1,0},{2,3},{3,2},{4,5},{5,4},{6,7},{7,6},{8,9},{9,8},{10,11... | collective-permute-start | bytes 3145736 | tf_op jit(solution)/shard_map/ppermute | solution.py:352
  94.7 10.7 %collective-permute-start.6 = (bf16[1024,128]{1,0:T(8,128)(2,1)S(1)}, bf16[1024,128]{1,0:T(8,128)(2,1)S(1)}, u32[]{:S(2)}, u32[]{:S(2)}) collective-permute-start(bf16[1024,128]{1,0:T(8,128)(2,1)S(1)} %collective-permute-done.4.refs_1_), channel_id=1, source_target_pairs={{0,64},{64,128},{128,192},{192,256},{256,320},{320,384},{384,448},... | collective-permute-start | bytes 786440 | tf_op jit(solution)/shard_map/ppermute | solution.py:288
  99.6 11.5 %collective-permute-start.7 = (bf16[1024,128]{1,0:T(8,128)(2,1)S(1)}, bf16[1024,128]{1,0:T(8,128)(2,1)S(1)}, u32[]{:S(2)}, u32[]{:S(2)}) collective-permute-start(bf16[1024,128]{1,0:T(8,128)(2,1)S(1)} %collective-permute-done.5.refs_2_), channel_id=1, source_target_pairs={{0,448},{64,0},{128,64},{192,128},{256,192},{320,256},{384,320},{4... | collective-permute-start | bytes 786440 | tf_op jit(solution)/shard_map/ppermute | solution.py:288
  105.5 10.6 %collective-permute-start.8 = (bf16[1024,128]{1,0:T(8,128)(2,1)S(1)}, bf16[1024,128]{1,0:T(8,128)(2,1)S(1)}, u32[]{:S(2)}, u32[]{:S(2)}) collective-permute-start(bf16[1024,128]{1,0:T(8,128)(2,1)S(1)} %collective-permute-done.6.refs_3_), channel_id=1, source_target_pairs={{0,64},{64,128},{128,192},{192,256},{256,320},{320,384},{384,448},... | collective-permute-start | bytes 786440 | tf_op jit(solution)/shard_map/ppermute | solution.py:288
  111.1 10.6 %collective-permute-start.9 = (bf16[1024,128]{1,0:T(8,128)(2,1)S(1)}, bf16[1024,128]{1,0:T(8,128)(2,1)S(1)}, u32[]{:S(2)}, u32[]{:S(2)}) collective-permute-start(bf16[1024,128]{1,0:T(8,128)(2,1)S(1)} %collective-permute-done.7.refs_4_), channel_id=1, source_target_pairs={{0,448},{64,0},{128,64},{192,128},{256,192},{320,256},{384,320},{4... | collective-permute-start | bytes 786440 | tf_op jit(solution)/shard_map/ppermute | solution.py:288
  121.8 8.5 %collective-permute-start.10 = (bf16[1024,128]{1,0:T(8,128)(2,1)S(1)}, bf16[1024,128]{1,0:T(8,128)(2,1)S(1)}, u32[]{:S(2)}, u32[]{:S(2)}) collective-permute-start(bf16[1024,128]{1,0:T(8,128)(2,1)S(1)} %get-tuple-element.17.refs_5_), channel_id=1, source_target_pairs={{0,64},{64,128},{128,192},{192,256},{256,320},{320,384},{384,448},... | collective-permute-start | bytes 786440 | tf_op jit(solution)/shard_map/ppermute | solution.py:288
  133.2 19.9 %collective-permute-start.12 = (bf16[4,2,256,128]{3,2,1,0:T(8,128)(2,1)S(1)}, bf16[4,2,256,128]{3,2,1,0:T(8,128)(2,1)S(1)}, u32[]{:S(2)}, u32[]{:S(2)}) collective-permute-start(bf16[4,2,256,128]{3,2,1,0:T(8,128)(2,1)S(1)} %get-tuple-element.22), channel_id=1, source_target_pairs={{0,14},{2,0},{4,2},{6,4},{8,6},{10,8},{12,10},{14,12},{1,15},{3,1}... | collective-permute-start | bytes 1572872 | tf_op jit(solution)/shard_map/ppermute | solution.py:251
  147.1 14.2 %collective-permute-start.11 = (bf16[4,2,256,128]{3,2,1,0:T(8,128)(2,1)S(1)}, bf16[4,2,256,128]{3,2,1,0:T(8,128)(2,1)S(1)}, u32[]{:S(2)}, u32[]{:S(2)}) collective-permute-start(bf16[4,2,256,128]{3,2,1,0:T(8,128)(2,1)S(1)} %get-tuple-element.21), channel_id=1, source_target_pairs={{0,2},{2,4},{4,6},{6,8},{8,10},{10,12},{12,14},{14,0},{1,3},{3,5},... | collective-permute-start | bytes 1572872 | tf_op jit(solution)/shard_map/ppermute | solution.py:251

commit v7 on v6

--- a/solution.py
+++ b/solution.py
@@ -198,12 +198,14 @@
 def project_kernel(offsets, part, own, other, *refs):
     weights, (same, cross) = refs[:-2], refs[-2:]
     count, rows, lane = same.shape[1:]
-    n = len(weights)
+    n = len(weights) - 1
     y = lax.axis_index("y")
     at = slice(part * count * rows, (part + 1) * count * rows)
     left = jnp.concatenate([own[at, :], other[at, :]], axis=1)
+    blocks = [w[...] for w in weights[:-2]]
+    blocks.append(jnp.concatenate([weights[-2][...], weights[-1][...]], axis=0))
     for pair in range(0, n, 2):
-        wide = jnp.concatenate([weights[pair][...], weights[pair + 1][...]], axis=1)
+        wide = jnp.concatenate(blocks[pair : pair + 2], axis=1)
         got = jnp.dot(left, wide, preferred_element_type=F32).astype(BF16)
         for i in range(2):
             owner = lax.rem(y - offsets[pair + i] + n, n)
@@ -226,10 +228,10 @@
     lane = blocks[0].shape[1]
     return call(
         functools.partial(project_kernel, tuple(w[0] for w in weights), part),
-        [shape((len(blocks) // 2, nx // 2, rows, lane))] * 2,
+        [shape(((len(blocks) - 1) // 2, nx // 2, rows, lane))] * 2,
         [vmem()] * (2 + len(blocks)),
         (own, other, *blocks),
-        2 * own.size * len(blocks) * lane,
+        2 * own.size * 8 * lane,
     )
 
 
@@ -307,15 +309,14 @@
     blocks = lax.all_to_all(packed, CTX, split_axis=0, concat_axis=0, tiled=True)
 
     block = weight_columns(out_weight)
-    weights = [(0, block)]
-    up = down = block
-    for d in (1, 2, 3, 4):
-        up = around(up, 1)
-        down = around(down, -1) if d < 4 else None
-        if d == 3:
-            both = [shape(up.shape)] * 2
-            up, down = call(relay_kernel, both, [vmem()] * 2, (up, down), 0)
-        weights += [(d, up)] if down is None else [(d, up), (-d, down)]
+    up, down = around(block, 1), around(block, -1)
+    up2, down2 = around(up, 1), around(down, -1)
+    weights = [(0, block), (1, up), (-1, down), (2, up2), (-2, down2)]
+    both = [shape(up.shape)] * 2
+    up, down = call(relay_kernel, both, [vmem()] * 2, (up, down), 0)
+    cut = up.shape[0] // 2
+    weights += [(3, around(up, 2)), (-3, around(down, -2))]
+    weights += [(4, around(up[:cut], 3)), (4, around(down[cut:], -3))]
 
     groups = medium_filters.shape[1]
     line = jnp.pad(medium_filters[::-1].T.astype(F32), ((0, 0), (1, HALF - 1)))

time: 192 us -> 203 us (1.057)
  the two profiles are of different devices: /device:TPU:24 before, /device:TPU:1 now
where the time goes in v7:
time: 203 us; the launch traced here: 202 us
  blocking collectives  80 us (39%)
  starting transfers between devices  67 us (33%)
  waiting for transfers between devices  35.2 us (17%)
  Pallas kernels  16.6 us (8%)
  local copies, waits for them, and re-layouts  2.24 us (1%)
    all_to_all x1, blocking collectives, operator(): lax.all_to_all(packed, CTX, split_axis=0, concat_axis=0, tiled=True)  48.9 us
    all_to_all x1, blocking collectives, operator(): lax.all_to_all(flat, ('zh', 'x'), split_axis=0, concat_axis=0, tiled=True)  31.1 us
    ppermute x8, starting transfers between devices, around(): return lax.ppermute(block, 'y', [(i, (i + distance) % n) for i in range(n)])  30.5 us
    ppermute x8, waiting for transfers between devices, around(): return lax.ppermute(block, 'y', [(i, (i + distance) % n) for i in range(n)])  19.4 us
    pallas_call x8, Pallas kernels, call(): pl.pallas_call(body, out_shape=outs, in_specs=ins, out_specs=[vmem()] * l...  14.4 us
    ppermute x2, waiting for transfers between devices, along_z(): lax.ppermute(block, ('zh', 'zl'), [(i, (i + distance) % n) for i in range...  13.3 us
    ppermute x2, starting transfers between devices, along_z(): lax.ppermute(block, ('zh', 'zl'), [(i, (i + distance) % n) for i in range...  12.6 us
    ppermute x1, starting transfers between devices, operator(): other = lax.ppermute(own, 'core', [(0, 1), (1, 0)])  7.95 us
  transfers between devices with their start and end apart: 15, of which 10 were waited for; matrix products, arithmetic and copies ran while one was open for 0% of the time, Pallas kernels for 3%

profile of v7, /device:TPU:1, one launch (start us, length us, event | category | flops | bytes accessed | tf_op | source)
XLA Modules:
  0.0 202.4 jit_solution(1982667934915982651)
XLA Ops:
  0.0 1.4 copy-done
  1.4 0.7 copy-done.2
  2.1 2.2 %pack.1 = bf16[32,3,16,512]{3,2,1,0:T(8,128)(2,1)S(1)} custom-call(s32[16,32]{1,0:T(8,128)S(1)} %bitcast.12, bf16[3,512,512]{2,1,0:T(8,128)(2,1)S(1)} %bitcast.11), custom_call_target="tpu_custom_call" | custom-call | flops 1000000 | bytes 3145728 | tf_op jit(solution)/shard_map/pack/pallas_call | solution.py:82
  4.3 0.0 copy-start.1
  4.3 0.0 copy-start.4
  4.3 48.9 %all_to_all.15.blocks = bf16[32,3,16,512]{3,2,1,0:T(8,128)(2,1)S(1)} all-to-all(bf16[32,3,16,512]{3,2,1,0:T(8,128)(2,1)S(1)} %pack.1), channel_id=1, replica_groups=mesh['y'=8,'x'=4,'zh'=4,'zl'=2,'core'=2] {'y','x'}, dimensions={0} | all-to-all | bytes 3145728 | tf_op jit(solution)/shard_map/all_to_all | solution.py:309
  53.2 2.4 %shard_map.73 = (bf16[256,512]{1,0:T(8,128)(2,1)S(1)}, bf16[152,512]{1,0:T(8,128)(2,1)S(1)}, bf16[24,512]{1,0:T(8,128)(2,1)S(1)}) custom-call(s32[16,32]{1,0:T(8,128)S(1)} %bitcast.13, s32[8]{0:T(128)S(1)} %copy-done.4, bf16[32,3,16,512]{3,2,1,0:T(8,128)(2,1)S(1)} %all_to_all.15.blocks, bf16[3,7,512]{2,1,0:T(8,128)(2,1)S(1)} %copy-done.1), custom_call_target="tpu_custom_call" | custom-call | flops 10000000 | bytes 2038816 | tf_op jit(solution)/shard_map/pallas_call | solution.py:35
  55.6 2.7 %collective-permute-start = (bf16[152,512]{1,0:T(8,128)(2,1)S(1)}, bf16[152,512]{1,0:T(8,128)(2,1)S(1)}, u32[]{:S(2)}, u32[]{:S(2)}) collective-permute-start(bf16[152,512]{1,0:T(8,128)(2,1)S(1)} %get-tuple-element.15), channel_id=1, source_target_pairs={{0,16},{16,32},{32,48},{48,64},{64,80},{80,96},{96,112},{112,128},... | collective-permute-start | bytes 466952 | tf_op jit(solution)/shard_map/ppermute | solution.py:267
  58.4 0.1 rev.3
  58.5 0.1 pad_convert_fusion.line
  58.6 1.1 shard_map.75.bands
  59.7 0.0 copy-start.5
  59.7 1.6 shard_map.74.query
  61.3 0.0 collective-permute-done.recv
  61.3 2.9 %shard_map.76 = bf16[4,256,512]{2,1,0:T(8,128)(2,1)} custom-call(s32[8]{0:T(128)S(1)} %copy-done.4, bf16[256,512]{1,0:T(8,128)(2,1)S(1)} %get-tuple-element.14.z, f32[256,512]{1,0:T(8,128)S(1)} %shard_map.74.query, bf16[152,512]{1,0:T(8,128)(2,1)S(1)} %collective-permute-done.recv, bf16[24,512]{1,0:T(8,128)(2,1)S(1)} %get-tuple-element.16.head, ...), custom_call_target="tpu_custom_call" | custom-call | flops 1000000000 | bytes 4135968 | tf_op jit(solution)/shard_map/pallas_call | solution.py:35
  64.2 4.3 %all-to-all-start.1 = ((bf16[4,256,512]{2,1,0:T(8,128)(2,1)}), bf16[4,256,512]{2,1,0:T(8,128)(2,1)S(1)}, u32[]{:S(2)}, u32[]{:S(2)}) async-start(bf16[4,256,512]{2,1,0:T(8,128)(2,1)} %shard_map.76), calls=%async_computation.1 | async-start | bytes 2097152 | tf_op jit(solution)/shard_map/all_to_all | solution.py:351
  68.5 7.0 %collective-permute-start.2 = (bf16[512,128]{1,0:T(8,128)(2,1)S(1)}, bf16[512,128]{1,0:T(8,128)(2,1)S(1)}, u32[]{:S(2)}, u32[]{:S(2)}) collective-permute-start(bf16[512,128]{1,0:T(8,128)(2,1)S(1)} %get-tuple-element.29), channel_id=1, source_target_pairs={{0,0},{1,16},{16,32},{17,48},{32,1},{33,17},{48,33},{49,49},{2,2},... | collective-permute-start | bytes 393224 | tf_op jit(solution)/shard_map/ppermute | solution.py:280
  75.6 1.9 collective-permute-start.3
  77.5 2.4 %all-to-all-done.1 = bf16[4,256,512]{2,1,0:T(8,128)(2,1)S(1)} async-done(((bf16[4,256,512]{2,1,0:T(8,128)(2,1)}), bf16[4,256,512]{2,1,0:T(8,128)(2,1)S(1)}, u32[]{:S(2)}, u32[]{:S(2)}) %all-to-all-start.1) | async-done | bytes 1048608 | tf_op jit(solution)/shard_map/all_to_all | solution.py:351
  79.9 7.9 %collective-permute-start.1 = (bf16[1024,512]{1,0:T(8,128)(2,1)S(1)}, bf16[1024,512]{1,0:T(8,128)(2,1)S(1)}, u32[]{:S(2)}, u32[]{:S(2)}) collective-permute-start(bf16[1024,512]{1,0:T(8,128)(2,1)S(1)} %bitcast.7), channel_id=1, source_target_pairs={{0,1},{1,0},{2,3},{3,2},{4,5},{5,4},{6,7},{7,6},{8,9},{9,8},{10,11... | collective-permute-start | bytes 3145736 | tf_op jit(solution)/shard_map/ppermute | solution.py:353
  87.9 0.0 collective-permute-done.2
  87.9 0.0 collective-permute-done.3
  88.0 4.0 %collective-permute-start.4 = (bf16[1024,128]{1,0:T(8,128)(2,1)S(1)}, bf16[1024,128]{1,0:T(8,128)(2,1)S(1)}, u32[]{:S(2)}, u32[]{:S(2)}) collective-permute-start(bf16[1024,128]{1,0:T(8,128)(2,1)S(1)} %pad_maximum_fusion.refs_0_), channel_id=1, source_target_pairs={{0,64},{64,128},{128,192},{192,256},{256,320},{320,384},{384,448},... | collective-permute-start | bytes 786440 | tf_op jit(solution)/shard_map/ppermute | solution.py:290
  92.0 2.5 %collective-permute-start.5 = (bf16[1024,128]{1,0:T(8,128)(2,1)S(1)}, bf16[1024,128]{1,0:T(8,128)(2,1)S(1)}, u32[]{:S(2)}, u32[]{:S(2)}) collective-permute-start(bf16[1024,128]{1,0:T(8,128)(2,1)S(1)} %pad_maximum_fusion.refs_0_), channel_id=1, source_target_pairs={{0,448},{64,0},{128,64},{192,128},{256,192},{320,256},{384,320},{4... | collective-permute-start | bytes 786440 | tf_op jit(solution)/shard_map/ppermute | solution.py:290
  94.5 4.4 %collective-permute-done.4.up.refs_1_ = bf16[1024,128]{1,0:T(8,128)(2,1)S(1)} collective-permute-done((bf16[1024,128]{1,0:T(8,128)(2,1)S(1)}, bf16[1024,128]{1,0:T(8,128)(2,1)S(1)}, u32[]{:S(2)}, u32[]{:S(2)}) %collective-permute-start.4) | collective-permute-done | bytes 262176 | tf_op jit(solution)/shard_map/ppermute | solution.py:290
  98.9 2.5 %collective-permute-done.5.down.refs_2_ = bf16[1024,128]{1,0:T(8,128)(2,1)S(1)} collective-permute-done((bf16[1024,128]{1,0:T(8,128)(2,1)S(1)}, bf16[1024,128]{1,0:T(8,128)(2,1)S(1)}, u32[]{:S(2)}, u32[]{:S(2)}) %collective-permute-start.5) | collective-permute-done | bytes 262176 | tf_op jit(solution)/shard_map/ppermute | solution.py:290
  101.5 7.5 %collective-permute-start.10 = (bf16[512,128]{1,0:T(8,128)(2,1)S(1)}, bf16[512,128]{1,0:T(8,128)(2,1)S(1)}, u32[]{:S(2)}, u32[]{:S(2)}) collective-permute-start(bf16[512,128]{1,0:T(8,128)(2,1)S(1)} %slice.26), channel_id=1, source_target_pairs={{0,192},{64,256},{128,320},{192,384},{256,448},{320,0},{384,64},{4... | collective-permute-start | bytes 393224 | tf_op jit(solution)/shard_map/ppermute | solution.py:290
  109.1 1.9 collective-permute-start.11
  111.0 4.3 %collective-permute-start.8 = (bf16[1024,128]{1,0:T(8,128)(2,1)S(1)}, bf16[1024,128]{1,0:T(8,128)(2,1)S(1)}, u32[]{:S(2)}, u32[]{:S(2)}) collective-permute-start(bf16[1024,128]{1,0:T(8,128)(2,1)S(1)} %get-tuple-element.17), channel_id=1, source_target_pairs={{0,128},{64,192},{128,256},{192,320},{256,384},{320,448},{384,0},{... | collective-permute-start | bytes 786440 | tf_op jit(solution)/shard_map/ppermute | solution.py:290
  115.3 3.1 %collective-permute-start.9 = (bf16[1024,128]{1,0:T(8,128)(2,1)S(1)}, bf16[1024,128]{1,0:T(8,128)(2,1)S(1)}, u32[]{:S(2)}, u32[]{:S(2)}) collective-permute-start(bf16[1024,128]{1,0:T(8,128)(2,1)S(1)} %get-tuple-element.18), channel_id=1, source_target_pairs={{0,384},{64,448},{128,0},{192,64},{256,128},{320,192},{384,256},{4... | collective-permute-start | bytes 786440 | tf_op jit(solution)/shard_map/ppermute | solution.py:290
  118.4 0.0 collective-permute-done.10.refs_7_
  118.4 2.2 %collective-permute-start.6 = (bf16[1024,128]{1,0:T(8,128)(2,1)S(1)}, bf16[1024,128]{1,0:T(8,128)(2,1)S(1)}, u32[]{:S(2)}, u32[]{:S(2)}) collective-permute-start(bf16[1024,128]{1,0:T(8,128)(2,1)S(1)} %collective-permute-done.4.up.refs_1_), channel_id=1, source_target_pairs={{0,64},{64,128},{128,192},{192,256},{256,320},{320,384},{384,448},... | collective-permute-start | bytes 786440 | tf_op jit(solution)/shard_map/ppermute | solution.py:290
  120.6 0.2 collective-permute-done.11.refs_8_
  120.8 4.9 %collective-permute-start.7 = (bf16[1024,128]{1,0:T(8,128)(2,1)S(1)}, bf16[1024,128]{1,0:T(8,128)(2,1)S(1)}, u32[]{:S(2)}, u32[]{:S(2)}) collective-permute-start(bf16[1024,128]{1,0:T(8,128)(2,1)S(1)} %collective-permute-done.5.down.refs_2_), channel_id=1, source_target_pairs={{0,448},{64,0},{128,64},{192,128},{256,192},{320,256},{384,320},{4... | collective-permute-start | bytes 786440 | tf_op jit(solution)/shard_map/ppermute | solution.py:290
  125.7 1.9 collective-permute-done.8.refs_5_
  127.6 4.9 %collective-permute-done.9.refs_6_ = bf16[1024,128]{1,0:T(8,128)(2,1)S(1)} collective-permute-done((bf16[1024,128]{1,0:T(8,128)(2,1)S(1)}, bf16[1024,128]{1,0:T(8,128)(2,1)S(1)}, u32[]{:S(2)}, u32[]{:S(2)}) %collective-permute-start.9) | collective-permute-done | bytes 262176 | tf_op jit(solution)/shard_map/ppermute | solution.py:290
  132.6 1.9 collective-permute-done.6.refs_3_
  134.5 3.6 %collective-permute-done.7.refs_4_ = bf16[1024,128]{1,0:T(8,128)(2,1)S(1)} collective-permute-done((bf16[1024,128]{1,0:T(8,128)(2,1)S(1)}, bf16[1024,128]{1,0:T(8,128)(2,1)S(1)}, u32[]{:S(2)}, u32[]{:S(2)}) %collective-permute-start.7) | collective-permute-done | bytes 262176 | tf_op jit(solution)/shard_map/ppermute | solution.py:290
  138.0 3.1 %shard_map.79 = (bf16[4,2,256,128]{3,2,1,0:T(8,128)(2,1)S(1)}, bf16[4,2,256,128]{3,2,1,0:T(8,128)(2,1)S(1)}) custom-call(bf16[1024,512]{1,0:T(8,128)(2,1)S(1)} %bitcast.8, bf16[1024,512]{1,0:T(8,128)(2,1)S(1)} %collective-permute-done.1.other, bf16[1024,128]{1,0:T(8,128)(2,1)S(1)} %pad_maximum_fusion.refs_0_, ...), custom_call_target="tpu_custom_call" | custom-call | flops 1073741824 | bytes 5242880 | tf_op jit(solution)/shard_map/pallas_call | solution.py:35
  141.1 10.7 %collective-permute-start.13 = (bf16[4,2,256,128]{3,2,1,0:T(8,128)(2,1)S(1)}, bf16[4,2,256,128]{3,2,1,0:T(8,128)(2,1)S(1)}, u32[]{:S(2)}, u32[]{:S(2)}) collective-permute-start(bf16[4,2,256,128]{3,2,1,0:T(8,128)(2,1)S(1)} %get-tuple-element.22), channel_id=1, source_target_pairs={{0,14},{2,0},{4,2},{6,4},{8,6},{10,8},{12,10},{14,12},{1,15},{3,1}... | collective-permute-start | bytes 1572872 | tf_op jit(solution)/shard_map/ppermute | solution.py:253
  151.8 3.1 %shard_map.78 = (bf16[4,2,256,128]{3,2,1,0:T(8,128)(2,1)S(1)}, bf16[4,2,256,128]{3,2,1,0:T(8,128)(2,1)S(1)}) custom-call(bf16[1024,512]{1,0:T(8,128)(2,1)S(1)} %bitcast.9, bf16[1024,512]{1,0:T(8,128)(2,1)S(1)} %collective-permute-done.1.other, bf16[1024,128]{1,0:T(8,128)(2,1)S(1)} %pad_maximum_fusion.refs_0_, ...), custom_call_target="tpu_custom_call" | custom-call | flops 1073741824 | bytes 5242880 | tf_op jit(solution)/shard_map/pallas_call | solution.py:35
  154.9 1.9 collective-permute-start.12
  156.8 5.2 %collective-permute-done.13.got1 = bf16[4,2,256,128]{3,2,1,0:T(8,128)(2,1)S(1)} collective-permute-done((bf16[4,2,256,128]{3,2,1,0:T(8,128)(2,1)S(1)}, bf16[4,2,256,128]{3,2,1,0:T(8,128)(2,1)S(1)}, u32[]{:S(2)}, u32[]{:S(2)}) %collective-permute-start.13) | collective-permute-done | bytes 524320 | tf_op jit(solution)/shard_map/ppermute | solution.py:253
  162.0 8.1 %collective-permute-done.12.got0 = bf16[4,2,256,128]{3,2,1,0:T(8,128)(2,1)S(1)} collective-permute-done((bf16[4,2,256,128]{3,2,1,0:T(8,128)(2,1)S(1)}, bf16[4,2,256,128]{3,2,1,0:T(8,128)(2,1)S(1)}, u32[]{:S(2)}, u32[]{:S(2)}) %collective-permute-start.12) | collective-permute-done | bytes 524320 | tf_op jit(solution)/shard_map/ppermute | solution.py:253
  170.1 0.2 shard_map.80
  170.4 31.1 %all_to_all.16 = bf16[16,256,128]{2,1,0:T(8,128)(2,1)S(1)} all-to-all(bf16[16,256,128]{2,1,0:T(8,128)(2,1)S(1)} %bitcast.10), channel_id=1, replica_groups=mesh['y'=8,'x'=4,'zh'=4,'zl'=2,'core'=2] {'zh','x'}, dimensions={0} | all-to-all | bytes 2097152 | tf_op jit(solution)/shard_map/all_to_all | solution.py:362
  201.5 0.1 slice_reduce_fusion.3
  201.6 0.7 pad_maximum_fusion.1
  (18 shorter events, 0.1 us)
Async XLA Ops:
  0.0 1.4 copy-start
  1.4 0.7 copy-start.2
  4.3 48.9 %copy-start.1 = (bf16[3,7,512]{2,1,0:T(8,128)(2,1)S(1)}, bf16[3,7,512]{2,1,0:T(8,128)(2,1)}, u32[]{:S(2)}) copy-start(bf16[3,7,512]{2,1,0:T(8,128)(2,1)} %taps.5) | copy-start | bytes 64516
  4.3 48.9 %copy-start.4 = (s32[8]{0:T(128)S(1)}, s32[8]{0:T(128)}, u32[]{:S(2)}) copy-start(s32[8]{0:T(128)} %lengths.5) | copy-start | bytes 100
  53.2 5.2 %copy-start.7 = (bf16[128,32]{0,1:T(8,128)(2,1)S(1)}, bf16[128,32]{0,1:T(8,128)(2,1)}, u32[]{:S(2)}) copy-start(bf16[128,32]{0,1:T(8,128)(2,1)} %param.9) | copy-start | bytes 24580
  53.2 6.5 %copy-start.3 = (s32[32,16]{0,1:T(8,128)S(1)}, s32[32,16]{0,1:T(8,128)}, u32[]{:S(2)}) copy-start(s32[32,16]{0,1:T(8,128)} %param.13) | copy-start | bytes 6148
  55.6 5.7 %collective-permute-start = (bf16[152,512]{1,0:T(8,128)(2,1)S(1)}, bf16[152,512]{1,0:T(8,128)(2,1)S(1)}, u32[]{:S(2)}, u32[]{:S(2)}) collective-permute-start(bf16[152,512]{1,0:T(8,128)(2,1)S(1)} %get-tuple-element.15), channel_id=1, source_target_pairs={{0,16},{16,32},{32,48},{48,64},{64,80},{80,96},{96,112},{112,128},... | collective-permute-start | bytes 466952 | tf_op jit(solution)/shard_map/ppermute | solution.py:267
  59.7 1.6 copy-start.5
  64.2 4.3 %copy-start.6 = (bf16[512,256]{1,0:T(8,128)(2,1)S(1)}, bf16[512,256]{1,0:T(8,128)(2,1)}, u32[]{:S(2)}) copy-start(bf16[512,256]{1,0:T(8,128)(2,1)} %param.11) | copy-start | bytes 786436
  64.2 15.7 %all-to-all-start.1 = ((bf16[4,256,512]{2,1,0:T(8,128)(2,1)}), bf16[4,256,512]{2,1,0:T(8,128)(2,1)S(1)}, u32[]{:S(2)}, u32[]{:S(2)}) async-start(bf16[4,256,512]{2,1,0:T(8,128)(2,1)} %shard_map.76), calls=%async_computation.1 | async-start | bytes 2097152 | tf_op jit(solution)/shard_map/all_to_all | solution.py:351
  68.5 19.3 %collective-permute-start.2 = (bf16[512,128]{1,0:T(8,128)(2,1)S(1)}, bf16[512,128]{1,0:T(8,128)(2,1)S(1)}, u32[]{:S(2)}, u32[]{:S(2)}) collective-permute-start(bf16[512,128]{1,0:T(8,128)(2,1)S(1)} %get-tuple-element.29), channel_id=1, source_target_pairs={{0,0},{1,16},{16,32},{17,48},{32,1},{33,17},{48,33},{49,49},{2,2},... | collective-permute-start | bytes 393224 | tf_op jit(solution)/shard_map/ppermute | solution.py:280
  75.6 12.3 %collective-permute-start.3 = (bf16[512,128]{1,0:T(8,128)(2,1)S(1)}, bf16[512,128]{1,0:T(8,128)(2,1)S(1)}, u32[]{:S(2)}, u32[]{:S(2)}) collective-permute-start(bf16[512,128]{1,0:T(8,128)(2,1)S(1)} %get-tuple-element.30), channel_id=1, source_target_pairs={{0,16},{1,0},{16,48},{17,32},{32,17},{33,1},{48,49},{49,33},{2,18}... | collective-permute-start | bytes 393224 | tf_op jit(solution)/shard_map/ppermute | solution.py:281
  79.9 58.1 %collective-permute-start.1 = (bf16[1024,512]{1,0:T(8,128)(2,1)S(1)}, bf16[1024,512]{1,0:T(8,128)(2,1)S(1)}, u32[]{:S(2)}, u32[]{:S(2)}) collective-permute-start(bf16[1024,512]{1,0:T(8,128)(2,1)S(1)} %bitcast.7), channel_id=1, source_target_pairs={{0,1},{1,0},{2,3},{3,2},{4,5},{5,4},{6,7},{7,6},{8,9},{9,8},{10,11... | collective-permute-start | bytes 3145736 | tf_op jit(solution)/shard_map/ppermute | solution.py:353
  88.0 11.0 %collective-permute-start.4 = (bf16[1024,128]{1,0:T(8,128)(2,1)S(1)}, bf16[1024,128]{1,0:T(8,128)(2,1)S(1)}, u32[]{:S(2)}, u32[]{:S(2)}) collective-permute-start(bf16[1024,128]{1,0:T(8,128)(2,1)S(1)} %pad_maximum_fusion.refs_0_), channel_id=1, source_target_pairs={{0,64},{64,128},{128,192},{192,256},{256,320},{320,384},{384,448},... | collective-permute-start | bytes 786440 | tf_op jit(solution)/shard_map/ppermute | solution.py:290
  92.0 9.5 %collective-permute-start.5 = (bf16[1024,128]{1,0:T(8,128)(2,1)S(1)}, bf16[1024,128]{1,0:T(8,128)(2,1)S(1)}, u32[]{:S(2)}, u32[]{:S(2)}) collective-permute-start(bf16[1024,128]{1,0:T(8,128)(2,1)S(1)} %pad_maximum_fusion.refs_0_), channel_id=1, source_target_pairs={{0,448},{64,0},{128,64},{192,128},{256,192},{320,256},{384,320},{4... | collective-permute-start | bytes 786440 | tf_op jit(solution)/shard_map/ppermute | solution.py:290
  101.5 16.9 %collective-permute-start.10 = (bf16[512,128]{1,0:T(8,128)(2,1)S(1)}, bf16[512,128]{1,0:T(8,128)(2,1)S(1)}, u32[]{:S(2)}, u32[]{:S(2)}) collective-permute-start(bf16[512,128]{1,0:T(8,128)(2,1)S(1)} %slice.26), channel_id=1, source_target_pairs={{0,192},{64,256},{128,320},{192,384},{256,448},{320,0},{384,64},{4... | collective-permute-start | bytes 393224 | tf_op jit(solution)/shard_map/ppermute | solution.py:290
  109.1 11.7 %collective-permute-start.11 = (bf16[512,128]{1,0:T(8,128)(2,1)S(1)}, bf16[512,128]{1,0:T(8,128)(2,1)S(1)}, u32[]{:S(2)}, u32[]{:S(2)}) collective-permute-start(bf16[512,128]{1,0:T(8,128)(2,1)S(1)} %slice.27), channel_id=1, source_target_pairs={{0,320},{64,384},{128,448},{192,0},{256,64},{320,128},{384,192},{4... | collective-permute-start | bytes 393224 | tf_op jit(solution)/shard_map/ppermute | solution.py:290
  111.0 16.6 %collective-permute-start.8 = (bf16[1024,128]{1,0:T(8,128)(2,1)S(1)}, bf16[1024,128]{1,0:T(8,128)(2,1)S(1)}, u32[]{:S(2)}, u32[]{:S(2)}) collective-permute-start(bf16[1024,128]{1,0:T(8,128)(2,1)S(1)} %get-tuple-element.17), channel_id=1, source_target_pairs={{0,128},{64,192},{128,256},{192,320},{256,384},{320,448},{384,0},{... | collective-permute-start | bytes 786440 | tf_op jit(solution)/shard_map/ppermute | solution.py:290
  115.3 17.3 %collective-permute-start.9 = (bf16[1024,128]{1,0:T(8,128)(2,1)S(1)}, bf16[1024,128]{1,0:T(8,128)(2,1)S(1)}, u32[]{:S(2)}, u32[]{:S(2)}) collective-permute-start(bf16[1024,128]{1,0:T(8,128)(2,1)S(1)} %get-tuple-element.18), channel_id=1, source_target_pairs={{0,384},{64,448},{128,0},{192,64},{256,128},{320,192},{384,256},{4... | collective-permute-start | bytes 786440 | tf_op jit(solution)/shard_map/ppermute | solution.py:290
  118.4 16.1 %collective-permute-start.6 = (bf16[1024,128]{1,0:T(8,128)(2,1)S(1)}, bf16[1024,128]{1,0:T(8,128)(2,1)S(1)}, u32[]{:S(2)}, u32[]{:S(2)}) collective-permute-start(bf16[1024,128]{1,0:T(8,128)(2,1)S(1)} %collective-permute-done.4.up.refs_1_), channel_id=1, source_target_pairs={{0,64},{64,128},{128,192},{192,256},{256,320},{320,384},{384,448},... | collective-permute-start | bytes 786440 | tf_op jit(solution)/shard_map/ppermute | solution.py:290
  120.8 17.2 %collective-permute-start.7 = (bf16[1024,128]{1,0:T(8,128)(2,1)S(1)}, bf16[1024,128]{1,0:T(8,128)(2,1)S(1)}, u32[]{:S(2)}, u32[]{:S(2)}) collective-permute-start(bf16[1024,128]{1,0:T(8,128)(2,1)S(1)} %collective-permute-done.5.down.refs_2_), channel_id=1, source_target_pairs={{0,448},{64,0},{128,64},{192,128},{256,192},{320,256},{384,320},{4... | collective-permute-start | bytes 786440 | tf_op jit(solution)/shard_map/ppermute | solution.py:290
  141.1 20.9 %collective-permute-start.13 = (bf16[4,2,256,128]{3,2,1,0:T(8,128)(2,1)S(1)}, bf16[4,2,256,128]{3,2,1,0:T(8,128)(2,1)S(1)}, u32[]{:S(2)}, u32[]{:S(2)}) collective-permute-start(bf16[4,2,256,128]{3,2,1,0:T(8,128)(2,1)S(1)} %get-tuple-element.22), channel_id=1, source_target_pairs={{0,14},{2,0},{4,2},{6,4},{8,6},{10,8},{12,10},{14,12},{1,15},{3,1}... | collective-permute-start | bytes 1572872 | tf_op jit(solution)/shard_map/ppermute | solution.py:253
  154.9 15.3 %collective-permute-start.12 = (bf16[4,2,256,128]{3,2,1,0:T(8,128)(2,1)S(1)}, bf16[4,2,256,128]{3,2,1,0:T(8,128)(2,1)S(1)}, u32[]{:S(2)}, u32[]{:S(2)}) collective-permute-start(bf16[4,2,256,128]{3,2,1,0:T(8,128)(2,1)S(1)} %get-tuple-element.21), channel_id=1, source_target_pairs={{0,2},{2,4},{4,6},{6,8},{8,10},{10,12},{12,14},{14,0},{1,3},{3,5},... | collective-permute-start | bytes 1572872 | tf_op jit(solution)/shard_map/ppermute | solution.py:253

commit v8 on v7

--- a/solution.py
+++ b/solution.py
@@ -88,7 +88,6 @@
         cost_estimate=pl.CostEstimate(
             flops=10**6, bytes_accessed=4 * src.size, transcendentals=0
         ),
-        compiler_params=pltpu.CompilerParams(vmem_limit_bytes=GRANT),
         name="pack",
     )(bpd, src)
 
@@ -190,48 +189,69 @@
                 out[copy, b * HALF : (b + 1) * HALF, cols] = value
 
 
-def relay_kernel(up, down, up_out, down_out):
-    up_out[...] = up[...]
-    down_out[...] = down[...]
-
-
-def project_kernel(offsets, part, own, other, *refs):
-    weights, (same, cross) = refs[:-2], refs[-2:]
-    count, rows, lane = same.shape[1:]
-    n = len(weights) - 1
+def join_kernel(block, up, down, up_out, down_out):
+    rows = block.shape[0]
+    for first, out in ((up, up_out), (down, down_out)):
+        out[:rows] = block[...]
+        out[rows:] = first[...]
+
+
+def halve_kernel(up, down, up_out, down_out):
+    rows = up_out.shape[0]
+    up_out[...] = up[:rows]
+    down_out[...] = down[rows:]
+
+
+DISTANCES = ((0, 2, -2, 4), (1, -1, 3, -3))
+
+
+def project_kernel(parts, cross, own, other, *refs):
+    block, up, down, up23, down23, up4, down4 = refs[:7]
+    outs = refs[7:]
+    count, rows, lane = outs[0].shape[1:]
+    k = block.shape[0]
+    n = 2 * outs[0].shape[0]
+    load = {
+        0: lambda: block[...],
+        1: lambda: up[...],
+        -1: lambda: down[...],
+        2: lambda: up23[:k],
+        3: lambda: up23[k:],
+        -2: lambda: down23[:k],
+        -3: lambda: down23[k:],
+        4: lambda: jnp.concatenate([up4[...], down4[...]], axis=0),
+    }
     y = lax.axis_index("y")
-    at = slice(part * count * rows, (part + 1) * count * rows)
-    left = jnp.concatenate([own[at, :], other[at, :]], axis=1)
-    blocks = [w[...] for w in weights[:-2]]
-    blocks.append(jnp.concatenate([weights[-2][...], weights[-1][...]], axis=0))
-    for pair in range(0, n, 2):
-        wide = jnp.concatenate(blocks[pair : pair + 2], axis=1)
-        got = jnp.dot(left, wide, preferred_element_type=F32).astype(BF16)
-        for i in range(2):
-            owner = lax.rem(y - offsets[pair + i] + n, n)
-            high = lax.div(owner, 2)
-            odd = lax.rem(owner + lax.axis_index("zl"), 2)
-            piece = got[:, i * lane : (i + 1) * lane].reshape(count, rows, lane)
-
-            @pl.when(odd == 0)
-            def _():
-                same[high] = piece
-
-            @pl.when(odd == 1)
-            def _():
-                cross[high] = piece
-
-
-def project(part, own, other, weights, nx):
+    parity = lax.rem(y + lax.axis_index("zl"), 2)
+
+    def fill(distances):
+        for part, out in zip(parts, outs):
+            at = slice(part * count * rows, (part + 1) * count * rows)
+            left = jnp.concatenate([own[at, :], other[at, :]], axis=1)
+            for pair in (distances[:2], distances[2:]):
+                wide = jnp.concatenate([load[d]() for d in pair], axis=1)
+                got = jnp.dot(left, wide, preferred_element_type=F32).astype(BF16)
+                for i, d in enumerate(pair):
+                    high = lax.div(lax.rem(y - d + n, n), 2)
+                    piece = got[:, i * lane : (i + 1) * lane]
+                    out[high] = piece.reshape(count, rows, lane)
+
+    for odd in range(2):
+
+        @pl.when(lax.rem(parity + odd, 2) == cross)
+        def _():
+            fill(DISTANCES[odd])
+
+
+def project(parts, cross, own, other, weights, nx):
     rows = own.shape[0] // nx
-    blocks = [w[1] for w in weights]
-    lane = blocks[0].shape[1]
+    lane = weights[0].shape[1]
     return call(
-        functools.partial(project_kernel, tuple(w[0] for w in weights), part),
-        [shape(((len(blocks) - 1) // 2, nx // 2, rows, lane))] * 2,
-        [vmem()] * (2 + len(blocks)),
-        (own, other, *blocks),
-        2 * own.size * 8 * lane,
+        functools.partial(project_kernel, parts, cross),
+        [shape((len(DISTANCES[0]), nx // 2, rows, lane))] * len(parts),
+        [vmem()] * (2 + len(weights)),
+        (own, other, *weights),
+        4 * own.size * 2 * len(parts) * lane,
     )
 
 
@@ -310,13 +330,13 @@
 
     block = weight_columns(out_weight)
     up, down = around(block, 1), around(block, -1)
-    up2, down2 = around(up, 1), around(down, -1)
-    weights = [(0, block), (1, up), (-1, down), (2, up2), (-2, down2)]
-    both = [shape(up.shape)] * 2
-    up, down = call(relay_kernel, both, [vmem()] * 2, (up, down), 0)
-    cut = up.shape[0] // 2
-    weights += [(3, around(up, 2)), (-3, around(down, -2))]
-    weights += [(4, around(up[:cut], 3)), (4, around(down[cut:], -3))]
+    double = [shape((2 * block.shape[0], block.shape[1]))] * 2
+    ups, downs = call(join_kernel, double, [vmem()] * 3, (block, up, down), 0)
+    up23, down23 = around(ups, 2), around(downs, -2)
+    half = [shape((block.shape[0] // 2, block.shape[1]))] * 2
+    up4, down4 = call(halve_kernel, half, [vmem()] * 2, (up, down), 0)
+    up4, down4 = around(up4, 3), around(down4, -3)
+    weights = (block, up, down, up23, down23, up4, down4)
 
     groups = medium_filters.shape[1]
     line = jnp.pad(medium_filters[::-1].T.astype(F32), ((0, 0), (1, HALF - 1)))
@@ -351,12 +371,12 @@
     own = lax.all_to_all(copies, "x", split_axis=0, concat_axis=0, tiled=True)
     own = own.reshape(nx * rows, width)
     other = lax.ppermute(own, "core", [(0, 1), (1, 0)])
-    mine, got = [], []
+    got = []
     for part, distance in ((0, 1), (1, -1)):
-        same, cross = project(part, own, other, weights, nx)
-        mine.append(same)
+        (cross,) = project((part,), 1, own, other, weights, nx)
         got.append(along_z(cross, distance))
-    nzh, _, _, lane = mine[0].shape
+    mine = project((0, 1), 0, own, other, weights, nx)
+    nzh, half, _, lane = mine[0].shape
     (pairs,) = call(pair_kernel, [shape((nzh, nx, rows, lane))], [vmem()] * 4, (*mine, *got), 10**6)
     flat = pairs.reshape(nzh * nx, rows, lane)
     parts = lax.all_to_all(flat, ("zh", "x"), split_axis=0, concat_axis=0, tiled=True)

time: 203 us -> 203 us (level)
  the two profiles are of different devices: /device:TPU:1 before, /device:TPU:72 now
where the time goes in v8:
time: 203 us; the launch traced here: 202 us
  blocking collectives  87 us (43%)
  waiting for transfers between devices  54.7 us (27%)
  starting transfers between devices  44.8 us (22%)
  Pallas kernels  14.1 us (7%)
    all_to_all x1, blocking collectives, operator(): lax.all_to_all(packed, CTX, split_axis=0, concat_axis=0, tiled=True)  50 us
    all_to_all x1, blocking collectives, operator(): lax.all_to_all(flat, ('zh', 'x'), split_axis=0, concat_axis=0, tiled=True)  36.9 us
    ppermute x6, waiting for transfers between devices, around(): return lax.ppermute(block, 'y', [(i, (i + distance) % n) for i in range(n)])  32.1 us
    ppermute x6, starting transfers between devices, around(): return lax.ppermute(block, 'y', [(i, (i + distance) % n) for i in range(n)])  23.5 us
    ppermute x2, waiting for transfers between devices, along_z(): lax.ppermute(block, ('zh', 'zl'), [(i, (i + distance) % n) for i in range...  12.8 us
    pallas_call x10, Pallas kernels, call(): pl.pallas_call(body, out_shape=outs, in_specs=ins, out_specs=[vmem()] * l...  11.2 us
    ppermute x1, starting transfers between devices, weight_columns(): b = lax.ppermute(flip, ('x', 'core'), route(lambda i: 1 - i))  6.58 us
    ppermute x2, starting transfers between devices, along_z(): lax.ppermute(block, ('zh', 'zl'), [(i, (i + distance) % n) for i in range...  6.2 us
  transfers between devices with their start and end apart: 13, of which 8 were waited for; matrix products, arithmetic and copies ran while one was open for 0% of the time, Pallas kernels for 2%

profile of v8, /device:TPU:72, one launch (start us, length us, event | category | flops | bytes accessed | tf_op | source)
XLA Modules:
  0.0 202.0 jit_solution(302849544257109760)
XLA Ops:
  0.0 2.9 %pack.1 = bf16[32,3,16,512]{3,2,1,0:T(8,128)(2,1)} custom-call(s32[16,32]{1,0:T(8,128)} %bitcast.12, bf16[3,512,512]{2,1,0:T(8,128)(2,1)} %bitcast.17), custom_call_target="tpu_custom_call" | custom-call | flops 1000000 | bytes 3145728 | tf_op jit(solution)/shard_map/pack/pallas_call | solution.py:82
  2.9 0.0 copy-start
  2.9 0.0 copy-start.1
  2.9 0.0 copy-start.2
  2.9 50.0 %all_to_all.15.blocks = bf16[32,3,16,512]{3,2,1,0:T(8,128)(2,1)S(1)} all-to-all(bf16[32,3,16,512]{3,2,1,0:T(8,128)(2,1)} %pack.1), channel_id=1, replica_groups=mesh['y'=8,'x'=4,'zh'=4,'zl'=2,'core'=2] {'y','x'}, dimensions={0} | all-to-all | bytes 3145728 | tf_op jit(solution)/shard_map/all_to_all | solution.py:329
  53.0 0.0 copy-done.2
  53.0 0.0 copy-start.5
  53.0 2.4 %shard_map.73 = (bf16[256,512]{1,0:T(8,128)(2,1)S(1)}, bf16[152,512]{1,0:T(8,128)(2,1)S(1)}, bf16[24,512]{1,0:T(8,128)(2,1)S(1)}) custom-call(s32[16,32]{1,0:T(8,128)S(1)} %bitcast.13, s32[8]{0:T(128)S(1)} %copy-done.2, bf16[32,3,16,512]{3,2,1,0:T(8,128)(2,1)S(1)} %all_to_all.15.blocks, bf16[3,7,512]{2,1,0:T(8,128)(2,1)S(1)} %copy-done), custom_call_target="tpu_custom_call" | custom-call | flops 10000000 | bytes 2038816 | tf_op jit(solution)/shard_map/pallas_call | solution.py:35
  55.4 2.2 %collective-permute-start = (bf16[152,512]{1,0:T(8,128)(2,1)S(1)}, bf16[152,512]{1,0:T(8,128)(2,1)S(1)}, u32[]{:S(2)}, u32[]{:S(2)}) collective-permute-start(bf16[152,512]{1,0:T(8,128)(2,1)S(1)} %get-tuple-element.15), channel_id=1, source_target_pairs={{0,16},{16,32},{32,48},{48,64},{64,80},{80,96},{96,112},{112,128},... | collective-permute-start | bytes 466952 | tf_op jit(solution)/shard_map/ppermute | solution.py:287
  57.6 0.1 rev.3
  57.7 0.1 pad_convert_fusion.line
  57.8 1.1 shard_map.75.bands
  58.9 0.0 copy-start.3
  59.0 1.6 shard_map.74.query
  60.6 4.1 %collective-permute-done.recv = bf16[152,512]{1,0:T(8,128)(2,1)S(1)} collective-permute-done((bf16[152,512]{1,0:T(8,128)(2,1)S(1)}, bf16[152,512]{1,0:T(8,128)(2,1)S(1)}, u32[]{:S(2)}, u32[]{:S(2)}) %collective-permute-start) | collective-permute-done | bytes 155680 | tf_op jit(solution)/shard_map/ppermute | solution.py:287
  64.7 2.9 %shard_map.76 = bf16[4,256,512]{2,1,0:T(8,128)(2,1)} custom-call(s32[8]{0:T(128)S(1)} %copy-done.2, bf16[256,512]{1,0:T(8,128)(2,1)S(1)} %get-tuple-element.14.z, f32[256,512]{1,0:T(8,128)S(1)} %shard_map.74.query, bf16[152,512]{1,0:T(8,128)(2,1)S(1)} %collective-permute-done.recv, bf16[24,512]{1,0:T(8,128)(2,1)S(1)} %get-tuple-element.16.head, ...), custom_call_target="tpu_custom_call" | custom-call | flops 1000000000 | bytes 4135968 | tf_op jit(solution)/shard_map/pallas_call | solution.py:35
  67.5 3.6 %all-to-all-start.1 = ((bf16[4,256,512]{2,1,0:T(8,128)(2,1)}), bf16[4,256,512]{2,1,0:T(8,128)(2,1)S(1)}, u32[]{:S(2)}, u32[]{:S(2)}) async-start(bf16[4,256,512]{2,1,0:T(8,128)(2,1)} %shard_map.76), calls=%async_computation.1 | async-start | bytes 2097152 | tf_op jit(solution)/shard_map/all_to_all | solution.py:371
  71.2 0.7 collective-permute-start.2
  71.9 6.6 %collective-permute-start.3 = (bf16[512,128]{1,0:T(8,128)(2,1)S(1)}, bf16[512,128]{1,0:T(8,128)(2,1)S(1)}, u32[]{:S(2)}, u32[]{:S(2)}) collective-permute-start(bf16[512,128]{1,0:T(8,128)(2,1)S(1)} %get-tuple-element.30), channel_id=1, source_target_pairs={{0,16},{1,0},{16,48},{17,32},{32,17},{33,1},{48,49},{49,33},{2,18}... | collective-permute-start | bytes 393224 | tf_op jit(solution)/shard_map/ppermute | solution.py:301
  78.5 5.7 %all-to-all-done.1 = bf16[4,256,512]{2,1,0:T(8,128)(2,1)S(1)} async-done(((bf16[4,256,512]{2,1,0:T(8,128)(2,1)}), bf16[4,256,512]{2,1,0:T(8,128)(2,1)S(1)}, u32[]{:S(2)}, u32[]{:S(2)}) %all-to-all-start.1) | async-done | bytes 1048608 | tf_op jit(solution)/shard_map/all_to_all | solution.py:371
  84.2 1.9 collective-permute-start.1
  86.2 0.0 collective-permute-done.2
  86.2 0.0 collective-permute-done.3
  86.2 1.9 collective-permute-start.5
  88.2 3.9 %collective-permute-start.4 = (bf16[1024,128]{1,0:T(8,128)(2,1)S(1)}, bf16[1024,128]{1,0:T(8,128)(2,1)S(1)}, u32[]{:S(2)}, u32[]{:S(2)}) collective-permute-start(bf16[1024,128]{1,0:T(8,128)(2,1)S(1)} %pad_maximum_fusion.block.refs_0_), channel_id=1, source_target_pairs={{0,64},{64,128},{128,192},{192,256},{256,320},{320,384},{384,448},... | collective-permute-start | bytes 786440 | tf_op jit(solution)/shard_map/ppermute | solution.py:310
  92.1 4.7 %collective-permute-done.5.down.refs_2_ = bf16[1024,128]{1,0:T(8,128)(2,1)S(1)} collective-permute-done((bf16[1024,128]{1,0:T(8,128)(2,1)S(1)}, bf16[1024,128]{1,0:T(8,128)(2,1)S(1)}, u32[]{:S(2)}, u32[]{:S(2)}) %collective-permute-start.5) | collective-permute-done | bytes 262176 | tf_op jit(solution)/shard_map/ppermute | solution.py:310
  96.8 1.9 collective-permute-done.4.up.refs_1_
  98.8 0.1 shard_map.77
  98.8 4.7 %collective-permute-start.6 = (bf16[2048,128]{1,0:T(8,128)(2,1)S(1)}, bf16[2048,128]{1,0:T(8,128)(2,1)S(1)}, u32[]{:S(2)}, u32[]{:S(2)}) collective-permute-start(bf16[2048,128]{1,0:T(8,128)(2,1)S(1)} %get-tuple-element.17), channel_id=1, source_target_pairs={{0,128},{64,192},{128,256},{192,320},{256,384},{320,448},{384,0},{... | collective-permute-start | bytes 1572872 | tf_op jit(solution)/shard_map/ppermute | solution.py:310
  103.6 3.2 %collective-permute-start.7 = (bf16[2048,128]{1,0:T(8,128)(2,1)S(1)}, bf16[2048,128]{1,0:T(8,128)(2,1)S(1)}, u32[]{:S(2)}, u32[]{:S(2)}) collective-permute-start(bf16[2048,128]{1,0:T(8,128)(2,1)S(1)} %get-tuple-element.18), channel_id=1, source_target_pairs={{0,384},{64,448},{128,0},{192,64},{256,128},{320,192},{384,256},{4... | collective-permute-start | bytes 1572872 | tf_op jit(solution)/shard_map/ppermute | solution.py:310
  106.8 7.8 %collective-permute-start.8 = (bf16[512,128]{1,0:T(8,128)(2,1)S(1)}, bf16[512,128]{1,0:T(8,128)(2,1)S(1)}, u32[]{:S(2)}, u32[]{:S(2)}) collective-permute-start(bf16[512,128]{1,0:T(8,128)(2,1)S(1)} %get-tuple-element.19), channel_id=1, source_target_pairs={{0,192},{64,256},{128,320},{192,384},{256,448},{320,0},{384,64},{4... | collective-permute-start | bytes 393224 | tf_op jit(solution)/shard_map/ppermute | solution.py:310
  114.7 1.9 collective-permute-start.9
  116.6 21.2 %collective-permute-done.8.refs_5_ = bf16[512,128]{1,0:T(8,128)(2,1)S(1)} collective-permute-done((bf16[512,128]{1,0:T(8,128)(2,1)S(1)}, bf16[512,128]{1,0:T(8,128)(2,1)S(1)}, u32[]{:S(2)}, u32[]{:S(2)}) %collective-permute-start.8) | collective-permute-done | bytes 131104 | tf_op jit(solution)/shard_map/ppermute | solution.py:310
  137.8 4.2 %collective-permute-done.9.refs_6_ = bf16[512,128]{1,0:T(8,128)(2,1)S(1)} collective-permute-done((bf16[512,128]{1,0:T(8,128)(2,1)S(1)}, bf16[512,128]{1,0:T(8,128)(2,1)S(1)}, u32[]{:S(2)}, u32[]{:S(2)}) %collective-permute-start.9) | collective-permute-done | bytes 131104 | tf_op jit(solution)/shard_map/ppermute | solution.py:310
  142.0 0.0 collective-permute-done.6.refs_3_
  142.0 0.0 collective-permute-done.7.refs_4_
  142.0 0.0 collective-permute-done.1.other
  142.0 0.8 shard_map.80
  142.8 4.3 %collective-permute-start.10 = (bf16[4,2,256,128]{3,2,1,0:T(8,128)(2,1)S(1)}, bf16[4,2,256,128]{3,2,1,0:T(8,128)(2,1)S(1)}, u32[]{:S(2)}, u32[]{:S(2)}) collective-permute-start(bf16[4,2,256,128]{3,2,1,0:T(8,128)(2,1)S(1)} %shard_map.80), channel_id=1, source_target_pairs={{0,2},{2,4},{4,6},{6,8},{8,10},{10,12},{12,14},{14,0},{1,3},{3,5},... | collective-permute-start | bytes 1572872 | tf_op jit(solution)/shard_map/ppermute | solution.py:273
  147.1 0.8 shard_map.81
  147.8 1.9 collective-permute-start.11
  149.8 1.4 shard_map.79
  151.1 7.4 %collective-permute-done.10.got0 = bf16[4,2,256,128]{3,2,1,0:T(8,128)(2,1)S(1)} collective-permute-done((bf16[4,2,256,128]{3,2,1,0:T(8,128)(2,1)S(1)}, bf16[4,2,256,128]{3,2,1,0:T(8,128)(2,1)S(1)}, u32[]{:S(2)}, u32[]{:S(2)}) %collective-permute-start.10) | collective-permute-done | bytes 524320 | tf_op jit(solution)/shard_map/ppermute | solution.py:273
  158.5 5.4 %collective-permute-done.11.got1 = bf16[4,2,256,128]{3,2,1,0:T(8,128)(2,1)S(1)} collective-permute-done((bf16[4,2,256,128]{3,2,1,0:T(8,128)(2,1)S(1)}, bf16[4,2,256,128]{3,2,1,0:T(8,128)(2,1)S(1)}, u32[]{:S(2)}, u32[]{:S(2)}) %collective-permute-start.11) | collective-permute-done | bytes 524320 | tf_op jit(solution)/shard_map/ppermute | solution.py:273
  163.9 0.2 shard_map.82
  164.2 36.9 %all_to_all.16 = bf16[16,256,128]{2,1,0:T(8,128)(2,1)S(1)} all-to-all(bf16[16,256,128]{2,1,0:T(8,128)(2,1)S(1)} %bitcast.11), channel_id=1, replica_groups=mesh['y'=8,'x'=4,'zh'=4,'zl'=2,'core'=2] {'zh','x'}, dimensions={0} | all-to-all | bytes 2097152 | tf_op jit(solution)/shard_map/all_to_all | solution.py:382
  201.1 0.1 slice_reduce_fusion.3
  201.3 0.7 pad_maximum_fusion.1
  (10 shorter events, 0.1 us)
Async XLA Ops:
  2.9 50.1 %copy-start = (bf16[3,7,512]{2,1,0:T(8,128)(2,1)S(1)}, bf16[3,7,512]{2,1,0:T(8,128)(2,1)}, u32[]{:S(2)}) copy-start(bf16[3,7,512]{2,1,0:T(8,128)(2,1)} %taps.5) | copy-start | bytes 64516
  2.9 50.1 %copy-start.1 = (s32[32,16]{0,1:T(8,128)S(1)}, s32[32,16]{0,1:T(8,128)}, u32[]{:S(2)}) copy-start(s32[32,16]{0,1:T(8,128)} %param.13) | copy-start | bytes 6148
  2.9 50.1 %copy-start.2 = (s32[8]{0:T(128)S(1)}, s32[8]{0:T(128)}, u32[]{:S(2)}) copy-start(s32[8]{0:T(128)} %lengths.5) | copy-start | bytes 100
  53.0 4.6 %copy-start.5 = (bf16[128,32]{0,1:T(8,128)(2,1)S(1)}, bf16[128,32]{0,1:T(8,128)(2,1)}, u32[]{:S(2)}) copy-start(bf16[128,32]{0,1:T(8,128)(2,1)} %param.9) | copy-start | bytes 24580
  55.4 9.2 %collective-permute-start = (bf16[152,512]{1,0:T(8,128)(2,1)S(1)}, bf16[152,512]{1,0:T(8,128)(2,1)S(1)}, u32[]{:S(2)}, u32[]{:S(2)}) collective-permute-start(bf16[152,512]{1,0:T(8,128)(2,1)S(1)} %get-tuple-element.15), channel_id=1, source_target_pairs={{0,16},{16,32},{32,48},{48,64},{64,80},{80,96},{96,112},{112,128},... | collective-permute-start | bytes 466952 | tf_op jit(solution)/shard_map/ppermute | solution.py:287
  58.9 5.7 %copy-start.3 = (f32[512]{0:T(512)S(1)}, f32[512]{0:T(512)}, u32[]{:S(2)}) copy-start(f32[512]{0:T(512)} %param.10) | copy-start | bytes 6148
  67.5 3.7 %copy-start.4 = (bf16[512,256]{1,0:T(8,128)(2,1)S(1)}, bf16[512,256]{1,0:T(8,128)(2,1)}, u32[]{:S(2)}) copy-start(bf16[512,256]{1,0:T(8,128)(2,1)} %param.11) | copy-start | bytes 786436
  67.5 16.7 %all-to-all-start.1 = ((bf16[4,256,512]{2,1,0:T(8,128)(2,1)}), bf16[4,256,512]{2,1,0:T(8,128)(2,1)S(1)}, u32[]{:S(2)}, u32[]{:S(2)}) async-start(bf16[4,256,512]{2,1,0:T(8,128)(2,1)} %shard_map.76), calls=%async_computation.1 | async-start | bytes 2097152 | tf_op jit(solution)/shard_map/all_to_all | solution.py:371
  71.2 14.9 %collective-permute-start.2 = (bf16[512,128]{1,0:T(8,128)(2,1)S(1)}, bf16[512,128]{1,0:T(8,128)(2,1)S(1)}, u32[]{:S(2)}, u32[]{:S(2)}) collective-permute-start(bf16[512,128]{1,0:T(8,128)(2,1)S(1)} %get-tuple-element.29), channel_id=1, source_target_pairs={{0,0},{1,16},{16,32},{17,48},{32,1},{33,17},{48,33},{49,49},{2,2},... | collective-permute-start | bytes 393224 | tf_op jit(solution)/shard_map/ppermute | solution.py:300
  71.9 14.3 %collective-permute-start.3 = (bf16[512,128]{1,0:T(8,128)(2,1)S(1)}, bf16[512,128]{1,0:T(8,128)(2,1)S(1)}, u32[]{:S(2)}, u32[]{:S(2)}) collective-permute-start(bf16[512,128]{1,0:T(8,128)(2,1)S(1)} %get-tuple-element.30), channel_id=1, source_target_pairs={{0,16},{1,0},{16,48},{17,32},{32,17},{33,1},{48,49},{49,33},{2,18}... | collective-permute-start | bytes 393224 | tf_op jit(solution)/shard_map/ppermute | solution.py:301
  84.2 57.8 %collective-permute-start.1 = (bf16[1024,512]{1,0:T(8,128)(2,1)S(1)}, bf16[1024,512]{1,0:T(8,128)(2,1)S(1)}, u32[]{:S(2)}, u32[]{:S(2)}) collective-permute-start(bf16[1024,512]{1,0:T(8,128)(2,1)S(1)} %bitcast.7), channel_id=1, source_target_pairs={{0,1},{1,0},{2,3},{3,2},{4,5},{5,4},{6,7},{7,6},{8,9},{9,8},{10,11... | collective-permute-start | bytes 3145736 | tf_op jit(solution)/shard_map/ppermute | solution.py:373
  86.2 10.6 %collective-permute-start.5 = (bf16[1024,128]{1,0:T(8,128)(2,1)S(1)}, bf16[1024,128]{1,0:T(8,128)(2,1)S(1)}, u32[]{:S(2)}, u32[]{:S(2)}) collective-permute-start(bf16[1024,128]{1,0:T(8,128)(2,1)S(1)} %pad_maximum_fusion.block.refs_0_), channel_id=1, source_target_pairs={{0,448},{64,0},{128,64},{192,128},{256,192},{320,256},{384,320},{4... | collective-permute-start | bytes 786440 | tf_op jit(solution)/shard_map/ppermute | solution.py:310
  88.2 10.6 %collective-permute-start.4 = (bf16[1024,128]{1,0:T(8,128)(2,1)S(1)}, bf16[1024,128]{1,0:T(8,128)(2,1)S(1)}, u32[]{:S(2)}, u32[]{:S(2)}) collective-permute-start(bf16[1024,128]{1,0:T(8,128)(2,1)S(1)} %pad_maximum_fusion.block.refs_0_), channel_id=1, source_target_pairs={{0,64},{64,128},{128,192},{192,256},{256,320},{320,384},{384,448},... | collective-permute-start | bytes 786440 | tf_op jit(solution)/shard_map/ppermute | solution.py:310
  98.8 43.1 %collective-permute-start.6 = (bf16[2048,128]{1,0:T(8,128)(2,1)S(1)}, bf16[2048,128]{1,0:T(8,128)(2,1)S(1)}, u32[]{:S(2)}, u32[]{:S(2)}) collective-permute-start(bf16[2048,128]{1,0:T(8,128)(2,1)S(1)} %get-tuple-element.17), channel_id=1, source_target_pairs={{0,128},{64,192},{128,256},{192,320},{256,384},{320,448},{384,0},{... | collective-permute-start | bytes 1572872 | tf_op jit(solution)/shard_map/ppermute | solution.py:310
  103.6 38.4 %collective-permute-start.7 = (bf16[2048,128]{1,0:T(8,128)(2,1)S(1)}, bf16[2048,128]{1,0:T(8,128)(2,1)S(1)}, u32[]{:S(2)}, u32[]{:S(2)}) collective-permute-start(bf16[2048,128]{1,0:T(8,128)(2,1)S(1)} %get-tuple-element.18), channel_id=1, source_target_pairs={{0,384},{64,448},{128,0},{192,64},{256,128},{320,192},{384,256},{4... | collective-permute-start | bytes 1572872 | tf_op jit(solution)/shard_map/ppermute | solution.py:310
  106.8 31.0 %collective-permute-start.8 = (bf16[512,128]{1,0:T(8,128)(2,1)S(1)}, bf16[512,128]{1,0:T(8,128)(2,1)S(1)}, u32[]{:S(2)}, u32[]{:S(2)}) collective-permute-start(bf16[512,128]{1,0:T(8,128)(2,1)S(1)} %get-tuple-element.19), channel_id=1, source_target_pairs={{0,192},{64,256},{128,320},{192,384},{256,448},{320,0},{384,64},{4... | collective-permute-start | bytes 393224 | tf_op jit(solution)/shard_map/ppermute | solution.py:310
  114.7 27.3 %collective-permute-start.9 = (bf16[512,128]{1,0:T(8,128)(2,1)S(1)}, bf16[512,128]{1,0:T(8,128)(2,1)S(1)}, u32[]{:S(2)}, u32[]{:S(2)}) collective-permute-start(bf16[512,128]{1,0:T(8,128)(2,1)S(1)} %get-tuple-element.20), channel_id=1, source_target_pairs={{0,320},{64,384},{128,448},{192,0},{256,64},{320,128},{384,192},{4... | collective-permute-start | bytes 393224 | tf_op jit(solution)/shard_map/ppermute | solution.py:310
  142.8 15.7 %collective-permute-start.10 = (bf16[4,2,256,128]{3,2,1,0:T(8,128)(2,1)S(1)}, bf16[4,2,256,128]{3,2,1,0:T(8,128)(2,1)S(1)}, u32[]{:S(2)}, u32[]{:S(2)}) collective-permute-start(bf16[4,2,256,128]{3,2,1,0:T(8,128)(2,1)S(1)} %shard_map.80), channel_id=1, source_target_pairs={{0,2},{2,4},{4,6},{6,8},{8,10},{10,12},{12,14},{14,0},{1,3},{3,5},... | collective-permute-start | bytes 1572872 | tf_op jit(solution)/shard_map/ppermute | solution.py:273
  147.8 16.1 %collective-permute-start.11 = (bf16[4,2,256,128]{3,2,1,0:T(8,128)(2,1)S(1)}, bf16[4,2,256,128]{3,2,1,0:T(8,128)(2,1)S(1)}, u32[]{:S(2)}, u32[]{:S(2)}) collective-permute-start(bf16[4,2,256,128]{3,2,1,0:T(8,128)(2,1)S(1)} %shard_map.81), channel_id=1, source_target_pairs={{0,14},{2,0},{4,2},{6,4},{8,6},{10,8},{12,10},{14,12},{1,15},{3,1}... | collective-permute-start | bytes 1572872 | tf_op jit(solution)/shard_map/ppermute | solution.py:273

commit v9 on v8

--- a/solution.py
+++ b/solution.py
@@ -189,36 +189,30 @@
                 out[copy, b * HALF : (b + 1) * HALF, cols] = value
 
 
-def join_kernel(block, up, down, up_out, down_out):
-    rows = block.shape[0]
-    for first, out in ((up, up_out), (down, down_out)):
-        out[:rows] = block[...]
-        out[rows:] = first[...]
-
-
-def halve_kernel(up, down, up_out, down_out):
-    rows = up_out.shape[0]
-    up_out[...] = up[:rows]
-    down_out[...] = down[rows:]
+def relay_kernel(up, down, up_out, down_out, up_half, down_half):
+    rows = up_half.shape[0]
+    up_out[...] = up[...]
+    down_out[...] = down[...]
+    up_half[...] = up[:rows]
+    down_half[...] = down[rows:]
 
 
 DISTANCES = ((0, 2, -2, 4), (1, -1, 3, -3))
 
 
 def project_kernel(parts, cross, own, other, *refs):
-    block, up, down, up23, down23, up4, down4 = refs[:7]
-    outs = refs[7:]
+    block, up, down, up2, down2, up3, down3, up4, down4 = refs[:9]
+    outs = refs[9:]
     count, rows, lane = outs[0].shape[1:]
-    k = block.shape[0]
     n = 2 * outs[0].shape[0]
     load = {
         0: lambda: block[...],
         1: lambda: up[...],
         -1: lambda: down[...],
-        2: lambda: up23[:k],
-        3: lambda: up23[k:],
-        -2: lambda: down23[:k],
-        -3: lambda: down23[k:],
+        2: lambda: up2[...],
+        -2: lambda: down2[...],
+        3: lambda: up3[...],
+        -3: lambda: down3[...],
         4: lambda: jnp.concatenate([up4[...], down4[...]], axis=0),
     }
     y = lax.axis_index("y")
@@ -330,13 +324,13 @@
 
     block = weight_columns(out_weight)
     up, down = around(block, 1), around(block, -1)
-    double = [shape((2 * block.shape[0], block.shape[1]))] * 2
-    ups, downs = call(join_kernel, double, [vmem()] * 3, (block, up, down), 0)
-    up23, down23 = around(ups, 2), around(downs, -2)
-    half = [shape((block.shape[0] // 2, block.shape[1]))] * 2
-    up4, down4 = call(halve_kernel, half, [vmem()] * 2, (up, down), 0)
-    up4, down4 = around(up4, 3), around(down4, -3)
-    weights = (block, up, down, up23, down23, up4, down4)
+    up2, down2 = around(block, 2), around(block, -2)
+    whole = shape(block.shape)
+    half = shape((block.shape[0] // 2, block.shape[1]))
+    relayed = call(relay_kernel, [whole, whole, half, half], [vmem()] * 2, (up2, down2), 0)
+    up3, down3 = around(relayed[0], 1), around(relayed[1], -1)
+    up4, down4 = around(relayed[2], 2), around(relayed[3], -2)
+    weights = (block, up, down, up2, down2, up3, down3, up4, down4)
 
     groups = medium_filters.shape[1]
     line = jnp.pad(medium_filters[::-1].T.astype(F32), ((0, 0), (1, HALF - 1)))

time: 203 us -> 196 us (0.966)
  the two profiles are of different devices: /device:TPU:72 before, /device:TPU:64 now
where the time goes in v9:
time: 196 us
  blocking collectives  87 us (44%)
  starting transfers between devices  49.2 us (25%)
  waiting for transfers between devices  43.9 us (22%)
  Pallas kernels  14.1 us (7%)
    all_to_all x1, blocking collectives, operator(): lax.all_to_all(packed, CTX, split_axis=0, concat_axis=0, tiled=True)  50.5 us
    all_to_all x1, blocking collectives, operator(): lax.all_to_all(flat, ('zh', 'x'), split_axis=0, concat_axis=0, tiled=True)  36.5 us
    ppermute x8, starting transfers between devices, around(): return lax.ppermute(block, 'y', [(i, (i + distance) % n) for i in range(n)])  29 us
    ppermute x8, waiting for transfers between devices, around(): return lax.ppermute(block, 'y', [(i, (i + distance) % n) for i in range(n)])  16 us
    ppermute x2, waiting for transfers between devices, along_z(): lax.ppermute(block, ('zh', 'zl'), [(i, (i + distance) % n) for i in range...  12.9 us
    all_to_all x1, waiting for transfers between devices, operator(): own = lax.all_to_all(copies, 'x', split_axis=0, concat_axis=0, tiled=True)  12.6 us
    pallas_call x9, Pallas kernels, call(): pl.pallas_call(body, out_shape=outs, in_specs=ins, out_specs=[vmem()] * l...  11.2 us
    ppermute x2, starting transfers between devices, along_z(): lax.ppermute(block, ('zh', 'zl'), [(i, (i + distance) % n) for i in range...  6.21 us
  transfers between devices with their start and end apart: 15, of which 8 were waited for; matrix products, arithmetic and copies ran while one was open for 0% of the time, Pallas kernels for 3%

profile of v9, /device:TPU:64, one launch (start us, length us, event | category | flops | bytes accessed | tf_op | source)
XLA Modules:
  0.0 195.7 jit_solution(7659872515695817963)
XLA Ops:
  0.0 2.9 %pack.1 = bf16[32,3,16,512]{3,2,1,0:T(8,128)(2,1)} custom-call(s32[16,32]{1,0:T(8,128)} %bitcast.12, bf16[3,512,512]{2,1,0:T(8,128)(2,1)} %bitcast.17), custom_call_target="tpu_custom_call" | custom-call | flops 1000000 | bytes 3145728 | tf_op jit(solution)/shard_map/pack/pallas_call | solution.py:82
  2.9 0.0 copy-start
  2.9 0.0 copy-start.1
  2.9 0.0 copy-start.2
  3.0 50.5 %all_to_all.15.blocks = bf16[32,3,16,512]{3,2,1,0:T(8,128)(2,1)S(1)} all-to-all(bf16[32,3,16,512]{3,2,1,0:T(8,128)(2,1)} %pack.1), channel_id=1, replica_groups=mesh['y'=8,'x'=4,'zh'=4,'zl'=2,'core'=2] {'y','x'}, dimensions={0} | all-to-all | bytes 3145728 | tf_op jit(solution)/shard_map/all_to_all | solution.py:323
  53.5 0.0 copy-start.5
  53.5 2.4 %shard_map.73 = (bf16[256,512]{1,0:T(8,128)(2,1)S(1)}, bf16[152,512]{1,0:T(8,128)(2,1)S(1)}, bf16[24,512]{1,0:T(8,128)(2,1)S(1)}) custom-call(s32[16,32]{1,0:T(8,128)S(1)} %bitcast.13, s32[8]{0:T(128)S(1)} %copy-done.2, bf16[32,3,16,512]{3,2,1,0:T(8,128)(2,1)S(1)} %all_to_all.15.blocks, bf16[3,7,512]{2,1,0:T(8,128)(2,1)S(1)} %copy-done), custom_call_target="tpu_custom_call" | custom-call | flops 10000000 | bytes 2038816 | tf_op jit(solution)/shard_map/pallas_call | solution.py:35
  55.9 2.6 %collective-permute-start = (bf16[152,512]{1,0:T(8,128)(2,1)S(1)}, bf16[152,512]{1,0:T(8,128)(2,1)S(1)}, u32[]{:S(2)}, u32[]{:S(2)}) collective-permute-start(bf16[152,512]{1,0:T(8,128)(2,1)S(1)} %get-tuple-element.15), channel_id=1, source_target_pairs={{0,16},{16,32},{32,48},{48,64},{64,80},{80,96},{96,112},{112,128},... | collective-permute-start | bytes 466952 | tf_op jit(solution)/shard_map/ppermute | solution.py:281
  58.5 0.1 rev.3
  58.6 0.1 pad_convert_fusion.line
  58.7 1.1 shard_map.75.bands
  59.8 0.0 copy-start.3
  59.8 1.6 shard_map.74.query
  61.4 2.9 %shard_map.76 = bf16[4,256,512]{2,1,0:T(8,128)(2,1)} custom-call(s32[8]{0:T(128)S(1)} %copy-done.2, bf16[256,512]{1,0:T(8,128)(2,1)S(1)} %get-tuple-element.14.z, f32[256,512]{1,0:T(8,128)S(1)} %shard_map.74.query, bf16[152,512]{1,0:T(8,128)(2,1)S(1)} %collective-permute-done.recv, bf16[24,512]{1,0:T(8,128)(2,1)S(1)} %get-tuple-element.16.head, ...), custom_call_target="tpu_custom_call" | custom-call | flops 1000000000 | bytes 4135968 | tf_op jit(solution)/shard_map/pallas_call | solution.py:35
  64.3 5.2 %all-to-all-start.1 = ((bf16[4,256,512]{2,1,0:T(8,128)(2,1)}), bf16[4,256,512]{2,1,0:T(8,128)(2,1)S(1)}, u32[]{:S(2)}, u32[]{:S(2)}) async-start(bf16[4,256,512]{2,1,0:T(8,128)(2,1)} %shard_map.76), calls=%async_computation.1 | async-start | bytes 2097152 | tf_op jit(solution)/shard_map/all_to_all | solution.py:365
  69.5 12.6 %all-to-all-done.1 = bf16[4,256,512]{2,1,0:T(8,128)(2,1)S(1)} async-done(((bf16[4,256,512]{2,1,0:T(8,128)(2,1)}), bf16[4,256,512]{2,1,0:T(8,128)(2,1)S(1)}, u32[]{:S(2)}, u32[]{:S(2)}) %all-to-all-start.1) | async-done | bytes 1048608 | tf_op jit(solution)/shard_map/all_to_all | solution.py:365
  82.0 1.9 collective-permute-start.1
  84.0 0.7 collective-permute-start.2
  84.7 3.7 %collective-permute-start.3 = (bf16[512,128]{1,0:T(8,128)(2,1)S(1)}, bf16[512,128]{1,0:T(8,128)(2,1)S(1)}, u32[]{:S(2)}, u32[]{:S(2)}) collective-permute-start(bf16[512,128]{1,0:T(8,128)(2,1)S(1)} %get-tuple-element.30), channel_id=1, source_target_pairs={{0,16},{1,0},{16,48},{17,32},{32,17},{33,1},{48,49},{49,33},{2,18}... | collective-permute-start | bytes 393224 | tf_op jit(solution)/shard_map/ppermute | solution.py:295
  88.4 2.5 %collective-permute-done.3 = bf16[512,128]{1,0:T(8,128)(2,1)S(1)} collective-permute-done((bf16[512,128]{1,0:T(8,128)(2,1)S(1)}, bf16[512,128]{1,0:T(8,128)(2,1)S(1)}, u32[]{:S(2)}, u32[]{:S(2)}) %collective-permute-start.3) | collective-permute-done | bytes 131104 | tf_op jit(solution)/shard_map/ppermute | solution.py:295
  91.0 5.5 %collective-permute-start.7 = (bf16[1024,128]{1,0:T(8,128)(2,1)S(1)}, bf16[1024,128]{1,0:T(8,128)(2,1)S(1)}, u32[]{:S(2)}, u32[]{:S(2)}) collective-permute-start(bf16[1024,128]{1,0:T(8,128)(2,1)S(1)} %pad_maximum_fusion.refs_0_), channel_id=1, source_target_pairs={{0,384},{64,448},{128,0},{192,64},{256,128},{320,192},{384,256},{4... | collective-permute-start | bytes 786440 | tf_op jit(solution)/shard_map/ppermute | solution.py:304
  96.4 1.9 collective-permute-start.6
  98.4 4.6 %collective-permute-start.5 = (bf16[1024,128]{1,0:T(8,128)(2,1)S(1)}, bf16[1024,128]{1,0:T(8,128)(2,1)S(1)}, u32[]{:S(2)}, u32[]{:S(2)}) collective-permute-start(bf16[1024,128]{1,0:T(8,128)(2,1)S(1)} %pad_maximum_fusion.refs_0_), channel_id=1, source_target_pairs={{0,448},{64,0},{128,64},{192,128},{256,192},{320,256},{384,320},{4... | collective-permute-start | bytes 786440 | tf_op jit(solution)/shard_map/ppermute | solution.py:304
  103.0 1.9 collective-permute-start.4
  104.9 2.8 %collective-permute-done.7.down.refs_4_ = bf16[1024,128]{1,0:T(8,128)(2,1)S(1)} collective-permute-done((bf16[1024,128]{1,0:T(8,128)(2,1)S(1)}, bf16[1024,128]{1,0:T(8,128)(2,1)S(1)}, u32[]{:S(2)}, u32[]{:S(2)}) %collective-permute-start.7) | collective-permute-done | bytes 262176 | tf_op jit(solution)/shard_map/ppermute | solution.py:304
  107.8 6.0 %collective-permute-done.6.up.refs_3_ = bf16[1024,128]{1,0:T(8,128)(2,1)S(1)} collective-permute-done((bf16[1024,128]{1,0:T(8,128)(2,1)S(1)}, bf16[1024,128]{1,0:T(8,128)(2,1)S(1)}, u32[]{:S(2)}, u32[]{:S(2)}) %collective-permute-start.6) | collective-permute-done | bytes 262176 | tf_op jit(solution)/shard_map/ppermute | solution.py:304
  113.8 0.1 shard_map.77
  113.9 1.9 collective-permute-start.8
  115.8 5.1 %collective-permute-start.9 = (bf16[1024,128]{1,0:T(8,128)(2,1)S(1)}, bf16[1024,128]{1,0:T(8,128)(2,1)S(1)}, u32[]{:S(2)}, u32[]{:S(2)}) collective-permute-start(bf16[1024,128]{1,0:T(8,128)(2,1)S(1)} %get-tuple-element.18), channel_id=1, source_target_pairs={{0,448},{64,0},{128,64},{192,128},{256,192},{320,256},{384,320},{4... | collective-permute-start | bytes 786440 | tf_op jit(solution)/shard_map/ppermute | solution.py:304
  121.0 1.9 collective-permute-start.10
  122.9 0.0 collective-permute-done.4.refs_1_
  122.9 6.0 %collective-permute-start.11 = (bf16[512,128]{1,0:T(8,128)(2,1)S(1)}, bf16[512,128]{1,0:T(8,128)(2,1)S(1)}, u32[]{:S(2)}, u32[]{:S(2)}) collective-permute-start(bf16[512,128]{1,0:T(8,128)(2,1)S(1)} %get-tuple-element.20), channel_id=1, source_target_pairs={{0,384},{64,448},{128,0},{192,64},{256,128},{320,192},{384,256},{4... | collective-permute-start | bytes 393224 | tf_op jit(solution)/shard_map/ppermute | solution.py:304
  129.0 3.7 %collective-permute-done.10.refs_7_ = bf16[512,128]{1,0:T(8,128)(2,1)S(1)} collective-permute-done((bf16[512,128]{1,0:T(8,128)(2,1)S(1)}, bf16[512,128]{1,0:T(8,128)(2,1)S(1)}, u32[]{:S(2)}, u32[]{:S(2)}) %collective-permute-start.10) | collective-permute-done | bytes 131104 | tf_op jit(solution)/shard_map/ppermute | solution.py:304
  132.7 3.4 %collective-permute-done.11.refs_8_ = bf16[512,128]{1,0:T(8,128)(2,1)S(1)} collective-permute-done((bf16[512,128]{1,0:T(8,128)(2,1)S(1)}, bf16[512,128]{1,0:T(8,128)(2,1)S(1)}, u32[]{:S(2)}, u32[]{:S(2)}) %collective-permute-start.11) | collective-permute-done | bytes 131104 | tf_op jit(solution)/shard_map/ppermute | solution.py:304
  136.1 0.0 collective-permute-done.8.refs_5_
  136.1 0.0 collective-permute-done.9.refs_6_
  136.1 0.0 collective-permute-done.1.other
  136.1 0.8 shard_map.79
  136.8 4.3 %collective-permute-start.12 = (bf16[4,2,256,128]{3,2,1,0:T(8,128)(2,1)S(1)}, bf16[4,2,256,128]{3,2,1,0:T(8,128)(2,1)S(1)}, u32[]{:S(2)}, u32[]{:S(2)}) collective-permute-start(bf16[4,2,256,128]{3,2,1,0:T(8,128)(2,1)S(1)} %shard_map.79), channel_id=1, source_target_pairs={{0,2},{2,4},{4,6},{6,8},{8,10},{10,12},{12,14},{14,0},{1,3},{3,5},... | collective-permute-start | bytes 1572872 | tf_op jit(solution)/shard_map/ppermute | solution.py:267
  141.1 0.8 shard_map.80
  141.9 1.9 collective-permute-start.13
  143.8 1.4 shard_map.78
  145.2 7.5 %collective-permute-done.12.got0 = bf16[4,2,256,128]{3,2,1,0:T(8,128)(2,1)S(1)} collective-permute-done((bf16[4,2,256,128]{3,2,1,0:T(8,128)(2,1)S(1)}, bf16[4,2,256,128]{3,2,1,0:T(8,128)(2,1)S(1)}, u32[]{:S(2)}, u32[]{:S(2)}) %collective-permute-start.12) | collective-permute-done | bytes 524320 | tf_op jit(solution)/shard_map/ppermute | solution.py:267
  152.7 5.4 %collective-permute-done.13.got1 = bf16[4,2,256,128]{3,2,1,0:T(8,128)(2,1)S(1)} collective-permute-done((bf16[4,2,256,128]{3,2,1,0:T(8,128)(2,1)S(1)}, bf16[4,2,256,128]{3,2,1,0:T(8,128)(2,1)S(1)}, u32[]{:S(2)}, u32[]{:S(2)}) %collective-permute-start.13) | collective-permute-done | bytes 524320 | tf_op jit(solution)/shard_map/ppermute | solution.py:267
  158.1 0.2 shard_map.81
  158.4 36.5 %all_to_all.16 = bf16[16,256,128]{2,1,0:T(8,128)(2,1)S(1)} all-to-all(bf16[16,256,128]{2,1,0:T(8,128)(2,1)S(1)} %bitcast.11), channel_id=1, replica_groups=mesh['y'=8,'x'=4,'zh'=4,'zl'=2,'core'=2] {'zh','x'}, dimensions={0} | all-to-all | bytes 2097152 | tf_op jit(solution)/shard_map/all_to_all | solution.py:376
  194.8 0.1 slice_reduce_fusion.3
  195.0 0.7 pad_maximum_fusion.1
  (13 shorter events, 0.1 us)
Async XLA Ops:
  2.9 50.5 %copy-start = (bf16[3,7,512]{2,1,0:T(8,128)(2,1)S(1)}, bf16[3,7,512]{2,1,0:T(8,128)(2,1)}, u32[]{:S(2)}) copy-start(bf16[3,7,512]{2,1,0:T(8,128)(2,1)} %taps.5) | copy-start | bytes 64516
  2.9 50.5 %copy-start.1 = (s32[32,16]{0,1:T(8,128)S(1)}, s32[32,16]{0,1:T(8,128)}, u32[]{:S(2)}) copy-start(s32[32,16]{0,1:T(8,128)} %param.13) | copy-start | bytes 6148
  2.9 50.5 %copy-start.2 = (s32[8]{0:T(128)S(1)}, s32[8]{0:T(128)}, u32[]{:S(2)}) copy-start(s32[8]{0:T(128)} %lengths.5) | copy-start | bytes 100
  53.5 5.0 %copy-start.5 = (bf16[128,32]{0,1:T(8,128)(2,1)S(1)}, bf16[128,32]{0,1:T(8,128)(2,1)}, u32[]{:S(2)}) copy-start(bf16[128,32]{0,1:T(8,128)(2,1)} %param.9) | copy-start | bytes 24580
  55.9 5.5 %collective-permute-start = (bf16[152,512]{1,0:T(8,128)(2,1)S(1)}, bf16[152,512]{1,0:T(8,128)(2,1)S(1)}, u32[]{:S(2)}, u32[]{:S(2)}) collective-permute-start(bf16[152,512]{1,0:T(8,128)(2,1)S(1)} %get-tuple-element.15), channel_id=1, source_target_pairs={{0,16},{16,32},{32,48},{48,64},{64,80},{80,96},{96,112},{112,128},... | collective-permute-start | bytes 466952 | tf_op jit(solution)/shard_map/ppermute | solution.py:281
  59.8 1.6 copy-start.3
  64.3 19.6 %copy-start.4 = (bf16[512,256]{1,0:T(8,128)(2,1)S(1)}, bf16[512,256]{1,0:T(8,128)(2,1)}, u32[]{:S(2)}) copy-start(bf16[512,256]{1,0:T(8,128)(2,1)} %param.11) | copy-start | bytes 786436
  64.3 17.7 %all-to-all-start.1 = ((bf16[4,256,512]{2,1,0:T(8,128)(2,1)}), bf16[4,256,512]{2,1,0:T(8,128)(2,1)S(1)}, u32[]{:S(2)}, u32[]{:S(2)}) async-start(bf16[4,256,512]{2,1,0:T(8,128)(2,1)} %shard_map.76), calls=%async_computation.1 | async-start | bytes 2097152 | tf_op jit(solution)/shard_map/all_to_all | solution.py:365
  82.0 54.0 %collective-permute-start.1 = (bf16[1024,512]{1,0:T(8,128)(2,1)S(1)}, bf16[1024,512]{1,0:T(8,128)(2,1)S(1)}, u32[]{:S(2)}, u32[]{:S(2)}) collective-permute-start(bf16[1024,512]{1,0:T(8,128)(2,1)S(1)} %bitcast.7), channel_id=1, source_target_pairs={{0,1},{1,0},{2,3},{3,2},{4,5},{5,4},{6,7},{7,6},{8,9},{9,8},{10,11... | collective-permute-start | bytes 3145736 | tf_op jit(solution)/shard_map/ppermute | solution.py:367
  84.0 4.4 %collective-permute-start.2 = (bf16[512,128]{1,0:T(8,128)(2,1)S(1)}, bf16[512,128]{1,0:T(8,128)(2,1)S(1)}, u32[]{:S(2)}, u32[]{:S(2)}) collective-permute-start(bf16[512,128]{1,0:T(8,128)(2,1)S(1)} %get-tuple-element.29), channel_id=1, source_target_pairs={{0,0},{1,16},{16,32},{17,48},{32,1},{33,17},{48,33},{49,49},{2,2},... | collective-permute-start | bytes 393224 | tf_op jit(solution)/shard_map/ppermute | solution.py:294
  84.7 6.2 %collective-permute-start.3 = (bf16[512,128]{1,0:T(8,128)(2,1)S(1)}, bf16[512,128]{1,0:T(8,128)(2,1)S(1)}, u32[]{:S(2)}, u32[]{:S(2)}) collective-permute-start(bf16[512,128]{1,0:T(8,128)(2,1)S(1)} %get-tuple-element.30), channel_id=1, source_target_pairs={{0,16},{1,0},{16,48},{17,32},{32,17},{33,1},{48,49},{49,33},{2,18}... | collective-permute-start | bytes 393224 | tf_op jit(solution)/shard_map/ppermute | solution.py:295
  91.0 16.8 %collective-permute-start.7 = (bf16[1024,128]{1,0:T(8,128)(2,1)S(1)}, bf16[1024,128]{1,0:T(8,128)(2,1)S(1)}, u32[]{:S(2)}, u32[]{:S(2)}) collective-permute-start(bf16[1024,128]{1,0:T(8,128)(2,1)S(1)} %pad_maximum_fusion.refs_0_), channel_id=1, source_target_pairs={{0,384},{64,448},{128,0},{192,64},{256,128},{320,192},{384,256},{4... | collective-permute-start | bytes 786440 | tf_op jit(solution)/shard_map/ppermute | solution.py:304
  96.4 17.4 %collective-permute-start.6 = (bf16[1024,128]{1,0:T(8,128)(2,1)S(1)}, bf16[1024,128]{1,0:T(8,128)(2,1)S(1)}, u32[]{:S(2)}, u32[]{:S(2)}) collective-permute-start(bf16[1024,128]{1,0:T(8,128)(2,1)S(1)} %pad_maximum_fusion.refs_0_), channel_id=1, source_target_pairs={{0,128},{64,192},{128,256},{192,320},{256,384},{320,448},{384,0},{... | collective-permute-start | bytes 786440 | tf_op jit(solution)/shard_map/ppermute | solution.py:304
  98.4 22.6 %collective-permute-start.5 = (bf16[1024,128]{1,0:T(8,128)(2,1)S(1)}, bf16[1024,128]{1,0:T(8,128)(2,1)S(1)}, u32[]{:S(2)}, u32[]{:S(2)}) collective-permute-start(bf16[1024,128]{1,0:T(8,128)(2,1)S(1)} %pad_maximum_fusion.refs_0_), channel_id=1, source_target_pairs={{0,448},{64,0},{128,64},{192,128},{256,192},{320,256},{384,320},{4... | collective-permute-start | bytes 786440 | tf_op jit(solution)/shard_map/ppermute | solution.py:304
  103.0 19.9 %collective-permute-start.4 = (bf16[1024,128]{1,0:T(8,128)(2,1)S(1)}, bf16[1024,128]{1,0:T(8,128)(2,1)S(1)}, u32[]{:S(2)}, u32[]{:S(2)}) collective-permute-start(bf16[1024,128]{1,0:T(8,128)(2,1)S(1)} %pad_maximum_fusion.refs_0_), channel_id=1, source_target_pairs={{0,64},{64,128},{128,192},{192,256},{256,320},{320,384},{384,448},... | collective-permute-start | bytes 786440 | tf_op jit(solution)/shard_map/ppermute | solution.py:304
  113.9 22.2 %collective-permute-start.8 = (bf16[1024,128]{1,0:T(8,128)(2,1)S(1)}, bf16[1024,128]{1,0:T(8,128)(2,1)S(1)}, u32[]{:S(2)}, u32[]{:S(2)}) collective-permute-start(bf16[1024,128]{1,0:T(8,128)(2,1)S(1)} %get-tuple-element.17), channel_id=1, source_target_pairs={{0,64},{64,128},{128,192},{192,256},{256,320},{320,384},{384,448},... | collective-permute-start | bytes 786440 | tf_op jit(solution)/shard_map/ppermute | solution.py:304
  115.8 20.2 %collective-permute-start.9 = (bf16[1024,128]{1,0:T(8,128)(2,1)S(1)}, bf16[1024,128]{1,0:T(8,128)(2,1)S(1)}, u32[]{:S(2)}, u32[]{:S(2)}) collective-permute-start(bf16[1024,128]{1,0:T(8,128)(2,1)S(1)} %get-tuple-element.18), channel_id=1, source_target_pairs={{0,448},{64,0},{128,64},{192,128},{256,192},{320,256},{384,320},{4... | collective-permute-start | bytes 786440 | tf_op jit(solution)/shard_map/ppermute | solution.py:304
  121.0 11.7 %collective-permute-start.10 = (bf16[512,128]{1,0:T(8,128)(2,1)S(1)}, bf16[512,128]{1,0:T(8,128)(2,1)S(1)}, u32[]{:S(2)}, u32[]{:S(2)}) collective-permute-start(bf16[512,128]{1,0:T(8,128)(2,1)S(1)} %get-tuple-element.19), channel_id=1, source_target_pairs={{0,128},{64,192},{128,256},{192,320},{256,384},{320,448},{384,0},{... | collective-permute-start | bytes 393224 | tf_op jit(solution)/shard_map/ppermute | solution.py:304
  122.9 13.1 %collective-permute-start.11 = (bf16[512,128]{1,0:T(8,128)(2,1)S(1)}, bf16[512,128]{1,0:T(8,128)(2,1)S(1)}, u32[]{:S(2)}, u32[]{:S(2)}) collective-permute-start(bf16[512,128]{1,0:T(8,128)(2,1)S(1)} %get-tuple-element.20), channel_id=1, source_target_pairs={{0,384},{64,448},{128,0},{192,64},{256,128},{320,192},{384,256},{4... | collective-permute-start | bytes 393224 | tf_op jit(solution)/shard_map/ppermute | solution.py:304
  136.8 15.8 %collective-permute-start.12 = (bf16[4,2,256,128]{3,2,1,0:T(8,128)(2,1)S(1)}, bf16[4,2,256,128]{3,2,1,0:T(8,128)(2,1)S(1)}, u32[]{:S(2)}, u32[]{:S(2)}) collective-permute-start(bf16[4,2,256,128]{3,2,1,0:T(8,128)(2,1)S(1)} %shard_map.79), channel_id=1, source_target_pairs={{0,2},{2,4},{4,6},{6,8},{8,10},{10,12},{12,14},{14,0},{1,3},{3,5},... | collective-permute-start | bytes 1572872 | tf_op jit(solution)/shard_map/ppermute | solution.py:267
  141.9 16.2 %collective-permute-start.13 = (bf16[4,2,256,128]{3,2,1,0:T(8,128)(2,1)S(1)}, bf16[4,2,256,128]{3,2,1,0:T(8,128)(2,1)S(1)}, u32[]{:S(2)}, u32[]{:S(2)}) collective-permute-start(bf16[4,2,256,128]{3,2,1,0:T(8,128)(2,1)S(1)} %shard_map.80), channel_id=1, source_target_pairs={{0,14},{2,0},{4,2},{6,4},{8,6},{10,8},{12,10},{14,12},{1,15},{3,1}... | collective-permute-start | bytes 1572872 | tf_op jit(solution)/shard_map/ppermute | solution.py:267

commit v10 on v9

--- a/solution.py
+++ b/solution.py
@@ -189,20 +189,17 @@
                 out[copy, b * HALF : (b + 1) * HALF, cols] = value
 
 
-def relay_kernel(up, down, up_out, down_out, up_half, down_half):
-    rows = up_half.shape[0]
+def relay_kernel(up, down, up_out, down_out):
     up_out[...] = up[...]
     down_out[...] = down[...]
-    up_half[...] = up[:rows]
-    down_half[...] = down[rows:]
 
 
 DISTANCES = ((0, 2, -2, 4), (1, -1, 3, -3))
 
 
 def project_kernel(parts, cross, own, other, *refs):
-    block, up, down, up2, down2, up3, down3, up4, down4 = refs[:9]
-    outs = refs[9:]
+    block, up, down, up2, down2, up3, down3, up4 = refs[:8]
+    outs = refs[8:]
     count, rows, lane = outs[0].shape[1:]
     n = 2 * outs[0].shape[0]
     load = {
@@ -213,7 +210,7 @@
         -2: lambda: down2[...],
         3: lambda: up3[...],
         -3: lambda: down3[...],
-        4: lambda: jnp.concatenate([up4[...], down4[...]], axis=0),
+        4: lambda: up4[...],
     }
     y = lax.axis_index("y")
     parity = lax.rem(y + lax.axis_index("zl"), 2)
@@ -324,13 +321,12 @@
 
     block = weight_columns(out_weight)
     up, down = around(block, 1), around(block, -1)
-    up2, down2 = around(block, 2), around(block, -2)
-    whole = shape(block.shape)
-    half = shape((block.shape[0] // 2, block.shape[1]))
-    relayed = call(relay_kernel, [whole, whole, half, half], [vmem()] * 2, (up2, down2), 0)
-    up3, down3 = around(relayed[0], 1), around(relayed[1], -1)
-    up4, down4 = around(relayed[2], 2), around(relayed[3], -2)
-    weights = (block, up, down, up2, down2, up3, down3, up4, down4)
+    up2, down2 = around(up, 1), around(down, -1)
+    both = [shape(block.shape)] * 2
+    far_up, far_down = call(relay_kernel, both, [vmem()] * 2, (up2, down2), 0)
+    up4 = around(far_up, 2)
+    up3, down3 = around(far_up, 1), around(far_down, -1)
+    weights = (block, up, down, up2, down2, up3, down3, up4)
 
     groups = medium_filters.shape[1]
     line = jnp.pad(medium_filters[::-1].T.astype(F32), ((0, 0), (1, HALF - 1)))
@@ -370,7 +366,7 @@
         (cross,) = project((part,), 1, own, other, weights, nx)
         got.append(along_z(cross, distance))
     mine = project((0, 1), 0, own, other, weights, nx)
-    nzh, half, _, lane = mine[0].shape
+    nzh, _, _, lane = mine[0].shape
     (pairs,) = call(pair_kernel, [shape((nzh, nx, rows, lane))], [vmem()] * 4, (*mine, *got), 10**6)
     flat = pairs.reshape(nzh * nx, rows, lane)
     parts = lax.all_to_all(flat, ("zh", "x"), split_axis=0, concat_axis=0, tiled=True)

time: 196 us -> 197 us (level)
  starting transfers between devices: 49.2 us -> 44.1 us
  waiting for transfers between devices: 43.9 us -> 49 us
    ppermute x8 -> x7, waiting for transfers between devices: 16 us -> 29.8 us  [around(): return lax.ppermute(block, 'y', [(i, (i + distance) % n) for i in range(n)])]
    ppermute x8 -> x7, starting transfers between devices: 29 us -> 20.9 us  [around(): return lax.ppermute(block, 'y', [(i, (i + distance) % n) for i in range(n)])]
    all_to_all x1, waiting for transfers between devices: 12.6 us -> 6.6 us  [operator(): own = lax.all_to_all(copies, 'x', split_axis=0, concat_axis=0, tiled=True)]
    ppermute x1, starting transfers between devices: 3.72 us -> 6.63 us  [weight_columns(): b = lax.ppermute(flip, ('x', 'core'), route(lambda i: 1 - i))]
    ppermute x1, waiting for transfers between devices: 2.48 us -> 0.01 us  [weight_columns(): b = lax.ppermute(flip, ('x', 'core'), route(lambda i: 1 - i))]
  transfers between devices with their start and end apart: 15 -> 14, of which waited for: 8 -> 9; matrix products, arithmetic and copies ran while one was open for 0% -> 0% of each run, Pallas kernels for 3% -> 2%
where the time goes in v10:
time: 197 us; the launch traced here: 196 us
  blocking collectives  87.4 us (44%)
  waiting for transfers between devices  49 us (25%)
  starting transfers between devices  44.1 us (22%)
  Pallas kernels  14.1 us (7%)
    all_to_all x1, blocking collectives, operator(): lax.all_to_all(packed, CTX, split_axis=0, concat_axis=0, tiled=True)  50.5 us
    all_to_all x1, blocking collectives, operator(): lax.all_to_all(flat, ('zh', 'x'), split_axis=0, concat_axis=0, tiled=True)  36.9 us
    ppermute x7, waiting for transfers between devices, around(): return lax.ppermute(block, 'y', [(i, (i + distance) % n) for i in range(n)])  29.8 us
    ppermute x7, starting transfers between devices, around(): return lax.ppermute(block, 'y', [(i, (i + distance) % n) for i in range(n)])  20.9 us
    ppermute x2, waiting for transfers between devices, along_z(): lax.ppermute(block, ('zh', 'zl'), [(i, (i + distance) % n) for i in range...  12.6 us
    pallas_call x9, Pallas kernels, call(): pl.pallas_call(body, out_shape=outs, in_specs=ins, out_specs=[vmem()] * l...  11.2 us
    ppermute x1, starting transfers between devices, weight_columns(): b = lax.ppermute(flip, ('x', 'core'), route(lambda i: 1 - i))  6.63 us
    all_to_all x1, waiting for transfers between devices, operator(): own = lax.all_to_all(copies, 'x', split_axis=0, concat_axis=0, tiled=True)  6.6 us
  transfers between devices with their start and end apart: 14, of which 9 were waited for; matrix products, arithmetic and copies ran while one was open for 0% of the time, Pallas kernels for 2%

profile of v10, /device:TPU:64, one launch (start us, length us, event | category | flops | bytes accessed | tf_op | source)
XLA Modules:
  0.0 195.9 jit_solution(8689967230019048438)
XLA Ops:
  0.0 2.9 %pack.1 = bf16[32,3,16,512]{3,2,1,0:T(8,128)(2,1)} custom-call(s32[16,32]{1,0:T(8,128)} %bitcast.12, bf16[3,512,512]{2,1,0:T(8,128)(2,1)} %bitcast.17), custom_call_target="tpu_custom_call" | custom-call | flops 1000000 | bytes 3145728 | tf_op jit(solution)/shard_map/pack/pallas_call | solution.py:82
  2.9 0.0 copy-start
  2.9 0.0 copy-start.1
  2.9 0.0 copy-start.2
  2.9 50.5 %all_to_all.15.blocks = bf16[32,3,16,512]{3,2,1,0:T(8,128)(2,1)S(1)} all-to-all(bf16[32,3,16,512]{3,2,1,0:T(8,128)(2,1)} %pack.1), channel_id=1, replica_groups=mesh['y'=8,'x'=4,'zh'=4,'zl'=2,'core'=2] {'y','x'}, dimensions={0} | all-to-all | bytes 3145728 | tf_op jit(solution)/shard_map/all_to_all | solution.py:320
  53.4 0.0 copy-start.5
  53.5 2.4 %shard_map.73 = (bf16[256,512]{1,0:T(8,128)(2,1)S(1)}, bf16[152,512]{1,0:T(8,128)(2,1)S(1)}, bf16[24,512]{1,0:T(8,128)(2,1)S(1)}) custom-call(s32[16,32]{1,0:T(8,128)S(1)} %bitcast.13, s32[8]{0:T(128)S(1)} %copy-done.2, bf16[32,3,16,512]{3,2,1,0:T(8,128)(2,1)S(1)} %all_to_all.15.blocks, bf16[3,7,512]{2,1,0:T(8,128)(2,1)S(1)} %copy-done), custom_call_target="tpu_custom_call" | custom-call | flops 10000000 | bytes 2038816 | tf_op jit(solution)/shard_map/pallas_call | solution.py:35
  55.9 2.6 %collective-permute-start = (bf16[152,512]{1,0:T(8,128)(2,1)S(1)}, bf16[152,512]{1,0:T(8,128)(2,1)S(1)}, u32[]{:S(2)}, u32[]{:S(2)}) collective-permute-start(bf16[152,512]{1,0:T(8,128)(2,1)S(1)} %get-tuple-element.13), channel_id=1, source_target_pairs={{0,16},{16,32},{32,48},{48,64},{64,80},{80,96},{96,112},{112,128},... | collective-permute-start | bytes 466952 | tf_op jit(solution)/shard_map/ppermute | solution.py:278
  58.5 0.1 rev.3
  58.6 0.1 pad_convert_fusion.line
  58.7 1.1 shard_map.75.bands
  59.8 0.0 copy-start.3
  59.8 1.6 shard_map.74.query
  61.4 0.0 collective-permute-done.recv
  61.4 2.9 %shard_map.76 = bf16[4,256,512]{2,1,0:T(8,128)(2,1)} custom-call(s32[8]{0:T(128)S(1)} %copy-done.2, bf16[256,512]{1,0:T(8,128)(2,1)S(1)} %get-tuple-element.12.z, f32[256,512]{1,0:T(8,128)S(1)} %shard_map.74.query, bf16[152,512]{1,0:T(8,128)(2,1)S(1)} %collective-permute-done.recv, bf16[24,512]{1,0:T(8,128)(2,1)S(1)} %get-tuple-element.14.head, ...), custom_call_target="tpu_custom_call" | custom-call | flops 1000000000 | bytes 4135968 | tf_op jit(solution)/shard_map/pallas_call | solution.py:35
  64.3 5.2 %all-to-all-start.1 = ((bf16[4,256,512]{2,1,0:T(8,128)(2,1)}), bf16[4,256,512]{2,1,0:T(8,128)(2,1)S(1)}, u32[]{:S(2)}, u32[]{:S(2)}) async-start(bf16[4,256,512]{2,1,0:T(8,128)(2,1)} %shard_map.76), calls=%async_computation.1 | async-start | bytes 2097152 | tf_op jit(solution)/shard_map/all_to_all | solution.py:361
  69.5 0.7 collective-permute-start.2
  70.2 6.6 %collective-permute-start.3 = (bf16[512,128]{1,0:T(8,128)(2,1)S(1)}, bf16[512,128]{1,0:T(8,128)(2,1)S(1)}, u32[]{:S(2)}, u32[]{:S(2)}) collective-permute-start(bf16[512,128]{1,0:T(8,128)(2,1)S(1)} %get-tuple-element.26), channel_id=1, source_target_pairs={{0,16},{1,0},{16,48},{17,32},{32,17},{33,1},{48,49},{49,33},{2,18}... | collective-permute-start | bytes 393224 | tf_op jit(solution)/shard_map/ppermute | solution.py:292
  76.8 6.6 %all-to-all-done.1 = bf16[4,256,512]{2,1,0:T(8,128)(2,1)S(1)} async-done(((bf16[4,256,512]{2,1,0:T(8,128)(2,1)}), bf16[4,256,512]{2,1,0:T(8,128)(2,1)S(1)}, u32[]{:S(2)}, u32[]{:S(2)}) %all-to-all-start.1) | async-done | bytes 1048608 | tf_op jit(solution)/shard_map/all_to_all | solution.py:361
  83.4 1.9 collective-permute-start.1
  85.4 0.0 collective-permute-done.2
  85.4 0.0 collective-permute-done.3
  85.4 4.1 %collective-permute-start.5 = (bf16[1024,128]{1,0:T(8,128)(2,1)S(1)}, bf16[1024,128]{1,0:T(8,128)(2,1)S(1)}, u32[]{:S(2)}, u32[]{:S(2)}) collective-permute-start(bf16[1024,128]{1,0:T(8,128)(2,1)S(1)} %pad_maximum_fusion.refs_0_), channel_id=1, source_target_pairs={{0,448},{64,0},{128,64},{192,128},{256,192},{320,256},{384,320},{4... | collective-permute-start | bytes 786440 | tf_op jit(solution)/shard_map/ppermute | solution.py:301
  89.5 2.1 %collective-permute-start.4 = (bf16[1024,128]{1,0:T(8,128)(2,1)S(1)}, bf16[1024,128]{1,0:T(8,128)(2,1)S(1)}, u32[]{:S(2)}, u32[]{:S(2)}) collective-permute-start(bf16[1024,128]{1,0:T(8,128)(2,1)S(1)} %pad_maximum_fusion.refs_0_), channel_id=1, source_target_pairs={{0,64},{64,128},{128,192},{192,256},{256,320},{320,384},{384,448},... | collective-permute-start | bytes 786440 | tf_op jit(solution)/shard_map/ppermute | solution.py:301
  91.7 5.0 %collective-permute-done.5.refs_2_ = bf16[1024,128]{1,0:T(8,128)(2,1)S(1)} collective-permute-done((bf16[1024,128]{1,0:T(8,128)(2,1)S(1)}, bf16[1024,128]{1,0:T(8,128)(2,1)S(1)}, u32[]{:S(2)}, u32[]{:S(2)}) %collective-permute-start.5) | collective-permute-done | bytes 262176 | tf_op jit(solution)/shard_map/ppermute | solution.py:301
  96.7 4.6 %collective-permute-start.7 = (bf16[1024,128]{1,0:T(8,128)(2,1)S(1)}, bf16[1024,128]{1,0:T(8,128)(2,1)S(1)}, u32[]{:S(2)}, u32[]{:S(2)}) collective-permute-start(bf16[1024,128]{1,0:T(8,128)(2,1)S(1)} %collective-permute-done.5.refs_2_), channel_id=1, source_target_pairs={{0,448},{64,0},{128,64},{192,128},{256,192},{320,256},{384,320},{4... | collective-permute-start | bytes 786440 | tf_op jit(solution)/shard_map/ppermute | solution.py:301
  101.3 0.0 collective-permute-done.4.refs_1_
  101.3 1.9 collective-permute-start.6
  103.3 3.4 %collective-permute-done.7.down.refs_4_ = bf16[1024,128]{1,0:T(8,128)(2,1)S(1)} collective-permute-done((bf16[1024,128]{1,0:T(8,128)(2,1)S(1)}, bf16[1024,128]{1,0:T(8,128)(2,1)S(1)}, u32[]{:S(2)}, u32[]{:S(2)}) %collective-permute-start.7) | collective-permute-done | bytes 262176 | tf_op jit(solution)/shard_map/ppermute | solution.py:301
  106.7 5.3 %collective-permute-done.6.up.refs_3_ = bf16[1024,128]{1,0:T(8,128)(2,1)S(1)} collective-permute-done((bf16[1024,128]{1,0:T(8,128)(2,1)S(1)}, bf16[1024,128]{1,0:T(8,128)(2,1)S(1)}, u32[]{:S(2)}, u32[]{:S(2)}) %collective-permute-start.6) | collective-permute-done | bytes 262176 | tf_op jit(solution)/shard_map/ppermute | solution.py:301
  112.0 2.1 %collective-permute-start.9 = (bf16[1024,128]{1,0:T(8,128)(2,1)S(1)}, bf16[1024,128]{1,0:T(8,128)(2,1)S(1)}, u32[]{:S(2)}, u32[]{:S(2)}) collective-permute-start(bf16[1024,128]{1,0:T(8,128)(2,1)S(1)} %get-tuple-element.16), channel_id=1, source_target_pairs={{0,448},{64,0},{128,64},{192,128},{256,192},{320,256},{384,320},{4... | collective-permute-start | bytes 786440 | tf_op jit(solution)/shard_map/ppermute | solution.py:301
  114.1 2.3 %collective-permute-start.10 = (bf16[1024,128]{1,0:T(8,128)(2,1)S(1)}, bf16[1024,128]{1,0:T(8,128)(2,1)S(1)}, u32[]{:S(2)}, u32[]{:S(2)}) collective-permute-start(bf16[1024,128]{1,0:T(8,128)(2,1)S(1)} %get-tuple-element.15), channel_id=1, source_target_pairs={{0,128},{64,192},{128,256},{192,320},{256,384},{320,448},{384,0},{... | collective-permute-start | bytes 786440 | tf_op jit(solution)/shard_map/ppermute | solution.py:301
  116.4 3.7 %collective-permute-start.8 = (bf16[1024,128]{1,0:T(8,128)(2,1)S(1)}, bf16[1024,128]{1,0:T(8,128)(2,1)S(1)}, u32[]{:S(2)}, u32[]{:S(2)}) collective-permute-start(bf16[1024,128]{1,0:T(8,128)(2,1)S(1)} %get-tuple-element.15), channel_id=1, source_target_pairs={{0,64},{64,128},{128,192},{192,256},{256,320},{320,384},{384,448},... | collective-permute-start | bytes 786440 | tf_op jit(solution)/shard_map/ppermute | solution.py:301
  120.2 0.5 collective-permute-done.9.refs_6_
  120.6 12.2 %collective-permute-done.10.refs_7_ = bf16[1024,128]{1,0:T(8,128)(2,1)S(1)} collective-permute-done((bf16[1024,128]{1,0:T(8,128)(2,1)S(1)}, bf16[1024,128]{1,0:T(8,128)(2,1)S(1)}, u32[]{:S(2)}, u32[]{:S(2)}) %collective-permute-start.10) | collective-permute-done | bytes 262176 | tf_op jit(solution)/shard_map/ppermute | solution.py:301
  132.8 3.4 %collective-permute-done.8.refs_5_ = bf16[1024,128]{1,0:T(8,128)(2,1)S(1)} collective-permute-done((bf16[1024,128]{1,0:T(8,128)(2,1)S(1)}, bf16[1024,128]{1,0:T(8,128)(2,1)S(1)}, u32[]{:S(2)}, u32[]{:S(2)}) %collective-permute-start.8) | collective-permute-done | bytes 262176 | tf_op jit(solution)/shard_map/ppermute | solution.py:301
  136.2 0.0 collective-permute-done.1.other
  136.2 0.7 shard_map.79
  137.0 4.3 %collective-permute-start.11 = (bf16[4,2,256,128]{3,2,1,0:T(8,128)(2,1)S(1)}, bf16[4,2,256,128]{3,2,1,0:T(8,128)(2,1)S(1)}, u32[]{:S(2)}, u32[]{:S(2)}) collective-permute-start(bf16[4,2,256,128]{3,2,1,0:T(8,128)(2,1)S(1)} %shard_map.79), channel_id=1, source_target_pairs={{0,2},{2,4},{4,6},{6,8},{8,10},{10,12},{12,14},{14,0},{1,3},{3,5},... | collective-permute-start | bytes 1572872 | tf_op jit(solution)/shard_map/ppermute | solution.py:264
  141.2 0.8 shard_map.80
  142.0 1.9 collective-permute-start.12
  143.9 1.4 shard_map.78
  145.3 7.2 %collective-permute-done.11.got0 = bf16[4,2,256,128]{3,2,1,0:T(8,128)(2,1)S(1)} collective-permute-done((bf16[4,2,256,128]{3,2,1,0:T(8,128)(2,1)S(1)}, bf16[4,2,256,128]{3,2,1,0:T(8,128)(2,1)S(1)}, u32[]{:S(2)}, u32[]{:S(2)}) %collective-permute-start.11) | collective-permute-done | bytes 524320 | tf_op jit(solution)/shard_map/ppermute | solution.py:264
  152.5 5.4 %collective-permute-done.12.got1 = bf16[4,2,256,128]{3,2,1,0:T(8,128)(2,1)S(1)} collective-permute-done((bf16[4,2,256,128]{3,2,1,0:T(8,128)(2,1)S(1)}, bf16[4,2,256,128]{3,2,1,0:T(8,128)(2,1)S(1)}, u32[]{:S(2)}, u32[]{:S(2)}) %collective-permute-start.12) | collective-permute-done | bytes 524320 | tf_op jit(solution)/shard_map/ppermute | solution.py:264
  157.9 0.2 shard_map.81
  158.2 36.9 %all_to_all.16 = bf16[16,256,128]{2,1,0:T(8,128)(2,1)S(1)} all-to-all(bf16[16,256,128]{2,1,0:T(8,128)(2,1)S(1)} %bitcast.11), channel_id=1, replica_groups=mesh['y'=8,'x'=4,'zh'=4,'zl'=2,'core'=2] {'zh','x'}, dimensions={0} | all-to-all | bytes 2097152 | tf_op jit(solution)/shard_map/all_to_all | solution.py:372
  195.1 0.1 slice_reduce_fusion.3
  195.2 0.7 pad_maximum_fusion.1
  (11 shorter events, 0.1 us)
Async XLA Ops:
  2.9 50.5 %copy-start = (bf16[3,7,512]{2,1,0:T(8,128)(2,1)S(1)}, bf16[3,7,512]{2,1,0:T(8,128)(2,1)}, u32[]{:S(2)}) copy-start(bf16[3,7,512]{2,1,0:T(8,128)(2,1)} %taps.5) | copy-start | bytes 64516
  2.9 50.5 %copy-start.1 = (s32[32,16]{0,1:T(8,128)S(1)}, s32[32,16]{0,1:T(8,128)}, u32[]{:S(2)}) copy-start(s32[32,16]{0,1:T(8,128)} %param.13) | copy-start | bytes 6148
  2.9 50.5 %copy-start.2 = (s32[8]{0:T(128)S(1)}, s32[8]{0:T(128)}, u32[]{:S(2)}) copy-start(s32[8]{0:T(128)} %lengths.5) | copy-start | bytes 100
  53.4 5.0 %copy-start.5 = (bf16[128,32]{0,1:T(8,128)(2,1)S(1)}, bf16[128,32]{0,1:T(8,128)(2,1)}, u32[]{:S(2)}) copy-start(bf16[128,32]{0,1:T(8,128)(2,1)} %param.9) | copy-start | bytes 24580
  55.9 5.5 %collective-permute-start = (bf16[152,512]{1,0:T(8,128)(2,1)S(1)}, bf16[152,512]{1,0:T(8,128)(2,1)S(1)}, u32[]{:S(2)}, u32[]{:S(2)}) collective-permute-start(bf16[152,512]{1,0:T(8,128)(2,1)S(1)} %get-tuple-element.13), channel_id=1, source_target_pairs={{0,16},{16,32},{32,48},{48,64},{64,80},{80,96},{96,112},{112,128},... | collective-permute-start | bytes 466952 | tf_op jit(solution)/shard_map/ppermute | solution.py:278
  59.8 1.6 copy-start.3
  64.3 5.2 %copy-start.4 = (bf16[512,256]{1,0:T(8,128)(2,1)S(1)}, bf16[512,256]{1,0:T(8,128)(2,1)}, u32[]{:S(2)}) copy-start(bf16[512,256]{1,0:T(8,128)(2,1)} %param.11) | copy-start | bytes 786436
  64.3 19.1 %all-to-all-start.1 = ((bf16[4,256,512]{2,1,0:T(8,128)(2,1)}), bf16[4,256,512]{2,1,0:T(8,128)(2,1)S(1)}, u32[]{:S(2)}, u32[]{:S(2)}) async-start(bf16[4,256,512]{2,1,0:T(8,128)(2,1)} %shard_map.76), calls=%async_computation.1 | async-start | bytes 2097152 | tf_op jit(solution)/shard_map/all_to_all | solution.py:361
  69.5 15.9 %collective-permute-start.2 = (bf16[512,128]{1,0:T(8,128)(2,1)S(1)}, bf16[512,128]{1,0:T(8,128)(2,1)S(1)}, u32[]{:S(2)}, u32[]{:S(2)}) collective-permute-start(bf16[512,128]{1,0:T(8,128)(2,1)S(1)} %get-tuple-element.25), channel_id=1, source_target_pairs={{0,0},{1,16},{16,32},{17,48},{32,1},{33,17},{48,33},{49,49},{2,2},... | collective-permute-start | bytes 393224 | tf_op jit(solution)/shard_map/ppermute | solution.py:291
  70.2 15.2 %collective-permute-start.3 = (bf16[512,128]{1,0:T(8,128)(2,1)S(1)}, bf16[512,128]{1,0:T(8,128)(2,1)S(1)}, u32[]{:S(2)}, u32[]{:S(2)}) collective-permute-start(bf16[512,128]{1,0:T(8,128)(2,1)S(1)} %get-tuple-element.26), channel_id=1, source_target_pairs={{0,16},{1,0},{16,48},{17,32},{32,17},{33,1},{48,49},{49,33},{2,18}... | collective-permute-start | bytes 393224 | tf_op jit(solution)/shard_map/ppermute | solution.py:292
  83.4 52.8 %collective-permute-start.1 = (bf16[1024,512]{1,0:T(8,128)(2,1)S(1)}, bf16[1024,512]{1,0:T(8,128)(2,1)S(1)}, u32[]{:S(2)}, u32[]{:S(2)}) collective-permute-start(bf16[1024,512]{1,0:T(8,128)(2,1)S(1)} %bitcast.7), channel_id=1, source_target_pairs={{0,1},{1,0},{2,3},{3,2},{4,5},{5,4},{6,7},{7,6},{8,9},{9,8},{10,11... | collective-permute-start | bytes 3145736 | tf_op jit(solution)/shard_map/ppermute | solution.py:363
  85.4 11.2 %collective-permute-start.5 = (bf16[1024,128]{1,0:T(8,128)(2,1)S(1)}, bf16[1024,128]{1,0:T(8,128)(2,1)S(1)}, u32[]{:S(2)}, u32[]{:S(2)}) collective-permute-start(bf16[1024,128]{1,0:T(8,128)(2,1)S(1)} %pad_maximum_fusion.refs_0_), channel_id=1, source_target_pairs={{0,448},{64,0},{128,64},{192,128},{256,192},{320,256},{384,320},{4... | collective-permute-start | bytes 786440 | tf_op jit(solution)/shard_map/ppermute | solution.py:301
  89.5 11.8 %collective-permute-start.4 = (bf16[1024,128]{1,0:T(8,128)(2,1)S(1)}, bf16[1024,128]{1,0:T(8,128)(2,1)S(1)}, u32[]{:S(2)}, u32[]{:S(2)}) collective-permute-start(bf16[1024,128]{1,0:T(8,128)(2,1)S(1)} %pad_maximum_fusion.refs_0_), channel_id=1, source_target_pairs={{0,64},{64,128},{128,192},{192,256},{256,320},{320,384},{384,448},... | collective-permute-start | bytes 786440 | tf_op jit(solution)/shard_map/ppermute | solution.py:301
  96.7 10.0 %collective-permute-start.7 = (bf16[1024,128]{1,0:T(8,128)(2,1)S(1)}, bf16[1024,128]{1,0:T(8,128)(2,1)S(1)}, u32[]{:S(2)}, u32[]{:S(2)}) collective-permute-start(bf16[1024,128]{1,0:T(8,128)(2,1)S(1)} %collective-permute-done.5.refs_2_), channel_id=1, source_target_pairs={{0,448},{64,0},{128,64},{192,128},{256,192},{320,256},{384,320},{4... | collective-permute-start | bytes 786440 | tf_op jit(solution)/shard_map/ppermute | solution.py:301
  101.3 10.7 %collective-permute-start.6 = (bf16[1024,128]{1,0:T(8,128)(2,1)S(1)}, bf16[1024,128]{1,0:T(8,128)(2,1)S(1)}, u32[]{:S(2)}, u32[]{:S(2)}) collective-permute-start(bf16[1024,128]{1,0:T(8,128)(2,1)S(1)} %collective-permute-done.4.refs_1_), channel_id=1, source_target_pairs={{0,64},{64,128},{128,192},{192,256},{256,320},{320,384},{384,448},... | collective-permute-start | bytes 786440 | tf_op jit(solution)/shard_map/ppermute | solution.py:301
  112.0 8.6 %collective-permute-start.9 = (bf16[1024,128]{1,0:T(8,128)(2,1)S(1)}, bf16[1024,128]{1,0:T(8,128)(2,1)S(1)}, u32[]{:S(2)}, u32[]{:S(2)}) collective-permute-start(bf16[1024,128]{1,0:T(8,128)(2,1)S(1)} %get-tuple-element.16), channel_id=1, source_target_pairs={{0,448},{64,0},{128,64},{192,128},{256,192},{320,256},{384,320},{4... | collective-permute-start | bytes 786440 | tf_op jit(solution)/shard_map/ppermute | solution.py:301
  114.1 18.7 %collective-permute-start.10 = (bf16[1024,128]{1,0:T(8,128)(2,1)S(1)}, bf16[1024,128]{1,0:T(8,128)(2,1)S(1)}, u32[]{:S(2)}, u32[]{:S(2)}) collective-permute-start(bf16[1024,128]{1,0:T(8,128)(2,1)S(1)} %get-tuple-element.15), channel_id=1, source_target_pairs={{0,128},{64,192},{128,256},{192,320},{256,384},{320,448},{384,0},{... | collective-permute-start | bytes 786440 | tf_op jit(solution)/shard_map/ppermute | solution.py:301
  116.4 19.8 %collective-permute-start.8 = (bf16[1024,128]{1,0:T(8,128)(2,1)S(1)}, bf16[1024,128]{1,0:T(8,128)(2,1)S(1)}, u32[]{:S(2)}, u32[]{:S(2)}) collective-permute-start(bf16[1024,128]{1,0:T(8,128)(2,1)S(1)} %get-tuple-element.15), channel_id=1, source_target_pairs={{0,64},{64,128},{128,192},{192,256},{256,320},{320,384},{384,448},... | collective-permute-start | bytes 786440 | tf_op jit(solution)/shard_map/ppermute | solution.py:301
  137.0 15.5 %collective-permute-start.11 = (bf16[4,2,256,128]{3,2,1,0:T(8,128)(2,1)S(1)}, bf16[4,2,256,128]{3,2,1,0:T(8,128)(2,1)S(1)}, u32[]{:S(2)}, u32[]{:S(2)}) collective-permute-start(bf16[4,2,256,128]{3,2,1,0:T(8,128)(2,1)S(1)} %shard_map.79), channel_id=1, source_target_pairs={{0,2},{2,4},{4,6},{6,8},{8,10},{10,12},{12,14},{14,0},{1,3},{3,5},... | collective-permute-start | bytes 1572872 | tf_op jit(solution)/shard_map/ppermute | solution.py:264
  142.0 15.9 %collective-permute-start.12 = (bf16[4,2,256,128]{3,2,1,0:T(8,128)(2,1)S(1)}, bf16[4,2,256,128]{3,2,1,0:T(8,128)(2,1)S(1)}, u32[]{:S(2)}, u32[]{:S(2)}) collective-permute-start(bf16[4,2,256,128]{3,2,1,0:T(8,128)(2,1)S(1)} %shard_map.80), channel_id=1, source_target_pairs={{0,14},{2,0},{4,2},{6,4},{8,6},{10,8},{12,10},{14,12},{1,15},{3,1}... | collective-permute-start | bytes 1572872 | tf_op jit(solution)/shard_map/ppermute | solution.py:264

commit v11 on v9

--- a/solution.py
+++ b/solution.py
@@ -324,12 +324,14 @@
 
     block = weight_columns(out_weight)
     up, down = around(block, 1), around(block, -1)
-    up2, down2 = around(block, 2), around(block, -2)
+    up2, down2 = around(up, 1), around(down, -1)
     whole = shape(block.shape)
     half = shape((block.shape[0] // 2, block.shape[1]))
-    relayed = call(relay_kernel, [whole, whole, half, half], [vmem()] * 2, (up2, down2), 0)
-    up3, down3 = around(relayed[0], 1), around(relayed[1], -1)
-    up4, down4 = around(relayed[2], 2), around(relayed[3], -2)
+    far_up, far_down, up_half, down_half = call(
+        relay_kernel, [whole, whole, half, half], [vmem()] * 2, (up2, down2), 0
+    )
+    up4, down4 = around(up_half, 2), around(down_half, -2)
+    up3, down3 = around(far_up, 1), around(far_down, -1)
     weights = (block, up, down, up2, down2, up3, down3, up4, down4)
 
     groups = medium_filters.shape[1]

time: 196 us -> 192 us (0.980)
  the two profiles are of different devices: /device:TPU:64 before, /device:TPU:80 now
where the time goes in v11:
time: 192 us; the launch traced here: 191 us
  blocking collectives  86.3 us (45%)
  starting transfers between devices  50.1 us (26%)
  waiting for transfers between devices  39.1 us (20%)
  Pallas kernels  14.1 us (7%)
    all_to_all x1, blocking collectives, operator(): lax.all_to_all(packed, CTX, split_axis=0, concat_axis=0, tiled=True)  49.5 us
    all_to_all x1, blocking collectives, operator(): lax.all_to_all(flat, ('zh', 'x'), split_axis=0, concat_axis=0, tiled=True)  36.8 us
    ppermute x8, starting transfers between devices, around(): return lax.ppermute(block, 'y', [(i, (i + distance) % n) for i in range(n)])  29.1 us
    ppermute x8, waiting for transfers between devices, around(): return lax.ppermute(block, 'y', [(i, (i + distance) % n) for i in range(n)])  18.5 us
    pallas_call x9, Pallas kernels, call(): pl.pallas_call(body, out_shape=outs, in_specs=ins, out_specs=[vmem()] * l...  11.2 us
    ppermute x2, waiting for transfers between devices, along_z(): lax.ppermute(block, ('zh', 'zl'), [(i, (i + distance) % n) for i in range...  9.86 us
    ppermute x1, starting transfers between devices, weight_columns(): b = lax.ppermute(flip, ('x', 'core'), route(lambda i: 1 - i))  6.58 us
    all_to_all x1, waiting for transfers between devices, operator(): own = lax.all_to_all(copies, 'x', split_axis=0, concat_axis=0, tiled=True)  6.31 us
  transfers between devices with their start and end apart: 15, of which 9 were waited for; matrix products, arithmetic and copies ran while one was open for 0% of the time, Pallas kernels for 3%

profile of v11, /device:TPU:80, one launch (start us, length us, event | category | flops | bytes accessed | tf_op | source)
XLA Modules:
  0.0 191.0 jit_solution(16496486348651157372)
XLA Ops:
  0.0 2.9 %pack.1 = bf16[32,3,16,512]{3,2,1,0:T(8,128)(2,1)} custom-call(s32[16,32]{1,0:T(8,128)} %bitcast.12, bf16[3,512,512]{2,1,0:T(8,128)(2,1)} %bitcast.17), custom_call_target="tpu_custom_call" | custom-call | flops 1000000 | bytes 3145728 | tf_op jit(solution)/shard_map/pack/pallas_call | solution.py:82
  2.9 0.0 copy-start
  2.9 0.0 copy-start.1
  2.9 0.0 copy-start.2
  3.0 49.5 %all_to_all.15.blocks = bf16[32,3,16,512]{3,2,1,0:T(8,128)(2,1)S(1)} all-to-all(bf16[32,3,16,512]{3,2,1,0:T(8,128)(2,1)} %pack.1), channel_id=1, replica_groups=mesh['y'=8,'x'=4,'zh'=4,'zl'=2,'core'=2] {'y','x'}, dimensions={0} | all-to-all | bytes 3145728 | tf_op jit(solution)/shard_map/all_to_all | solution.py:323
  52.5 0.0 copy-start.5
  52.5 2.4 %shard_map.73 = (bf16[256,512]{1,0:T(8,128)(2,1)S(1)}, bf16[152,512]{1,0:T(8,128)(2,1)S(1)}, bf16[24,512]{1,0:T(8,128)(2,1)S(1)}) custom-call(s32[16,32]{1,0:T(8,128)S(1)} %bitcast.13, s32[8]{0:T(128)S(1)} %copy-done.2, bf16[32,3,16,512]{3,2,1,0:T(8,128)(2,1)S(1)} %all_to_all.15.blocks, bf16[3,7,512]{2,1,0:T(8,128)(2,1)S(1)} %copy-done), custom_call_target="tpu_custom_call" | custom-call | flops 10000000 | bytes 2038816 | tf_op jit(solution)/shard_map/pallas_call | solution.py:35
  54.9 1.9 %collective-permute-start = (bf16[152,512]{1,0:T(8,128)(2,1)S(1)}, bf16[152,512]{1,0:T(8,128)(2,1)S(1)}, u32[]{:S(2)}, u32[]{:S(2)}) collective-permute-start(bf16[152,512]{1,0:T(8,128)(2,1)S(1)} %get-tuple-element.15), channel_id=1, source_target_pairs={{0,16},{16,32},{32,48},{48,64},{64,80},{80,96},{96,112},{112,128},... | collective-permute-start | bytes 466952 | tf_op jit(solution)/shard_map/ppermute | solution.py:281
  56.8 0.1 rev.3
  56.9 0.1 pad_convert_fusion.line
  57.0 1.1 shard_map.75.bands
  58.1 0.0 copy-start.3
  58.1 1.6 shard_map.74.query
  59.8 4.4 %collective-permute-done.recv = bf16[152,512]{1,0:T(8,128)(2,1)S(1)} collective-permute-done((bf16[152,512]{1,0:T(8,128)(2,1)S(1)}, bf16[152,512]{1,0:T(8,128)(2,1)S(1)}, u32[]{:S(2)}, u32[]{:S(2)}) %collective-permute-start) | collective-permute-done | bytes 155680 | tf_op jit(solution)/shard_map/ppermute | solution.py:281
  64.1 2.9 %shard_map.76 = bf16[4,256,512]{2,1,0:T(8,128)(2,1)} custom-call(s32[8]{0:T(128)S(1)} %copy-done.2, bf16[256,512]{1,0:T(8,128)(2,1)S(1)} %get-tuple-element.14.z, f32[256,512]{1,0:T(8,128)S(1)} %shard_map.74.query, bf16[152,512]{1,0:T(8,128)(2,1)S(1)} %collective-permute-done.recv, bf16[24,512]{1,0:T(8,128)(2,1)S(1)} %get-tuple-element.16.head, ...), custom_call_target="tpu_custom_call" | custom-call | flops 1000000000 | bytes 4135968 | tf_op jit(solution)/shard_map/pallas_call | solution.py:35
  67.0 3.6 %all-to-all-start.1 = ((bf16[4,256,512]{2,1,0:T(8,128)(2,1)}), bf16[4,256,512]{2,1,0:T(8,128)(2,1)S(1)}, u32[]{:S(2)}, u32[]{:S(2)}) async-start(bf16[4,256,512]{2,1,0:T(8,128)(2,1)} %shard_map.76), calls=%async_computation.1 | async-start | bytes 2097152 | tf_op jit(solution)/shard_map/all_to_all | solution.py:367
  70.7 0.7 collective-permute-start.2
  71.4 6.6 %collective-permute-start.3 = (bf16[512,128]{1,0:T(8,128)(2,1)S(1)}, bf16[512,128]{1,0:T(8,128)(2,1)S(1)}, u32[]{:S(2)}, u32[]{:S(2)}) collective-permute-start(bf16[512,128]{1,0:T(8,128)(2,1)S(1)} %get-tuple-element.30), channel_id=1, source_target_pairs={{0,16},{1,0},{16,48},{17,32},{32,17},{33,1},{48,49},{49,33},{2,18}... | collective-permute-start | bytes 393224 | tf_op jit(solution)/shard_map/ppermute | solution.py:295
  78.0 6.3 %all-to-all-done.1 = bf16[4,256,512]{2,1,0:T(8,128)(2,1)S(1)} async-done(((bf16[4,256,512]{2,1,0:T(8,128)(2,1)}), bf16[4,256,512]{2,1,0:T(8,128)(2,1)S(1)}, u32[]{:S(2)}, u32[]{:S(2)}) %all-to-all-start.1) | async-done | bytes 1048608 | tf_op jit(solution)/shard_map/all_to_all | solution.py:367
  84.3 1.9 collective-permute-start.1
  86.2 0.0 collective-permute-done.2
  86.2 0.0 collective-permute-done.3
  86.3 2.3 %collective-permute-start.5 = (bf16[1024,128]{1,0:T(8,128)(2,1)S(1)}, bf16[1024,128]{1,0:T(8,128)(2,1)S(1)}, u32[]{:S(2)}, u32[]{:S(2)}) collective-permute-start(bf16[1024,128]{1,0:T(8,128)(2,1)S(1)} %pad_maximum_fusion.refs_0_), channel_id=1, source_target_pairs={{0,448},{64,0},{128,64},{192,128},{256,192},{320,256},{384,320},{4... | collective-permute-start | bytes 786440 | tf_op jit(solution)/shard_map/ppermute | solution.py:304
  88.6 3.5 %collective-permute-start.4 = (bf16[1024,128]{1,0:T(8,128)(2,1)S(1)}, bf16[1024,128]{1,0:T(8,128)(2,1)S(1)}, u32[]{:S(2)}, u32[]{:S(2)}) collective-permute-start(bf16[1024,128]{1,0:T(8,128)(2,1)S(1)} %pad_maximum_fusion.refs_0_), channel_id=1, source_target_pairs={{0,64},{64,128},{128,192},{192,256},{256,320},{320,384},{384,448},... | collective-permute-start | bytes 786440 | tf_op jit(solution)/shard_map/ppermute | solution.py:304
  92.1 4.7 %collective-permute-done.5.refs_2_ = bf16[1024,128]{1,0:T(8,128)(2,1)S(1)} collective-permute-done((bf16[1024,128]{1,0:T(8,128)(2,1)S(1)}, bf16[1024,128]{1,0:T(8,128)(2,1)S(1)}, u32[]{:S(2)}, u32[]{:S(2)}) %collective-permute-start.5) | collective-permute-done | bytes 262176 | tf_op jit(solution)/shard_map/ppermute | solution.py:304
  96.9 2.3 %collective-permute-start.7 = (bf16[1024,128]{1,0:T(8,128)(2,1)S(1)}, bf16[1024,128]{1,0:T(8,128)(2,1)S(1)}, u32[]{:S(2)}, u32[]{:S(2)}) collective-permute-start(bf16[1024,128]{1,0:T(8,128)(2,1)S(1)} %collective-permute-done.5.refs_2_), channel_id=1, source_target_pairs={{0,448},{64,0},{128,64},{192,128},{256,192},{320,256},{384,320},{4... | collective-permute-start | bytes 786440 | tf_op jit(solution)/shard_map/ppermute | solution.py:304
  99.2 0.0 collective-permute-done.4.refs_1_
  99.2 4.0 %collective-permute-start.6 = (bf16[1024,128]{1,0:T(8,128)(2,1)S(1)}, bf16[1024,128]{1,0:T(8,128)(2,1)S(1)}, u32[]{:S(2)}, u32[]{:S(2)}) collective-permute-start(bf16[1024,128]{1,0:T(8,128)(2,1)S(1)} %collective-permute-done.4.refs_1_), channel_id=1, source_target_pairs={{0,64},{64,128},{128,192},{192,256},{256,320},{320,384},{384,448},... | collective-permute-start | bytes 786440 | tf_op jit(solution)/shard_map/ppermute | solution.py:304
  103.2 4.4 %collective-permute-done.7.down.refs_4_ = bf16[1024,128]{1,0:T(8,128)(2,1)S(1)} collective-permute-done((bf16[1024,128]{1,0:T(8,128)(2,1)S(1)}, bf16[1024,128]{1,0:T(8,128)(2,1)S(1)}, u32[]{:S(2)}, u32[]{:S(2)}) %collective-permute-start.7) | collective-permute-done | bytes 262176 | tf_op jit(solution)/shard_map/ppermute | solution.py:304
  107.7 1.2 collective-permute-done.6.up.refs_3_
  108.8 0.1 shard_map.77
  108.9 4.9 %collective-permute-start.8 = (bf16[1024,128]{1,0:T(8,128)(2,1)S(1)}, bf16[1024,128]{1,0:T(8,128)(2,1)S(1)}, u32[]{:S(2)}, u32[]{:S(2)}) collective-permute-start(bf16[1024,128]{1,0:T(8,128)(2,1)S(1)} %get-tuple-element.17), channel_id=1, source_target_pairs={{0,64},{64,128},{128,192},{192,256},{256,320},{320,384},{384,448},... | collective-permute-start | bytes 786440 | tf_op jit(solution)/shard_map/ppermute | solution.py:304
  113.8 1.9 %collective-permute-start.9 = (bf16[1024,128]{1,0:T(8,128)(2,1)S(1)}, bf16[1024,128]{1,0:T(8,128)(2,1)S(1)}, u32[]{:S(2)}, u32[]{:S(2)}) collective-permute-start(bf16[1024,128]{1,0:T(8,128)(2,1)S(1)} %get-tuple-element.18), channel_id=1, source_target_pairs={{0,448},{64,0},{128,64},{192,128},{256,192},{320,256},{384,320},{4... | collective-permute-start | bytes 786440 | tf_op jit(solution)/shard_map/ppermute | solution.py:304
  115.7 8.3 %collective-permute-start.10 = (bf16[512,128]{1,0:T(8,128)(2,1)S(1)}, bf16[512,128]{1,0:T(8,128)(2,1)S(1)}, u32[]{:S(2)}, u32[]{:S(2)}) collective-permute-start(bf16[512,128]{1,0:T(8,128)(2,1)S(1)} %get-tuple-element.19), channel_id=1, source_target_pairs={{0,128},{64,192},{128,256},{192,320},{256,384},{320,448},{384,0},{... | collective-permute-start | bytes 393224 | tf_op jit(solution)/shard_map/ppermute | solution.py:304
  124.0 1.9 %collective-permute-start.11 = (bf16[512,128]{1,0:T(8,128)(2,1)S(1)}, bf16[512,128]{1,0:T(8,128)(2,1)S(1)}, u32[]{:S(2)}, u32[]{:S(2)}) collective-permute-start(bf16[512,128]{1,0:T(8,128)(2,1)S(1)} %get-tuple-element.20), channel_id=1, source_target_pairs={{0,384},{64,448},{128,0},{192,64},{256,128},{320,192},{384,256},{4... | collective-permute-start | bytes 393224 | tf_op jit(solution)/shard_map/ppermute | solution.py:304
  125.9 0.8 collective-permute-done.10.refs_7_
  126.7 7.4 %collective-permute-done.11.refs_8_ = bf16[512,128]{1,0:T(8,128)(2,1)S(1)} collective-permute-done((bf16[512,128]{1,0:T(8,128)(2,1)S(1)}, bf16[512,128]{1,0:T(8,128)(2,1)S(1)}, u32[]{:S(2)}, u32[]{:S(2)}) %collective-permute-start.11) | collective-permute-done | bytes 131104 | tf_op jit(solution)/shard_map/ppermute | solution.py:304
  134.1 0.8 shard_map.79
  134.8 4.3 %collective-permute-start.12 = (bf16[4,2,256,128]{3,2,1,0:T(8,128)(2,1)S(1)}, bf16[4,2,256,128]{3,2,1,0:T(8,128)(2,1)S(1)}, u32[]{:S(2)}, u32[]{:S(2)}) collective-permute-start(bf16[4,2,256,128]{3,2,1,0:T(8,128)(2,1)S(1)} %shard_map.79), channel_id=1, source_target_pairs={{0,2},{2,4},{4,6},{6,8},{8,10},{10,12},{12,14},{14,0},{1,3},{3,5},... | collective-permute-start | bytes 1572872 | tf_op jit(solution)/shard_map/ppermute | solution.py:267
  139.1 0.8 shard_map.80
  139.9 1.9 %collective-permute-start.13 = (bf16[4,2,256,128]{3,2,1,0:T(8,128)(2,1)S(1)}, bf16[4,2,256,128]{3,2,1,0:T(8,128)(2,1)S(1)}, u32[]{:S(2)}, u32[]{:S(2)}) collective-permute-start(bf16[4,2,256,128]{3,2,1,0:T(8,128)(2,1)S(1)} %shard_map.80), channel_id=1, source_target_pairs={{0,14},{2,0},{4,2},{6,4},{8,6},{10,8},{12,10},{14,12},{1,15},{3,1}... | collective-permute-start | bytes 1572872 | tf_op jit(solution)/shard_map/ppermute | solution.py:267
  141.8 1.4 shard_map.78
  143.2 4.4 %collective-permute-done.12.got0 = bf16[4,2,256,128]{3,2,1,0:T(8,128)(2,1)S(1)} collective-permute-done((bf16[4,2,256,128]{3,2,1,0:T(8,128)(2,1)S(1)}, bf16[4,2,256,128]{3,2,1,0:T(8,128)(2,1)S(1)}, u32[]{:S(2)}, u32[]{:S(2)}) %collective-permute-start.12) | collective-permute-done | bytes 524320 | tf_op jit(solution)/shard_map/ppermute | solution.py:267
  147.6 5.4 %collective-permute-done.13.got1 = bf16[4,2,256,128]{3,2,1,0:T(8,128)(2,1)S(1)} collective-permute-done((bf16[4,2,256,128]{3,2,1,0:T(8,128)(2,1)S(1)}, bf16[4,2,256,128]{3,2,1,0:T(8,128)(2,1)S(1)}, u32[]{:S(2)}, u32[]{:S(2)}) %collective-permute-start.13) | collective-permute-done | bytes 524320 | tf_op jit(solution)/shard_map/ppermute | solution.py:267
  153.1 0.2 shard_map.81
  153.3 36.8 %all_to_all.16 = bf16[16,256,128]{2,1,0:T(8,128)(2,1)S(1)} all-to-all(bf16[16,256,128]{2,1,0:T(8,128)(2,1)S(1)} %bitcast.11), channel_id=1, replica_groups=mesh['y'=8,'x'=4,'zh'=4,'zl'=2,'core'=2] {'zh','x'}, dimensions={0} | all-to-all | bytes 2097152 | tf_op jit(solution)/shard_map/all_to_all | solution.py:378
  190.1 0.1 slice_reduce_fusion.3
  190.2 0.7 pad_maximum_fusion.1
  (13 shorter events, 0.1 us)
Async XLA Ops:
  2.9 49.5 %copy-start = (bf16[3,7,512]{2,1,0:T(8,128)(2,1)S(1)}, bf16[3,7,512]{2,1,0:T(8,128)(2,1)}, u32[]{:S(2)}) copy-start(bf16[3,7,512]{2,1,0:T(8,128)(2,1)} %taps.5) | copy-start | bytes 64516
  2.9 49.5 %copy-start.1 = (s32[32,16]{0,1:T(8,128)S(1)}, s32[32,16]{0,1:T(8,128)}, u32[]{:S(2)}) copy-start(s32[32,16]{0,1:T(8,128)} %param.13) | copy-start | bytes 6148
  2.9 49.5 %copy-start.2 = (s32[8]{0:T(128)S(1)}, s32[8]{0:T(128)}, u32[]{:S(2)}) copy-start(s32[8]{0:T(128)} %lengths.5) | copy-start | bytes 100
  52.5 4.4 %copy-start.5 = (bf16[128,32]{0,1:T(8,128)(2,1)S(1)}, bf16[128,32]{0,1:T(8,128)(2,1)}, u32[]{:S(2)}) copy-start(bf16[128,32]{0,1:T(8,128)(2,1)} %param.9) | copy-start | bytes 24580
  54.9 9.2 %collective-permute-start = (bf16[152,512]{1,0:T(8,128)(2,1)S(1)}, bf16[152,512]{1,0:T(8,128)(2,1)S(1)}, u32[]{:S(2)}, u32[]{:S(2)}) collective-permute-start(bf16[152,512]{1,0:T(8,128)(2,1)S(1)} %get-tuple-element.15), channel_id=1, source_target_pairs={{0,16},{16,32},{32,48},{48,64},{64,80},{80,96},{96,112},{112,128},... | collective-permute-start | bytes 466952 | tf_op jit(solution)/shard_map/ppermute | solution.py:281
  58.1 6.0 %copy-start.3 = (f32[512]{0:T(512)S(1)}, f32[512]{0:T(512)}, u32[]{:S(2)}) copy-start(f32[512]{0:T(512)} %param.10) | copy-start | bytes 6148
  67.0 3.7 %copy-start.4 = (bf16[512,256]{1,0:T(8,128)(2,1)S(1)}, bf16[512,256]{1,0:T(8,128)(2,1)}, u32[]{:S(2)}) copy-start(bf16[512,256]{1,0:T(8,128)(2,1)} %param.11) | copy-start | bytes 786436
  67.0 17.3 %all-to-all-start.1 = ((bf16[4,256,512]{2,1,0:T(8,128)(2,1)}), bf16[4,256,512]{2,1,0:T(8,128)(2,1)S(1)}, u32[]{:S(2)}, u32[]{:S(2)}) async-start(bf16[4,256,512]{2,1,0:T(8,128)(2,1)} %shard_map.76), calls=%async_computation.1 | async-start | bytes 2097152 | tf_op jit(solution)/shard_map/all_to_all | solution.py:367
  70.7 15.5 %collective-permute-start.2 = (bf16[512,128]{1,0:T(8,128)(2,1)S(1)}, bf16[512,128]{1,0:T(8,128)(2,1)S(1)}, u32[]{:S(2)}, u32[]{:S(2)}) collective-permute-start(bf16[512,128]{1,0:T(8,128)(2,1)S(1)} %get-tuple-element.29), channel_id=1, source_target_pairs={{0,0},{1,16},{16,32},{17,48},{32,1},{33,17},{48,33},{49,49},{2,2},... | collective-permute-start | bytes 393224 | tf_op jit(solution)/shard_map/ppermute | solution.py:294
  71.4 14.8 %collective-permute-start.3 = (bf16[512,128]{1,0:T(8,128)(2,1)S(1)}, bf16[512,128]{1,0:T(8,128)(2,1)S(1)}, u32[]{:S(2)}, u32[]{:S(2)}) collective-permute-start(bf16[512,128]{1,0:T(8,128)(2,1)S(1)} %get-tuple-element.30), channel_id=1, source_target_pairs={{0,16},{1,0},{16,48},{17,32},{32,17},{33,1},{48,49},{49,33},{2,18}... | collective-permute-start | bytes 393224 | tf_op jit(solution)/shard_map/ppermute | solution.py:295
  84.3 49.8 %collective-permute-start.1 = (bf16[1024,512]{1,0:T(8,128)(2,1)S(1)}, bf16[1024,512]{1,0:T(8,128)(2,1)S(1)}, u32[]{:S(2)}, u32[]{:S(2)}) collective-permute-start(bf16[1024,512]{1,0:T(8,128)(2,1)S(1)} %bitcast.7), channel_id=1, source_target_pairs={{0,1},{1,0},{2,3},{3,2},{4,5},{5,4},{6,7},{7,6},{8,9},{9,8},{10,11... | collective-permute-start | bytes 3145736 | tf_op jit(solution)/shard_map/ppermute | solution.py:369
  86.3 10.6 %collective-permute-start.5 = (bf16[1024,128]{1,0:T(8,128)(2,1)S(1)}, bf16[1024,128]{1,0:T(8,128)(2,1)S(1)}, u32[]{:S(2)}, u32[]{:S(2)}) collective-permute-start(bf16[1024,128]{1,0:T(8,128)(2,1)S(1)} %pad_maximum_fusion.refs_0_), channel_id=1, source_target_pairs={{0,448},{64,0},{128,64},{192,128},{256,192},{320,256},{384,320},{4... | collective-permute-start | bytes 786440 | tf_op jit(solution)/shard_map/ppermute | solution.py:304
  88.6 10.6 %collective-permute-start.4 = (bf16[1024,128]{1,0:T(8,128)(2,1)S(1)}, bf16[1024,128]{1,0:T(8,128)(2,1)S(1)}, u32[]{:S(2)}, u32[]{:S(2)}) collective-permute-start(bf16[1024,128]{1,0:T(8,128)(2,1)S(1)} %pad_maximum_fusion.refs_0_), channel_id=1, source_target_pairs={{0,64},{64,128},{128,192},{192,256},{256,320},{320,384},{384,448},... | collective-permute-start | bytes 786440 | tf_op jit(solution)/shard_map/ppermute | solution.py:304
  96.9 10.8 %collective-permute-start.7 = (bf16[1024,128]{1,0:T(8,128)(2,1)S(1)}, bf16[1024,128]{1,0:T(8,128)(2,1)S(1)}, u32[]{:S(2)}, u32[]{:S(2)}) collective-permute-start(bf16[1024,128]{1,0:T(8,128)(2,1)S(1)} %collective-permute-done.5.refs_2_), channel_id=1, source_target_pairs={{0,448},{64,0},{128,64},{192,128},{256,192},{320,256},{384,320},{4... | collective-permute-start | bytes 786440 | tf_op jit(solution)/shard_map/ppermute | solution.py:304
  99.2 9.6 %collective-permute-start.6 = (bf16[1024,128]{1,0:T(8,128)(2,1)S(1)}, bf16[1024,128]{1,0:T(8,128)(2,1)S(1)}, u32[]{:S(2)}, u32[]{:S(2)}) collective-permute-start(bf16[1024,128]{1,0:T(8,128)(2,1)S(1)} %collective-permute-done.4.refs_1_), channel_id=1, source_target_pairs={{0,64},{64,128},{128,192},{192,256},{256,320},{320,384},{384,448},... | collective-permute-start | bytes 786440 | tf_op jit(solution)/shard_map/ppermute | solution.py:304
  108.9 25.1 %collective-permute-start.8 = (bf16[1024,128]{1,0:T(8,128)(2,1)S(1)}, bf16[1024,128]{1,0:T(8,128)(2,1)S(1)}, u32[]{:S(2)}, u32[]{:S(2)}) collective-permute-start(bf16[1024,128]{1,0:T(8,128)(2,1)S(1)} %get-tuple-element.17), channel_id=1, source_target_pairs={{0,64},{64,128},{128,192},{192,256},{256,320},{320,384},{384,448},... | collective-permute-start | bytes 786440 | tf_op jit(solution)/shard_map/ppermute | solution.py:304
  113.8 20.3 %collective-permute-start.9 = (bf16[1024,128]{1,0:T(8,128)(2,1)S(1)}, bf16[1024,128]{1,0:T(8,128)(2,1)S(1)}, u32[]{:S(2)}, u32[]{:S(2)}) collective-permute-start(bf16[1024,128]{1,0:T(8,128)(2,1)S(1)} %get-tuple-element.18), channel_id=1, source_target_pairs={{0,448},{64,0},{128,64},{192,128},{256,192},{320,256},{384,320},{4... | collective-permute-start | bytes 786440 | tf_op jit(solution)/shard_map/ppermute | solution.py:304
  115.7 11.0 %collective-permute-start.10 = (bf16[512,128]{1,0:T(8,128)(2,1)S(1)}, bf16[512,128]{1,0:T(8,128)(2,1)S(1)}, u32[]{:S(2)}, u32[]{:S(2)}) collective-permute-start(bf16[512,128]{1,0:T(8,128)(2,1)S(1)} %get-tuple-element.19), channel_id=1, source_target_pairs={{0,128},{64,192},{128,256},{192,320},{256,384},{320,448},{384,0},{... | collective-permute-start | bytes 393224 | tf_op jit(solution)/shard_map/ppermute | solution.py:304
  124.0 10.1 %collective-permute-start.11 = (bf16[512,128]{1,0:T(8,128)(2,1)S(1)}, bf16[512,128]{1,0:T(8,128)(2,1)S(1)}, u32[]{:S(2)}, u32[]{:S(2)}) collective-permute-start(bf16[512,128]{1,0:T(8,128)(2,1)S(1)} %get-tuple-element.20), channel_id=1, source_target_pairs={{0,384},{64,448},{128,0},{192,64},{256,128},{320,192},{384,256},{4... | collective-permute-start | bytes 393224 | tf_op jit(solution)/shard_map/ppermute | solution.py:304
  134.8 12.8 %collective-permute-start.12 = (bf16[4,2,256,128]{3,2,1,0:T(8,128)(2,1)S(1)}, bf16[4,2,256,128]{3,2,1,0:T(8,128)(2,1)S(1)}, u32[]{:S(2)}, u32[]{:S(2)}) collective-permute-start(bf16[4,2,256,128]{3,2,1,0:T(8,128)(2,1)S(1)} %shard_map.79), channel_id=1, source_target_pairs={{0,2},{2,4},{4,6},{6,8},{8,10},{10,12},{12,14},{14,0},{1,3},{3,5},... | collective-permute-start | bytes 1572872 | tf_op jit(solution)/shard_map/ppermute | solution.py:267
  139.9 13.2 %collective-permute-start.13 = (bf16[4,2,256,128]{3,2,1,0:T(8,128)(2,1)S(1)}, bf16[4,2,256,128]{3,2,1,0:T(8,128)(2,1)S(1)}, u32[]{:S(2)}, u32[]{:S(2)}) collective-permute-start(bf16[4,2,256,128]{3,2,1,0:T(8,128)(2,1)S(1)} %shard_map.80), channel_id=1, source_target_pairs={{0,14},{2,0},{4,2},{6,4},{8,6},{10,8},{12,10},{14,12},{1,15},{3,1}... | collective-permute-start | bytes 1572872 | tf_op jit(solution)/shard_map/ppermute | solution.py:267
